TPU v7x, 256 devices: a whole 4x4x8 slice. The times are simulated.
256 devices in a mesh: pix: 64 (over y, z, core), plane: 4 (over x).
Axes of the slice: x: 4, y: 4, z: 8, core: 2. Of those that a mesh axis runs over, the one named last changes fastest.
Arguments:
- movie: bfloat16 [4, 2048, 256, 256], P('plane', 'pix'), may hold values from -6 to 6
- footprints: bfloat16 [4, 8192, 1024], P('plane', 'pix'), may hold values from 0 to 0.019897461
- traces: bfloat16 [4, 8192, 256], P('plane', 'pix'), may hold values from 0 to 2
- stripe: int32 [4, 8192, 1], P('plane', 'pix'), may hold values from 0 to 63; in each aligned block of 128 rows (0 to 127, 128 to 255, ..., all dimensions but the last counted through in order) at most 4 rows name the same one
- column: int32 [4, 8192], P('plane', 'pix'), may hold values from 0 to 224
- annulus_gain: float32 [4, 256], P('plane'), may hold values from 1 to 8
- decay_slow: float32 [4, 8192], P('plane', 'pix'), may hold values from 0.4 to 0.9
- decay_fast: float32 [4, 8192], P('plane', 'pix'), may hold values from 0.05 to 0.3
Outputs:
- background: bfloat16 [4, 2048, 256, 256], P('plane', 'pix')
- traces_new: float32 [4, 8192, 256], P('plane', 'pix')
Inputs may be any that keep to these rules, and one draw needn't show every extreme that they name: Among the 128 neurons of one device (aligned blocks of 128 neurons of a plane), no stripe is named more than 4 times, and some device names one stripe exactly 4 times.
All inputs are finite; a program needn't handle non-finite values.
Results may differ from a plain program's by a relative error of at most 0.001.
The roundings to bfloat16 on the way count: a program that leaves them out, or rounds other values in their place, can miss the bound.
Values may be sent and summed in bfloat16 or wider, within the bound.
A program may use at most 128 MiB of HBM per device.

v0:
```python
import numpy as np
import ml_dtypes
import jax
import jax.numpy as jnp
from jax import lax
from jax.experimental import pallas as pl
from jax.experimental.pallas import tpu as pltpu
from jax.sharding import PartitionSpec as P

FOOT = 32
RAD = 12
GR = 3


lam_floor = 0.1
noise_eps = 1e-05
norm_eps = 1e-05
sigma_twice = 4.5


def with_halo(array, sides, width):
    for axis, dim in sides:
        devices, length = (lax.axis_size(axis), array.shape[dim])
        up = [(i, (i + 1) % devices) for i in range(devices - 1)]
        down = [(j, i) for i, j in up]
        last = lax.slice_in_dim(array, length - width, length, axis=dim)
        initial = lax.slice_in_dim(array, 0, width, axis=dim)
        before = lax.ppermute(last, axis, up)
        after = lax.ppermute(initial, axis, down)
        array = jnp.concatenate([before, array, after], axis=dim)
    return array


def deconvolve(updated, decay_slow, decay_fast):
    lag_one = jnp.pad(updated, ((0, 0), (1, 0)))[:, :-1]
    lag_two = jnp.pad(updated, ((0, 0), (2, 0)))[:, :-2]
    driven = (
        updated
        - (decay_slow + decay_fast)[:, None] * lag_one
        + (decay_slow * decay_fast)[:, None] * lag_two
    )
    return jnp.maximum(driven - lam_floor, 0.0)


def reconvolve(spikes, decay_slow, decay_fast):
    frame_count = spikes.shape[1]
    slow_col, fast_col = decay_slow[:, None], decay_fast[:, None]

    def geometric_run(values, ratio):
        total, power, shift = values, ratio, 1
        while shift < frame_count:
            lagged = jnp.pad(total, ((0, 0), (shift, 0)))[:, :-shift]
            total = total + power * lagged
            power = power * power
            shift *= 2
        return total

    slow_run = geometric_run(spikes, slow_col)
    fast_run = geometric_run(spikes, fast_col)
    kernel_scale = (1.0 - decay_slow) * (1.0 - decay_fast) / (decay_slow - decay_fast)
    return kernel_scale[:, None] * (slow_col * slow_run - fast_col * fast_run)


def tap_values():
    offsets = np.arange(-GR, GR + 1).astype(np.float64)
    raw = np.exp(-offsets * offsets / sigma_twice)
    taps = (raw / raw.sum()).astype(np.float32).astype(ml_dtypes.bfloat16)
    return taps.astype(np.float32)


def band_constants(col_count):
    index = np.arange(col_count)
    gap = index[None, :] - index[:, None]
    box = (np.abs(gap) <= RAD).astype(np.float32)
    side = (np.abs(gap) == RAD).astype(np.float32)
    taps = tap_values()
    blur = np.zeros((col_count, col_count), np.float32)
    for offset in range(-GR, GR + 1):
        blur = blur + np.where(gap == offset, taps[offset + GR], 0.0)
    wcat = np.concatenate([box, side], axis=0).astype(ml_dtypes.bfloat16)
    return wcat, blur.astype(ml_dtypes.bfloat16)


def stencil_kernel(edge_ref, top_ref, own_ref, bot_ref, wcat_ref, blur_ref, gain_ref, denom_ref,
                   back_ref, norm_ref, hsum_ref, ssum_ref, rows_ref):
    halo = top_ref.shape[0]
    own = own_ref.shape[0]
    cols = own_ref.shape[1]
    taps = [float(v) for v in tap_values()]

    def horizontal(e, row):
        prod = jnp.dot(wcat_ref[...], row, preferred_element_type=jnp.float32)
        hsum_ref[e] = prod[:cols]
        ssum_ref[e] = prod[cols:]

    def top_h(r, c):
        horizontal(r, top_ref[r])
        return c

    def own_h(r, c):
        horizontal(halo + r, own_ref[r])
        return c

    def bot_h(r, c):
        horizontal(halo + own + r, bot_ref[r])
        return c

    lax.fori_loop(0, halo, top_h, 0)
    lax.fori_loop(0, own, own_h, 0)
    lax.fori_loop(0, halo, bot_h, 0)

    first = halo - GR
    side = ssum_ref[first - RAD]
    for i in range(1, 2 * RAD - 1):
        side = side + ssum_ref[first - RAD + i]
    gain = gain_ref[...]

    def detrend(k, side, row, keep):
        e = first + k
        side = side + ssum_ref[e + RAD - 1] - ssum_ref[e - RAD]
        total = hsum_ref[e - RAD] + hsum_ref[e + RAD] + side
        fit = gain * total / (8.0 * RAD)
        residual_f = row.astype(jnp.float32)
        det = (residual_f - fit).astype(jnp.bfloat16)
        if keep is not None:
            det = (det.astype(jnp.float32) * keep).astype(jnp.bfloat16)
        rows_ref[k] = jnp.dot(blur_ref[...], det, preferred_element_type=jnp.float32)
        return side, fit

    keep_top = edge_ref[0]
    keep_bot = edge_ref[1]

    def top_d(k, side):
        side, _ = detrend(k, side, top_ref[first + k], keep_top)
        return side

    def own_d(r, side):
        side, fit = detrend(GR + r, side, own_ref[r], None)
        back_ref[r] = fit.astype(back_ref.dtype)
        return side

    def bot_d(r, side):
        side, _ = detrend(GR + own + r, side, bot_ref[r], keep_bot)
        return side

    side = lax.fori_loop(0, GR, top_d, side)
    side = lax.fori_loop(0, own, own_d, side)
    side = lax.fori_loop(0, GR, bot_d, side)

    def smooth(y, c):
        acc = taps[0] * rows_ref[y]
        for o in range(1, 2 * GR + 1):
            acc = acc + taps[o] * rows_ref[y + o]
        norm_ref[y] = (acc / denom_ref[y]).astype(norm_ref.dtype)
        return c

    lax.fori_loop(0, own, smooth, 0)


def stencil(edge, top, own, bot, gain_col, denom, frame_block=128):
    halo, own_rows, cols, frames = top.shape[0], own.shape[0], own.shape[1], own.shape[2]
    ext = 2 * halo + own_rows
    wcat, blur = band_constants(cols)
    grid = (frames // frame_block,)
    row_block = lambda n: pl.BlockSpec((n, cols, frame_block), lambda j: (0, 0, j))
    fixed = lambda shape: pl.BlockSpec(shape, lambda j: (0,) * len(shape))
    return pl.pallas_call(
        stencil_kernel,
        grid=grid,
        in_specs=[
            pl.BlockSpec(memory_space=pltpu.SMEM),
            row_block(halo), row_block(own_rows), row_block(halo),
            fixed((2 * cols, cols)), fixed((cols, cols)), fixed((cols, 1)), fixed((own_rows, cols, 1)),
        ],
        out_specs=[row_block(own_rows), row_block(own_rows)],
        out_shape=[jax.ShapeDtypeStruct(own.shape, jnp.bfloat16), jax.ShapeDtypeStruct(own.shape, jnp.bfloat16)],
        scratch_shapes=[
            pltpu.VMEM((ext, cols, frame_block), jnp.float32),
            pltpu.VMEM((ext, cols, frame_block), jnp.float32),
            pltpu.VMEM((own_rows + 2 * GR, cols, frame_block), jnp.float32),
        ],
        compiler_params=pltpu.CompilerParams(vmem_limit_bytes=60 * 1024 * 1024),
    )(edge, top, own, bot, jnp.asarray(wcat), jnp.asarray(blur), gain_col, denom)


def on_device(movie, footprints, traces, stripe, column, annulus_gain, decay_slow, decay_fast):
    pix_count = lax.axis_size("pix")
    row_count = movie.shape[1]
    col_count = movie.shape[2]
    frame_count = movie.shape[3]
    neuron_count = footprints.shape[1]
    capacity = max(2, 2 * neuron_count // pix_count)
    slot_count = pix_count * capacity
    target_stripe = stripe[0, :, 0]
    neuron_index = jnp.arange(neuron_count)
    earlier_same = (target_stripe[:, None] == target_stripe[None, :]) & (
        neuron_index[None, :] < neuron_index[:, None]
    )
    arrival_rank = jnp.sum(earlier_same.astype(jnp.int32), axis=1)
    slot_index = target_stripe * capacity + arrival_rank
    placement = slot_index[:, None] == jnp.arange(slot_count)[None, :]
    placement_b = placement.astype(jnp.bfloat16)
    contract_first = (((0,), (0,)), ((), ()))
    tile_width, trace_width = footprints.shape[2], traces.shape[2]
    column_lanes = jnp.broadcast_to(
        (column[0] + 1).astype(jnp.bfloat16)[:, None], (neuron_count, 128)
    )
    payload = jnp.concatenate([footprints[0], traces[0], column_lanes], axis=1)
    outbox = lax.dot_general(
        placement_b, payload, contract_first, preferred_element_type=jnp.float32
    ).astype(jnp.bfloat16)
    inbox = lax.all_to_all(outbox, "pix", split_axis=0, concat_axis=0, tiled=True)
    tile_inbox = inbox[:, :tile_width]
    trace_inbox = inbox[:, tile_width : tile_width + trace_width]
    column_inbox = inbox[:, tile_width + trace_width].astype(jnp.int32)
    left_edge = column_inbox - 1
    covered = left_edge[:, None] + jnp.arange(FOOT)[None, :]
    column_onehot = (covered[:, :, None] == jnp.arange(col_count)[None, None, :]).astype(
        jnp.bfloat16
    )
    tile_grid = tile_inbox.reshape(slot_count, FOOT, FOOT)
    footprint_rows = (
        jnp.einsum("srj,sjc->src", tile_grid, column_onehot, preferred_element_type=jnp.float32)
        .astype(jnp.bfloat16)
        .reshape(slot_count, FOOT * col_count)
    )
    model_image = lax.dot_general(
        footprint_rows, trace_inbox, contract_first, preferred_element_type=jnp.float32
    )
    residual = (
        movie[0].astype(jnp.float32).reshape(row_count * col_count, frame_count) - model_image
    ).astype(jnp.bfloat16)
    residual = residual.reshape(row_count, col_count, frame_count)
    halo = RAD + GR
    pix_index = lax.axis_index("pix")
    up = [(i, i + 1) for i in range(pix_count - 1)]
    down = [(j, i) for i, j in up]
    top_halo = lax.ppermute(residual[row_count - halo :], "pix", up)
    bottom_halo = lax.ppermute(residual[:halo], "pix", down)
    residual_f = residual.astype(jnp.float32)
    frame_step = residual_f[:, :, 1:] - residual_f[:, :, :-1]
    noise_level = jnp.sum(frame_step * frame_step, axis=2) / (frame_count - 1)
    noise_stack = with_halo(noise_level[None], (("plane", 0),), 1)
    pooled = (noise_stack[0] + 2.0 * noise_stack[1] + noise_stack[2]) / 4.0
    denom = jnp.sqrt(pooled + noise_eps)[:, :, None]
    edge = jnp.stack([pix_index > 0, pix_index < pix_count - 1]).astype(jnp.float32)
    background, normalized = stencil(
        edge, top_halo, residual, bottom_halo, annulus_gain[0][:, None], denom
    )
    normalized = normalized.reshape(row_count * col_count, frame_count)
    slot_gradient = jnp.dot(footprint_rows, normalized, preferred_element_type=jnp.float32)
    home_gradient = lax.all_to_all(slot_gradient, "pix", split_axis=0, concat_axis=0, tiled=True)
    gradient = lax.dot_general(
        placement.astype(jnp.float32),
        home_gradient,
        (((1,), (0,)), ((), ())),
        precision=lax.Precision.HIGHEST,
    )
    foot_f = footprints[0].astype(jnp.float32)
    step_size = 1.0 / (jnp.sum(foot_f * foot_f, axis=1) + norm_eps)
    updated = traces[0].astype(jnp.float32) + step_size[:, None] * gradient
    spikes = deconvolve(updated, decay_slow[0], decay_fast[0])
    traces_new = reconvolve(spikes, decay_slow[0], decay_fast[0])
    return (background[None], traces_new[None])


def solution(mesh):
    placed = (
        P("plane", "pix", None, None),
        P("plane", "pix", None),
        P("plane", "pix", None),
        P("plane", "pix", None),
        P("plane", "pix"),
        P("plane", None),
        P("plane", "pix"),
        P("plane", "pix"),
    )
    return jax.shard_map(
        on_device,
        mesh=mesh,
        in_specs=placed,
        out_specs=(P("plane", "pix", None, None), P("plane", "pix", None)),
        check_vma=False,
    )
```

profile of v0, /device:TPU:1, one launch (start us, length us, event | category | flops | bytes accessed | tf_op | source)
XLA Modules:
  0.0 194.2 jit_solution(16570540940288053326)
XLA Ops:
  0.6 0.9 convert_reduce_fusion
  1.5 0.7 multiply_add_fusion.2
  2.2 0.7 convert_bitcast_fusion
  2.9 0.1 broadcast_in_dim.6
  2.9 1.5 convolution_convert_fusion
  4.4 0.2 all_to_all.14
  4.6 34.6 %all_to_all.21 = bf16[64,4,1408]{2,1,0:T(4,128)(2,1)S(1)} all-to-all(bf16[64,4,1408]{2,1,0:T(4,128)(2,1)S(1)} %all_to_all.14), channel_id=1, replica_groups=mesh['pix'=64,'plane'=4] {'pix'}, dimensions={0} | all-to-all | bytes 1441792 | tf_op jit(solution)/shard_map/all_to_all | solution.py:212
  39.2 0.2 all_to_all.16
  39.3 0.1 slice.105
  39.4 0.1 add_reduce_fusion
  39.5 0.2 copy.52
  39.7 3.0 %copy.53 = bf16[256,32,32]{2,1,0:T(8,128)(2,1)S(1)} copy(bf16[256,32,32]{0,2,1:T(8,128)(2,1)S(1)} %bitcast.61) | data formatting | bytes 1048576 | tf_op jit(solution)/shard_map/reshape | solution.py:221
  42.7 0.1 iota_add_fusion
  42.8 2.7 %fusion.7 = bf16[256,32,256]{2,1,0:T(8,128)(2,1)S(1)} fusion(bf16[256,32,32]{2,1,0:T(8,128)(2,1)S(1)} %copy.53, s32[256,32]{1,0:T(8,128)S(1)} %iota_add_fusion), kind=kOutput, calls=%fused_computation.11 | convolution fusion | flops 138412032 | bytes 4751360 | tf_op jit(solution)/shard_map/srj,sjc->src/dot_general | solution.py:223
  45.5 0.0 copy-start.1
  45.5 0.0 copy-start.2
  45.5 4.4 %copy.59 = bf16[32,8,32,256]{3,1,2,0:T(8,128)(2,1)S(1)} copy(bf16[32,8,32,256]{3,2,1,0:T(8,128)(2,1)S(1)} %bitcast.58) | data formatting | bytes 8388608
  50.0 0.0 copy-done.1
  50.0 0.0 copy-done.2
  50.0 4.6 %bitcast_convert_fusion = (f32[32,256,256]{2,1,0:T(8,128)}, bf16[8192,256]{1,0:T(8,128)(2,1)S(1)}) fusion(bf16[256,8192]{1,0:T(8,128)(2,1)S(1)} %bitcast.59, bf16[256,1408]{1,0:T(8,128)(2,1)S(1)} %all_to_all.16, bf16[8192,256]{1,0:T(8,128)(2,1)S(1)} %bitcast.60), kind=kOutput, calls=%fused_computation.100 | convolution fusion | flops 1082130432 | bytes 21102592 | tf_op jit(solution)/shard_map/dot_general | solution.py:227
  54.6 2.0 %copy-done = bf16[8192,256]{1,0:T(8,128)(2,1)} copy-done((bf16[8192,256]{1,0:T(8,128)(2,1)}, bf16[8192,256]{1,0:T(8,128)(2,1)S(1)}, u32[]{:S(2)}) %copy-start) | copy-done | bytes 4194328
  56.6 2.2 %fusion.66 = (bf16[3840,256]{1,0:T(8,128)(2,1)}, bf16[3840,256]{1,0:T(8,128)(2,1)}) fusion(bf16[8192,256]{1,0:T(8,128)(2,1)S(1)} %get-tuple-element.32), kind=kLoop, calls=%fused_computation.111 | loop fusion | bytes 7864320 | tf_op jit(solution)/shard_map/slice | solution.py:239
  58.8 3.2 %collective-permute-start = (bf16[15,256,256]{2,1,0:T(8,128)(2,1)}, bf16[15,256,256]{2,1,0:T(8,128)(2,1)S(1)}, u32[]{:S(2)}, u32[]{:S(2)}) collective-permute-start(bf16[15,256,256]{2,1,0:T(8,128)(2,1)} %bitcast.8), channel_id=1, source_target_pairs={{0,4},{4,8},{8,12},{12,16},{16,20},{20,24},{24,28},{28,32},{32,36}... | collective-permute-start | bytes 5898248 | tf_op jit(solution)/shard_map/ppermute | solution.py:238
  62.0 2.1 %collective-permute-start.1 = (bf16[15,256,256]{2,1,0:T(8,128)(2,1)}, bf16[15,256,256]{2,1,0:T(8,128)(2,1)}, u32[]{:S(2)}, u32[]{:S(2)}) collective-permute-start(bf16[15,256,256]{2,1,0:T(8,128)(2,1)} %bitcast.10), channel_id=1, source_target_pairs={{4,0},{8,4},{12,8},{16,12},{20,16},{24,20},{28,24},{32,28},{36,32}... | collective-permute-start | bytes 5898248 | tf_op jit(solution)/shard_map/ppermute | solution.py:239
  64.1 0.0 copy-done.4
  64.1 0.1 multiply_reduce_fusion
  64.2 9.2 %fusion.2 = f32[32,256]{1,0:T(8,128)S(1)} fusion(f32[32,256,256]{2,1,0:T(8,128)} %get-tuple-element.31), kind=kLoop, calls=%fused_computation.4 | loop fusion | flops 6258688 | bytes 16744448 | tf_op jit(solution)/shard_map/reduce_sum | solution.py:242
  73.5 3.1 %collective-permute-start.2 = (f32[1,32,256]{2,1,0:T(8,128)S(1)}, f32[1,32,256]{2,1,0:T(8,128)S(1)}, u32[]{:S(2)}, u32[]{:S(2)}) collective-permute-start(f32[1,32,256]{2,1,0:T(8,128)S(1)} %multiply_bitcast_fusion), channel_id=1, source_target_pairs={{0,1},{1,2},{2,3},{4,5},{5,6},{6,7},{8,9},{9,10},{10,11},{12,13},{... | collective-permute-start | bytes 98312 | tf_op jit(solution)/shard_map/ppermute | solution.py:28
  76.6 0.6 add_convert_fusion.edge_ref
  77.2 0.0 copy-done.8
  77.2 0.8 copy.56.gain_ref
  78.0 1.3 collective-permute-start.3
  79.3 7.8 %dot_general.20 = bf16[64,4,8192]{2,1,0:T(4,128)(2,1)} reshape(bf16[256,32,256]{2,1,0:T(8,128)(2,1)} %copy-done.1) | data formatting | bytes 8388608 | tf_op jit(solution)/shard_map/dot_general | solution.py:251
  87.1 0.0 collective-permute-done.2
  87.1 2.7 %copy.54 = f32[32,256,1]{2,1,0:T(8,128)} copy(f32[32,256,1]{1,0,2:T(8,128)S(1)} %bitcast_add_fusion) | data formatting | bytes 65536 | tf_op jit(solution)/shard_map/add | solution.py:244
  89.8 0.0 collective-permute-done.3
  89.8 2.6 %copy.55 = f32[32,256,1]{2,1,0:T(8,128)} copy(f32[32,256,1]{1,0,2:T(8,128)S(1)} %bitcast.64) | data formatting | bytes 65536 | tf_op jit(solution)/shard_map/squeeze | solution.py:244
  92.4 6.8 %add_sqrt_fusion.denom_ref = f32[32,256,1]{2,1,0:T(8,128)} fusion(f32[32,256,1]{2,1,0:T(8,128)} %copy.54, f32[32,256,1]{2,1,0:T(8,128)} %copy.55), kind=kLoop, calls=%fused_computation.9 | loop fusion | flops 24576 | bytes 98304 | tf_op jit(solution)/shard_map/sqrt | solution.py:245
  99.2 0.0 collective-permute-done.top_ref
  99.2 0.0 collective-permute-done.1.bot_ref
  99.2 1.3 copy-done.3
  100.5 61.7 %shard_map.113 = (bf16[32,256,256]{2,1,0:T(8,128)(2,1)}, bf16[32,256,256]{2,1,0:T(8,128)(2,1)}) custom-call(f32[2]{0:T(128)} %add_convert_fusion.edge_ref, bf16[15,256,256]{2,1,0:T(8,128)(2,1)} %copy-done.3, bf16[32,256,256]{2,1,0:T(8,128)(2,1)} %bitcast.57, bf16[15,256,256]{2,1,0:T(8,128)(2,1)} %collective-permute-done.1.bot_ref, ...), custom_call_target="tpu_custom_call" | custom-call | tf_op jit(solution)/shard_map/pallas_call | solution.py:167
  162.2 0.0 copy-start.5
  162.2 8.2 %fusion.4 = f32[64,4,256]{2,0,1:T(8,128)S(1)} fusion(bf16[8192,256,1]{1,0,2:T(8,128)(2,1)} %bitcast.71, bf16[64,4,8192]{2,1,0:T(4,128)(2,1)} %dot_general.20), kind=kOutput, calls=%fused_computation.7 | convolution fusion | flops 1073741824 | bytes 8650752 | tf_op jit(solution)/shard_map/dot_general | solution.py:251
  170.4 0.9 copy.58
  171.3 8.0 %all-to-all-start.1 = ((f32[64,4,256]{2,1,0:T(4,128)}), f32[64,4,256]{2,1,0:T(4,128)S(1)}, u32[]{:S(2)}, u32[]{:S(2)}) async-start(f32[64,4,256]{2,1,0:T(4,128)} %copy.58), calls=%async_computation.1 | async-start | bytes 524288 | tf_op jit(solution)/shard_map/all_to_all | solution.py:252
  179.3 0.0 copy-done.6
  179.3 11.9 %all-to-all-done.1 = f32[64,4,256]{2,1,0:T(4,128)S(1)} async-done(((f32[64,4,256]{2,1,0:T(4,128)}), f32[64,4,256]{2,1,0:T(4,128)S(1)}, u32[]{:S(2)}, u32[]{:S(2)}) %all-to-all-start.1) | async-done | bytes 262176 | tf_op jit(solution)/shard_map/all_to_all | solution.py:252
  191.3 0.1 all_to_all.18
  191.4 0.3 fusion.8
  191.7 0.2 fusion.18
  191.8 0.2 multiply_add_fusion
  192.0 0.2 fusion.21
  192.2 0.1 fusion.41
  192.3 0.1 fusion.43
  192.4 0.1 fusion.23
  192.5 0.1 fusion.25
  192.7 0.1 fusion.45
  192.8 0.1 fusion.47
  192.9 0.1 fusion.49
  193.0 0.1 fusion.27
  193.2 0.1 fusion.29
  193.3 0.1 fusion.31
  193.4 0.8 fusion.37
  (13 shorter events, 0.1 us)
Async XLA Ops:
  45.5 4.5 %copy-start.1 = (bf16[256,32,256]{2,1,0:T(8,128)(2,1)}, bf16[256,32,256]{2,1,0:T(8,128)(2,1)S(1)}, u32[]{:S(2)}) copy-start(bf16[256,32,256]{2,1,0:T(8,128)(2,1)S(1)} %fusion.7) | copy-start | bytes 12582916
  45.5 4.5 %copy-start.2 = (bf16[1,32,256,256]{3,2,1,0:T(8,128)(2,1)S(1)}, bf16[1,32,256,256]{3,2,1,0:T(8,128)(2,1)}, u32[]{:S(2)}) copy-start(bf16[1,32,256,256]{3,2,1,0:T(8,128)(2,1)} %param.10) | copy-start | bytes 12582916
  54.6 2.0 %copy-start = (bf16[8192,256]{1,0:T(8,128)(2,1)}, bf16[8192,256]{1,0:T(8,128)(2,1)S(1)}, u32[]{:S(2)}) copy-start(bf16[8192,256]{1,0:T(8,128)(2,1)S(1)} %get-tuple-element.32) | copy-start | bytes 12582916
  54.6 9.5 %copy-start.4 = (bf16[1,128,1024]{2,1,0:T(8,128)(2,1)S(1)}, bf16[1,128,1024]{2,1,0:T(8,128)(2,1)}, u32[]{:S(2)}) copy-start(bf16[1,128,1024]{2,1,0:T(8,128)(2,1)} %param.11) | copy-start | bytes 786436
  58.8 40.4 %collective-permute-start = (bf16[15,256,256]{2,1,0:T(8,128)(2,1)}, bf16[15,256,256]{2,1,0:T(8,128)(2,1)S(1)}, u32[]{:S(2)}, u32[]{:S(2)}) collective-permute-start(bf16[15,256,256]{2,1,0:T(8,128)(2,1)} %bitcast.8), channel_id=1, source_target_pairs={{0,4},{4,8},{8,12},{12,16},{16,20},{20,24},{24,28},{28,32},{32,36}... | collective-permute-start | bytes 5898248 | tf_op jit(solution)/shard_map/ppermute | solution.py:238
  62.0 37.2 %collective-permute-start.1 = (bf16[15,256,256]{2,1,0:T(8,128)(2,1)}, bf16[15,256,256]{2,1,0:T(8,128)(2,1)}, u32[]{:S(2)}, u32[]{:S(2)}) collective-permute-start(bf16[15,256,256]{2,1,0:T(8,128)(2,1)} %bitcast.10), channel_id=1, source_target_pairs={{4,0},{8,4},{12,8},{16,12},{20,16},{24,20},{28,24},{32,28},{36,32}... | collective-permute-start | bytes 5898248 | tf_op jit(solution)/shard_map/ppermute | solution.py:239
  64.2 13.0 %copy-start.8 = (f32[1,256]{1,0:T(1,128)S(1)}, f32[1,256]{1,0:T(1,128)}, u32[]{:S(2)}) copy-start(f32[1,256]{1,0:T(1,128)} %param.15) | copy-start | bytes 3076
  73.5 13.6 %collective-permute-start.2 = (f32[1,32,256]{2,1,0:T(8,128)S(1)}, f32[1,32,256]{2,1,0:T(8,128)S(1)}, u32[]{:S(2)}, u32[]{:S(2)}) collective-permute-start(f32[1,32,256]{2,1,0:T(8,128)S(1)} %multiply_bitcast_fusion), channel_id=1, source_target_pairs={{0,1},{1,2},{2,3},{4,5},{5,6},{6,7},{8,9},{9,10},{10,11},{12,13},{... | collective-permute-start | bytes 98312 | tf_op jit(solution)/shard_map/ppermute | solution.py:28
  78.0 11.8 %collective-permute-start.3 = (f32[1,32,256]{2,1,0:T(8,128)S(1)}, f32[1,32,256]{2,1,0:T(8,128)S(1)}, u32[]{:S(2)}, u32[]{:S(2)}) collective-permute-start(f32[1,32,256]{2,1,0:T(8,128)S(1)} %multiply_bitcast_fusion), channel_id=1, source_target_pairs={{1,0},{2,1},{3,2},{5,4},{6,5},{7,6},{9,8},{10,9},{11,10},{13,12},{... | collective-permute-start | bytes 98312 | tf_op jit(solution)/shard_map/ppermute | solution.py:29
  99.2 1.3 copy-start.3
  162.2 17.1 %copy-start.6 = (f32[1,128]{1,0:T(1,128)S(1)}, f32[1,128]{1,0:T(1,128)}, u32[]{:S(2)}) copy-start(f32[1,128]{1,0:T(1,128)} %param.17) | copy-start | bytes 1540
  162.2 17.1 %copy-start.7 = (f32[1,128]{1,0:T(1,128)S(1)}, f32[1,128]{1,0:T(1,128)}, u32[]{:S(2)}) copy-start(f32[1,128]{1,0:T(1,128)} %param.16) | copy-start | bytes 1540
  162.2 29.2 %copy-start.5 = (bf16[1,128,256]{2,1,0:T(8,128)(2,1)S(1)}, bf16[1,128,256]{2,1,0:T(8,128)(2,1)}, u32[]{:S(2)}) copy-start(bf16[1,128,256]{2,1,0:T(8,128)(2,1)} %param.12) | copy-start | bytes 196612
  171.3 20.0 %all-to-all-start.1 = ((f32[64,4,256]{2,1,0:T(4,128)}), f32[64,4,256]{2,1,0:T(4,128)S(1)}, u32[]{:S(2)}, u32[]{:S(2)}) async-start(f32[64,4,256]{2,1,0:T(4,128)} %copy.58), calls=%async_computation.1 | async-start | bytes 524288 | tf_op jit(solution)/shard_map/all_to_all | solution.py:252
where the time goes:
time: 195 us; the launch traced here: 194 us
  Pallas kernels  61.7 us (32%)
  blocking collectives  34.6 us (18%)
  local copies, waits for them, and re-layouts  28.5 us (15%)
  other arithmetic  21.7 us (11%)
  starting transfers between devices  17.7 us (9%)
  matrix products  17.2 us (9%)
  waiting for transfers between devices  11.9 us (6%)
    pallas_call x1, Pallas kernels, stencil(): pl.pallas_call(stencil_kernel, grid=grid, in_specs=[pl.BlockSpec(memory_s...  61.7 us
    all_to_all x1, blocking collectives, on_device(): lax.all_to_all(outbox, 'pix', split_axis=0, concat_axis=0, tiled=True)  34.6 us
    all_to_all x1, waiting for transfers between devices, on_device(): lax.all_to_all(slot_gradient, 'pix', split_axis=0, concat_axis=0, tiled=T...  11.9 us
    reduce_sum x1, other arithmetic, on_device(): noise_level = jnp.sum(frame_step * frame_step, axis=2) / (frame_count - 1)  9.25 us
    dot_general x2, local copies, waits for them, and re-layouts, on_device(): jnp.dot(footprint_rows, normalized, preferred_element_type=jnp.float32)  8.72 us
    dot_general x1, matrix products, on_device(): jnp.dot(footprint_rows, normalized, preferred_element_type=jnp.float32)  8.18 us
    all_to_all x1, starting transfers between devices, on_device(): lax.all_to_all(slot_gradient, 'pix', split_axis=0, concat_axis=0, tiled=T...  7.99 us
    unnamed x19, local copies, waits for them, and re-layouts  7.73 us
  transfers between devices with their start and end apart: 5, of which 1 were waited for; matrix products, arithmetic and copies ran while one was open for 16% of the time, Pallas kernels for 0%

commit v1 on v0

--- a/solution.py
+++ b/solution.py
@@ -81,8 +81,8 @@
     return wcat, blur.astype(ml_dtypes.bfloat16)
 
 
-def stencil_kernel(edge_ref, top_ref, own_ref, bot_ref, wcat_ref, blur_ref, gain_ref, denom_ref,
-                   back_ref, norm_ref, hsum_ref, ssum_ref, rows_ref):
+def stencil_kernel(edge_ref, top_ref, own_ref, bot_ref, wcat_ref, blur_ref, scale_ref, recip_ref,
+                   frows_ref, back_ref, grad_ref, hsum_ref, ssum_ref, rows_ref):
     halo = top_ref.shape[0]
     own = own_ref.shape[0]
     cols = own_ref.shape[1]
@@ -113,13 +113,12 @@
     side = ssum_ref[first - RAD]
     for i in range(1, 2 * RAD - 1):
         side = side + ssum_ref[first - RAD + i]
-    gain = gain_ref[...]
 
     def detrend(k, side, row, keep):
         e = first + k
         side = side + ssum_ref[e + RAD - 1] - ssum_ref[e - RAD]
         total = hsum_ref[e - RAD] + hsum_ref[e + RAD] + side
-        fit = gain * total / (8.0 * RAD)
+        fit = scale_ref[...] * total
         residual_f = row.astype(jnp.float32)
         det = (residual_f - fit).astype(jnp.bfloat16)
         if keep is not None:
@@ -147,18 +146,22 @@
     side = lax.fori_loop(0, own, own_d, side)
     side = lax.fori_loop(0, GR, bot_d, side)
 
+    grad_ref[...] = jnp.zeros_like(grad_ref)
+
     def smooth(y, c):
-        acc = taps[0] * rows_ref[y]
-        for o in range(1, 2 * GR + 1):
-            acc = acc + taps[o] * rows_ref[y + o]
-        norm_ref[y] = (acc / denom_ref[y]).astype(norm_ref.dtype)
+        acc = taps[GR] * rows_ref[y + GR]
+        for o in range(GR):
+            acc = acc + taps[o] * (rows_ref[y + o] + rows_ref[y + 2 * GR - o])
+        normalized = (acc * recip_ref[y]).astype(jnp.bfloat16)
+        grad_ref[...] += jnp.dot(frows_ref[y], normalized, preferred_element_type=jnp.float32)
         return c
 
     lax.fori_loop(0, own, smooth, 0)
 
 
-def stencil(edge, top, own, bot, gain_col, denom, frame_block=128):
+def stencil(edge, top, own, bot, scale, recip, frows, frame_block=128):
     halo, own_rows, cols, frames = top.shape[0], own.shape[0], own.shape[1], own.shape[2]
+    slots = frows.shape[1]
     ext = 2 * halo + own_rows
     wcat, blur = band_constants(cols)
     grid = (frames // frame_block,)
@@ -170,17 +173,19 @@
         in_specs=[
             pl.BlockSpec(memory_space=pltpu.SMEM),
             row_block(halo), row_block(own_rows), row_block(halo),
-            fixed((2 * cols, cols)), fixed((cols, cols)), fixed((cols, 1)), fixed((own_rows, cols, 1)),
+            fixed((2 * cols, cols)), fixed((cols, cols)), fixed((cols, frame_block)),
+            fixed((own_rows, cols, frame_block)), fixed((own_rows, slots, cols)),
         ],
-        out_specs=[row_block(own_rows), row_block(own_rows)],
-        out_shape=[jax.ShapeDtypeStruct(own.shape, jnp.bfloat16), jax.ShapeDtypeStruct(own.shape, jnp.bfloat16)],
+        out_specs=[row_block(own_rows), pl.BlockSpec((slots, frame_block), lambda j: (0, j))],
+        out_shape=[jax.ShapeDtypeStruct(own.shape, jnp.bfloat16),
+                   jax.ShapeDtypeStruct((slots, frames), jnp.float32)],
         scratch_shapes=[
             pltpu.VMEM((ext, cols, frame_block), jnp.float32),
             pltpu.VMEM((ext, cols, frame_block), jnp.float32),
             pltpu.VMEM((own_rows + 2 * GR, cols, frame_block), jnp.float32),
         ],
         compiler_params=pltpu.CompilerParams(vmem_limit_bytes=60 * 1024 * 1024),
-    )(edge, top, own, bot, jnp.asarray(wcat), jnp.asarray(blur), gain_col, denom)
+    )(edge, top, own, bot, jnp.asarray(wcat), jnp.asarray(blur), scale, recip, frows)
 
 
 def on_device(movie, footprints, traces, stripe, column, annulus_gain, decay_slow, decay_fast):
@@ -219,36 +224,43 @@
         jnp.bfloat16
     )
     tile_grid = tile_inbox.reshape(slot_count, FOOT, FOOT)
-    footprint_rows = (
-        jnp.einsum("srj,sjc->src", tile_grid, column_onehot, preferred_element_type=jnp.float32)
-        .astype(jnp.bfloat16)
-        .reshape(slot_count, FOOT * col_count)
-    )
-    model_image = lax.dot_general(
-        footprint_rows, trace_inbox, contract_first, preferred_element_type=jnp.float32
-    )
-    residual = (
-        movie[0].astype(jnp.float32).reshape(row_count * col_count, frame_count) - model_image
+    frows = jnp.einsum(
+        "srj,sjc->rsc", tile_grid, column_onehot, preferred_element_type=jnp.float32
     ).astype(jnp.bfloat16)
-    residual = residual.reshape(row_count, col_count, frame_count)
+    model_image = jnp.einsum(
+        "rsc,st->rct", frows, trace_inbox, preferred_element_type=jnp.float32
+    )
+    residual = (movie[0].astype(jnp.float32) - model_image).astype(jnp.bfloat16)
     halo = RAD + GR
     pix_index = lax.axis_index("pix")
     up = [(i, i + 1) for i in range(pix_count - 1)]
     down = [(j, i) for i, j in up]
     top_halo = lax.ppermute(residual[row_count - halo :], "pix", up)
     bottom_halo = lax.ppermute(residual[:halo], "pix", down)
-    residual_f = residual.astype(jnp.float32)
-    frame_step = residual_f[:, :, 1:] - residual_f[:, :, :-1]
-    noise_level = jnp.sum(frame_step * frame_step, axis=2) / (frame_count - 1)
+    frame_index = np.arange(frame_count)
+    step_matrix = (
+        (frame_index[:, None] == frame_index[None, :] + 1).astype(np.float32)
+        - (frame_index[:, None] == frame_index[None, :]).astype(np.float32)
+    ) * (frame_index[None, :] < frame_count - 1)
+    frame_step = jnp.dot(
+        residual.reshape(row_count * col_count, frame_count),
+        jnp.asarray(step_matrix, jnp.bfloat16),
+        preferred_element_type=jnp.float32,
+    )
+    noise_level = (jnp.sum(frame_step * frame_step, axis=1) / (frame_count - 1)).reshape(
+        row_count, col_count
+    )
     noise_stack = with_halo(noise_level[None], (("plane", 0),), 1)
     pooled = (noise_stack[0] + 2.0 * noise_stack[1] + noise_stack[2]) / 4.0
-    denom = jnp.sqrt(pooled + noise_eps)[:, :, None]
+    frame_block = 128
+    recip = jnp.broadcast_to(
+        (1.0 / jnp.sqrt(pooled + noise_eps))[:, :, None], (row_count, col_count, frame_block)
+    )
+    scale = jnp.broadcast_to((annulus_gain[0] / (8.0 * RAD))[:, None], (col_count, frame_block))
     edge = jnp.stack([pix_index > 0, pix_index < pix_count - 1]).astype(jnp.float32)
-    background, normalized = stencil(
-        edge, top_halo, residual, bottom_halo, annulus_gain[0][:, None], denom
-    )
-    normalized = normalized.reshape(row_count * col_count, frame_count)
-    slot_gradient = jnp.dot(footprint_rows, normalized, preferred_element_type=jnp.float32)
+    background, slot_gradient = stencil(
+        edge, top_halo, residual, bottom_halo, scale, recip, frows, frame_block
+    )
     home_gradient = lax.all_to_all(slot_gradient, "pix", split_axis=0, concat_axis=0, tiled=True)
     gradient = lax.dot_general(
         placement.astype(jnp.float32),

time: 195 us -> 178 us (0.913)
  other arithmetic: 21.7 us -> 5.7 us
  waiting for transfers between devices: 11.9 us -> 20.8 us
  local copies, waits for them, and re-layouts: 28.5 us -> 19.6 us
  matrix products: 17.2 us -> 13.2 us
  Pallas kernels: 61.7 us -> 64.2 us
    reduce_sum x1 -> x0, other arithmetic: 9.25 us -> none  [on_device(): noise_level = jnp.sum(frame_step * frame_step, axis=2) / (frame_count - 1)]
    sqrt x1, other arithmetic: 6.77 us -> 0.02 us  [on_device(): jnp.sqrt(pooled + noise_eps)]
    unnamed x19 -> x20, local copies, waits for them, and re-layouts: 7.73 us -> 1.99 us
    ppermute x1, waiting for transfers between devices: 0.01 us -> 4.42 us  [on_device(): top_halo = lax.ppermute(residual[row_count - halo:], 'pix', up)]
    ppermute x1, waiting for transfers between devices: 0.01 us -> 4.39 us  [on_device(): bottom_halo = lax.ppermute(residual[:halo], 'pix', down)]
    dot_general x3, matrix products: 15.5 us -> 11.5 us  [the longest x1 5.21 us: on_device(): jnp.einsum('rsc,st->rct', frows, trace_inbox, preferred_element_type=jnp....]
    broadcast_in_dim x0 -> x2, local copies, waits for them, and re-layouts: none -> 3.32 us  [the longest x1 2.57 us: on_device(): jnp.broadcast_to((1.0 / jnp.sqrt(pooled + noise_eps))[:, :, None], (row_c...]
    add x1 -> x0, local copies, waits for them, and re-layouts: 2.68 us -> none  [on_device(): pooled = (noise_stack[0] + 2.0 * noise_stack[1] + noise_stack[2]) / 4.0]
  transfers between devices with their start and end apart: 5 -> 5, of which waited for: 1 -> 3; matrix products, arithmetic and copies ran while one was open for 16% -> 6% of each run, Pallas kernels for 0% -> 0%
where the time goes in v1:
time: 178 us; the launch traced here: 177 us
  Pallas kernels  64.2 us (36%)
  blocking collectives  34.6 us (19%)
  waiting for transfers between devices  20.8 us (12%)
  local copies, waits for them, and re-layouts  19.6 us (11%)
  starting transfers between devices  18.1 us (10%)
  matrix products  13.2 us (7%)
  other arithmetic  5.7 us (3%)
    pallas_call x1, Pallas kernels, stencil(): pl.pallas_call(stencil_kernel, grid=grid, in_specs=[pl.BlockSpec(memory_s...  64.2 us
    all_to_all x1, blocking collectives, on_device(): lax.all_to_all(outbox, 'pix', split_axis=0, concat_axis=0, tiled=True)  34.6 us
    all_to_all x1, waiting for transfers between devices, on_device(): lax.all_to_all(slot_gradient, 'pix', split_axis=0, concat_axis=0, tiled=T...  11.9 us
    all_to_all x1, starting transfers between devices, on_device(): lax.all_to_all(slot_gradient, 'pix', split_axis=0, concat_axis=0, tiled=T...  8.39 us
    dot_general x1, local copies, waits for them, and re-layouts, on_device(): jnp.einsum('srj,sjc->rsc', tile_grid, column_onehot, preferred_element_ty...  6.52 us
    dot_general x1, matrix products, on_device(): jnp.einsum('rsc,st->rct', frows, trace_inbox, preferred_element_type=jnp....  5.21 us
    ppermute x1, waiting for transfers between devices, on_device(): top_halo = lax.ppermute(residual[row_count - halo:], 'pix', up)  4.42 us
    ppermute x1, waiting for transfers between devices, on_device(): bottom_halo = lax.ppermute(residual[:halo], 'pix', down)  4.39 us
  transfers between devices with their start and end apart: 5, of which 3 were waited for; matrix products, arithmetic and copies ran while one was open for 6% of the time, Pallas kernels for 0%

profile of v1, /device:TPU:1, one launch (start us, length us, event | category | flops | bytes accessed | tf_op | source)
XLA Modules:
  0.0 177.2 jit_solution(3144981423729476104)
XLA Ops:
  0.6 0.9 convert_reduce_fusion
  1.5 0.7 multiply_add_fusion.2
  2.2 0.7 convert_bitcast_fusion
  2.9 0.1 broadcast_in_dim.10
  2.9 1.5 convolution_convert_fusion
  4.4 0.2 all_to_all.16
  4.6 34.6 %all_to_all.24 = bf16[64,4,1408]{2,1,0:T(4,128)(2,1)S(1)} all-to-all(bf16[64,4,1408]{2,1,0:T(4,128)(2,1)S(1)} %all_to_all.16), channel_id=1, replica_groups=mesh['pix'=64,'plane'=4] {'pix'}, dimensions={0} | all-to-all | bytes 1441792 | tf_op jit(solution)/shard_map/all_to_all | solution.py:217
  39.2 0.2 all_to_all.18
  39.3 0.1 slice.90
  39.4 0.1 add_reduce_fusion
  39.5 0.2 copy.19
  39.7 3.0 %copy.20 = bf16[256,32,32]{2,1,0:T(8,128)(2,1)S(1)} copy(bf16[256,32,32]{0,2,1:T(8,128)(2,1)S(1)} %bitcast.64) | data formatting | bytes 1048576 | tf_op jit(solution)/shard_map/reshape | solution.py:226
  42.7 0.0 copy-start.8
  42.8 0.1 iota_add_fusion
  42.9 2.8 %fusion.1 = bf16[256,256,32]{1,2,0:T(8,128)(2,1)S(1)} fusion(bf16[256,32,32]{2,1,0:T(8,128)(2,1)S(1)} %copy.20, s32[256,32]{1,0:T(8,128)S(1)} %iota_add_fusion), kind=kOutput, calls=%fused_computation.5 | convolution fusion | flops 136314880 | bytes 4751360 | tf_op jit(solution)/shard_map/srj,sjc->rsc/dot_general | solution.py:227
  45.7 0.0 copy-done.8
  45.7 0.0 copy-start.1
  45.7 5.2 %fusion.own_ref = bf16[32,256,256]{2,1,0:T(8,128)(2,1)S(1)} fusion(bf16[1,32,256,256]{3,2,1,0:T(8,128)(2,1)S(1)} %copy-done.8, bf16[256,1408]{1,0:T(8,128)(2,1)S(1)} %all_to_all.18, bf16[256,256,32]{1,2,0:T(8,128)(2,1)S(1)} %fusion.1), kind=kOutput, calls=%fused_computation.2 | convolution fusion | flops 1080033280 | bytes 12713984 | tf_op jit(solution)/shard_map/rsc,st->rct/dot_general | solution.py:230
  50.9 0.0 copy-done.1
  50.9 0.0 copy-start
  50.9 1.9 %copy-done = bf16[32,256,256]{2,1,0:T(8,128)(2,1)} copy-done((bf16[32,256,256]{2,1,0:T(8,128)(2,1)}, bf16[32,256,256]{2,1,0:T(8,128)(2,1)S(1)}, u32[]{:S(2)}) %copy-start) | copy-done | bytes 4194328
  52.9 0.0 copy-start.3
  52.9 2.3 %fusion.65 = (bf16[15,256,256]{2,1,0:T(8,128)(2,1)}, bf16[15,256,256]{2,1,0:T(8,128)(2,1)}) fusion(bf16[32,256,256]{2,1,0:T(8,128)(2,1)S(1)} %fusion.own_ref), kind=kLoop, calls=%fused_computation.113 | loop fusion | bytes 7864320 | tf_op jit(solution)/shard_map/slice | solution.py:239
  55.1 3.2 %collective-permute-start = (bf16[15,256,256]{2,1,0:T(8,128)(2,1)}, bf16[15,256,256]{2,1,0:T(8,128)(2,1)S(1)}, u32[]{:S(2)}, u32[]{:S(2)}) collective-permute-start(bf16[15,256,256]{2,1,0:T(8,128)(2,1)} %get-tuple-element.11), channel_id=1, source_target_pairs={{0,4},{4,8},{8,12},{12,16},{16,20},{20,24},{24,28},{28,32},{32,36}... | collective-permute-start | bytes 5898248 | tf_op jit(solution)/shard_map/ppermute | solution.py:238
  58.3 1.9 %collective-permute-start.1 = (bf16[15,256,256]{2,1,0:T(8,128)(2,1)}, bf16[15,256,256]{2,1,0:T(8,128)(2,1)}, u32[]{:S(2)}, u32[]{:S(2)}) collective-permute-start(bf16[15,256,256]{2,1,0:T(8,128)(2,1)} %get-tuple-element.10), channel_id=1, source_target_pairs={{4,0},{8,4},{12,8},{16,12},{20,16},{24,20},{28,24},{32,28},{36,32}... | collective-permute-start | bytes 5898248 | tf_op jit(solution)/shard_map/ppermute | solution.py:239
  60.3 0.0 copy-done.3
  60.3 0.1 multiply_reduce_fusion
  60.4 0.0 copy-done.7
  60.4 0.0 copy-done.9
  60.4 3.5 %fusion.4 = f32[8192]{0:T(1024)S(1)} fusion(bf16[8192,256]{1,0:T(8,128)(2,1)} %bitcast.63, bf16[256,256]{1,0:T(8,128)(2,1)S(1)} %copy-done.9), kind=kOutput, calls=%fused_computation.9 | convolution fusion | flops 1077927936 | bytes 4358144 | tf_op jit(solution)/shard_map/dot_general | solution.py:245
  64.0 3.1 %collective-permute-start.2 = (f32[1,32,256]{2,1,0:T(8,128)S(1)}, f32[1,32,256]{2,1,0:T(8,128)S(1)}, u32[]{:S(2)}, u32[]{:S(2)}) collective-permute-start(f32[1,32,256]{2,1,0:T(8,128)S(1)} %div.43), channel_id=1, source_target_pairs={{0,1},{1,2},{2,3},{4,5},{5,6},{6,7},{8,9},{9,10},{10,11},{12,13},{... | collective-permute-start | bytes 98312 | tf_op jit(solution)/shard_map/ppermute | solution.py:28
  67.1 1.5 collective-permute-start.3
  68.6 0.6 add_convert_fusion.edge_ref
  69.2 6.5 %copy.28 = bf16[256,256,32]{1,0,2:T(8,128)(2,1)} copy(bf16[256,256,32]{1,2,0:T(8,128)(2,1)} %copy-done.1) | data formatting | bytes 8388608 | tf_op jit(solution)/shard_map/srj,sjc->rsc/dot_general | solution.py:227
  75.7 0.0 collective-permute-done.2
  75.7 0.0 collective-permute-done.3
  75.8 4.4 %collective-permute-done.top_ref = bf16[15,256,256]{2,1,0:T(8,128)(2,1)S(1)} collective-permute-done((bf16[15,256,256]{2,1,0:T(8,128)(2,1)}, bf16[15,256,256]{2,1,0:T(8,128)(2,1)S(1)}, u32[]{:S(2)}, u32[]{:S(2)}) %collective-permute-start) | collective-permute-done | bytes 1966112 | tf_op jit(solution)/shard_map/ppermute | solution.py:238
  80.2 4.4 %collective-permute-done.1.bot_ref = bf16[15,256,256]{2,1,0:T(8,128)(2,1)} collective-permute-done((bf16[15,256,256]{2,1,0:T(8,128)(2,1)}, bf16[15,256,256]{2,1,0:T(8,128)(2,1)}, u32[]{:S(2)}, u32[]{:S(2)}) %collective-permute-start.1) | collective-permute-done | bytes 1966112 | tf_op jit(solution)/shard_map/ppermute | solution.py:239
  84.6 2.6 %broadcast_in_dim.12.recip_ref = f32[32,256,128]{2,1,0:T(8,128)} broadcast(f32[32,256]{1,0:T(8,128)S(1)} %fusion.55), dimensions={0,1} | broadcast | bytes 4227072 | tf_op jit(solution)/shard_map/broadcast_in_dim | solution.py:256
  87.2 0.8 broadcast_in_dim.11.scale_ref
  87.9 0.0 copy-done.2
  87.9 64.2 %shard_map.122 = (bf16[32,256,256]{2,1,0:T(8,128)(2,1)}, f32[256,256]{1,0:T(8,128)}) custom-call(f32[2]{0:T(128)} %add_convert_fusion.edge_ref, bf16[15,256,256]{2,1,0:T(8,128)(2,1)} %copy-done.2, bf16[32,256,256]{2,1,0:T(8,128)(2,1)} %copy-done, bf16[15,256,256]{2,1,0:T(8,128)(2,1)} %collective-permute-done.1.bot_ref, ...), custom_call_target="tpu_custom_call" | custom-call | tf_op jit(solution)/shard_map/pallas_call | solution.py:170
  152.1 1.7 all_to_all.19
  153.8 8.4 %all-to-all-start.1 = ((f32[64,4,256]{2,1,0:T(4,128)}), f32[64,4,256]{2,1,0:T(4,128)S(1)}, u32[]{:S(2)}, u32[]{:S(2)}) async-start(f32[64,4,256]{2,1,0:T(4,128)} %all_to_all.19), calls=%async_computation.1 | async-start | bytes 524288 | tf_op jit(solution)/shard_map/all_to_all | solution.py:264
  162.3 0.0 copy-done.5
  162.3 0.0 copy-done.6
  162.3 11.9 %all-to-all-done.1 = f32[64,4,256]{2,1,0:T(4,128)S(1)} async-done(((f32[64,4,256]{2,1,0:T(4,128)}), f32[64,4,256]{2,1,0:T(4,128)S(1)}, u32[]{:S(2)}, u32[]{:S(2)}) %all-to-all-start.1) | async-done | bytes 262176 | tf_op jit(solution)/shard_map/all_to_all | solution.py:264
  174.2 0.1 all_to_all.21
  174.3 0.0 copy-done.4
  174.3 0.3 fusion.5
  174.6 0.2 fusion.15
  174.8 0.2 multiply_add_fusion
  175.0 0.2 fusion.18
  175.2 0.1 fusion.38
  175.3 0.1 fusion.40
  175.4 0.1 fusion.20
  175.5 0.1 fusion.22
  175.6 0.1 fusion.42
  175.8 0.1 fusion.44
  175.9 0.1 fusion.46
  176.0 0.1 fusion.24
  176.1 0.1 fusion.26
  176.2 0.1 fusion.28
  176.4 0.8 fusion.34
  (14 shorter events, 0.1 us)
Async XLA Ops:
  42.7 2.9 %copy-start.8 = (bf16[1,32,256,256]{3,2,1,0:T(8,128)(2,1)S(1)}, bf16[1,32,256,256]{3,2,1,0:T(8,128)(2,1)}, u32[]{:S(2)}) copy-start(bf16[1,32,256,256]{3,2,1,0:T(8,128)(2,1)} %param.11) | copy-start | bytes 12582916
  45.7 5.2 %copy-start.1 = (bf16[256,256,32]{1,2,0:T(8,128)(2,1)}, bf16[256,256,32]{1,2,0:T(8,128)(2,1)S(1)}, u32[]{:S(2)}) copy-start(bf16[256,256,32]{1,2,0:T(8,128)(2,1)S(1)} %fusion.1) | copy-start | bytes 12582916
  50.9 2.0 %copy-start = (bf16[32,256,256]{2,1,0:T(8,128)(2,1)}, bf16[32,256,256]{2,1,0:T(8,128)(2,1)S(1)}, u32[]{:S(2)}) copy-start(bf16[32,256,256]{2,1,0:T(8,128)(2,1)S(1)} %fusion.own_ref) | copy-start | bytes 12582916
  52.9 7.4 %copy-start.3 = (bf16[1,128,1024]{2,1,0:T(8,128)(2,1)S(1)}, bf16[1,128,1024]{2,1,0:T(8,128)(2,1)}, u32[]{:S(2)}) copy-start(bf16[1,128,1024]{2,1,0:T(8,128)(2,1)} %param.12) | copy-start | bytes 786436
  52.9 7.6 %copy-start.7 = (f32[1,256]{1,0:T(1,128)S(1)}, f32[1,256]{1,0:T(1,128)}, u32[]{:S(2)}) copy-start(f32[1,256]{1,0:T(1,128)} %param.16) | copy-start | bytes 3076
  52.9 7.6 %copy-start.9 = (bf16[256,256]{1,0:T(8,128)(2,1)S(1)}, bf16[256,256]{1,0:T(8,128)(2,1)}, u32[]{:S(2)}) copy-start(bf16[256,256]{1,0:T(8,128)(2,1)} %constant.48.clone) | copy-start | bytes 393220
  55.1 25.1 %collective-permute-start = (bf16[15,256,256]{2,1,0:T(8,128)(2,1)}, bf16[15,256,256]{2,1,0:T(8,128)(2,1)S(1)}, u32[]{:S(2)}, u32[]{:S(2)}) collective-permute-start(bf16[15,256,256]{2,1,0:T(8,128)(2,1)} %get-tuple-element.11), channel_id=1, source_target_pairs={{0,4},{4,8},{8,12},{12,16},{16,20},{20,24},{24,28},{28,32},{32,36}... | collective-permute-start | bytes 5898248 | tf_op jit(solution)/shard_map/ppermute | solution.py:238
  58.3 26.3 %collective-permute-start.1 = (bf16[15,256,256]{2,1,0:T(8,128)(2,1)}, bf16[15,256,256]{2,1,0:T(8,128)(2,1)}, u32[]{:S(2)}, u32[]{:S(2)}) collective-permute-start(bf16[15,256,256]{2,1,0:T(8,128)(2,1)} %get-tuple-element.10), channel_id=1, source_target_pairs={{4,0},{8,4},{12,8},{16,12},{20,16},{24,20},{28,24},{32,28},{36,32}... | collective-permute-start | bytes 5898248 | tf_op jit(solution)/shard_map/ppermute | solution.py:239
  64.0 11.8 %collective-permute-start.2 = (f32[1,32,256]{2,1,0:T(8,128)S(1)}, f32[1,32,256]{2,1,0:T(8,128)S(1)}, u32[]{:S(2)}, u32[]{:S(2)}) collective-permute-start(f32[1,32,256]{2,1,0:T(8,128)S(1)} %div.43), channel_id=1, source_target_pairs={{0,1},{1,2},{2,3},{4,5},{5,6},{6,7},{8,9},{9,10},{10,11},{12,13},{... | collective-permute-start | bytes 98312 | tf_op jit(solution)/shard_map/ppermute | solution.py:28
  67.1 8.6 %collective-permute-start.3 = (f32[1,32,256]{2,1,0:T(8,128)S(1)}, f32[1,32,256]{2,1,0:T(8,128)S(1)}, u32[]{:S(2)}, u32[]{:S(2)}) collective-permute-start(f32[1,32,256]{2,1,0:T(8,128)S(1)} %div.43), channel_id=1, source_target_pairs={{1,0},{2,1},{3,2},{5,4},{6,5},{7,6},{9,8},{10,9},{11,10},{13,12},{... | collective-permute-start | bytes 98312 | tf_op jit(solution)/shard_map/ppermute | solution.py:29
  80.2 7.7 %copy-start.2 = (bf16[15,256,256]{2,1,0:T(8,128)(2,1)}, bf16[15,256,256]{2,1,0:T(8,128)(2,1)S(1)}, u32[]{:S(2)}) copy-start(bf16[15,256,256]{2,1,0:T(8,128)(2,1)S(1)} %collective-permute-done.top_ref) | copy-start | bytes 5898244
  87.9 74.3 %copy-start.5 = (f32[1,128]{1,0:T(1,128)S(1)}, f32[1,128]{1,0:T(1,128)}, u32[]{:S(2)}) copy-start(f32[1,128]{1,0:T(1,128)} %param.18) | copy-start | bytes 1540
  87.9 74.3 %copy-start.6 = (f32[1,128]{1,0:T(1,128)S(1)}, f32[1,128]{1,0:T(1,128)}, u32[]{:S(2)}) copy-start(f32[1,128]{1,0:T(1,128)} %param.17) | copy-start | bytes 1540
  87.9 86.4 %copy-start.4 = (bf16[1,128,256]{2,1,0:T(8,128)(2,1)S(1)}, bf16[1,128,256]{2,1,0:T(8,128)(2,1)}, u32[]{:S(2)}) copy-start(bf16[1,128,256]{2,1,0:T(8,128)(2,1)} %param.13) | copy-start | bytes 196612
  153.8 20.4 %all-to-all-start.1 = ((f32[64,4,256]{2,1,0:T(4,128)}), f32[64,4,256]{2,1,0:T(4,128)S(1)}, u32[]{:S(2)}, u32[]{:S(2)}) async-start(f32[64,4,256]{2,1,0:T(4,128)} %all_to_all.19), calls=%async_computation.1 | async-start | bytes 524288 | tf_op jit(solution)/shard_map/all_to_all | solution.py:264

commit v2 on v1

--- a/solution.py
+++ b/solution.py
@@ -1,3 +1,4 @@
+import functools
 import numpy as np
 import ml_dtypes
 import jax
@@ -188,6 +189,70 @@
     )(edge, top, own, bot, jnp.asarray(wcat), jnp.asarray(blur), scale, recip, frows)
 
 
+MESH = pl.DeviceIdType.MESH
+
+
+def exchange_kernel(out_ref, in_ref, send_sem, recv_sem, local_sem):
+    count = out_ref.shape[0]
+    me = lax.axis_index("pix")
+    barrier = pltpu.get_barrier_semaphore()
+
+    def peer_at(k):
+        return lax.rem(me + k, count)
+
+    def source_at(k):
+        return lax.rem(me + count - k, count)
+
+    def remote(target, block):
+        return pltpu.make_async_remote_copy(
+            src_ref=out_ref.at[target],
+            dst_ref=in_ref.at[block],
+            send_sem=send_sem.at[target],
+            recv_sem=recv_sem.at[block],
+            device_id={"pix": target},
+            device_id_type=MESH,
+        )
+
+    def greet(k, c):
+        pl.semaphore_signal(barrier, inc=1, device_id={"pix": peer_at(k)}, device_id_type=MESH)
+        return c
+
+    lax.fori_loop(1, count, greet, 0)
+    pl.semaphore_wait(barrier, count - 1)
+
+    def launch(k, c):
+        remote(peer_at(k), me).start()
+        return c
+
+    lax.fori_loop(1, count, launch, 0)
+    local = pltpu.make_async_copy(out_ref.at[me], in_ref.at[me], local_sem)
+    local.start()
+    local.wait()
+
+    def finish(k, c):
+        remote(peer_at(k), me).wait_send()
+        remote(source_at(k), source_at(k)).wait_recv()
+        return c
+
+    lax.fori_loop(1, count, finish, 0)
+
+
+def exchange(outbox, collective):
+    count = outbox.shape[0]
+    return pl.pallas_call(
+        exchange_kernel,
+        out_shape=jax.ShapeDtypeStruct(outbox.shape, outbox.dtype),
+        in_specs=[pl.BlockSpec(memory_space=pl.ANY)],
+        out_specs=pl.BlockSpec(memory_space=pl.ANY),
+        scratch_shapes=[
+            pltpu.SemaphoreType.DMA((count,)),
+            pltpu.SemaphoreType.DMA((count,)),
+            pltpu.SemaphoreType.DMA,
+        ],
+        compiler_params=pltpu.CompilerParams(collective_id=collective, has_side_effects=True),
+    )(outbox)
+
+
 def on_device(movie, footprints, traces, stripe, column, annulus_gain, decay_slow, decay_fast):
     pix_count = lax.axis_size("pix")
     row_count = movie.shape[1]
@@ -214,7 +279,7 @@
     outbox = lax.dot_general(
         placement_b, payload, contract_first, preferred_element_type=jnp.float32
     ).astype(jnp.bfloat16)
-    inbox = lax.all_to_all(outbox, "pix", split_axis=0, concat_axis=0, tiled=True)
+    inbox = exchange(outbox.reshape(pix_count, capacity, -1), 0).reshape(slot_count, -1)
     tile_inbox = inbox[:, :tile_width]
     trace_inbox = inbox[:, tile_width : tile_width + trace_width]
     column_inbox = inbox[:, tile_width + trace_width].astype(jnp.int32)
@@ -261,7 +326,9 @@
     background, slot_gradient = stencil(
         edge, top_halo, residual, bottom_halo, scale, recip, frows, frame_block
     )
-    home_gradient = lax.all_to_all(slot_gradient, "pix", split_axis=0, concat_axis=0, tiled=True)
+    home_gradient = exchange(slot_gradient.reshape(pix_count, capacity, -1), 1).reshape(
+        slot_count, -1
+    )
     gradient = lax.dot_general(
         placement.astype(jnp.float32),
         home_gradient,

time: 178 us -> 171 us (0.961)
  Pallas kernels: 64.2 us -> 112 us
  blocking collectives: 34.6 us -> 0 us
  waiting for transfers between devices: 20.8 us -> 10.9 us
  starting transfers between devices: 18.1 us -> 9.42 us
  matrix products: 13.2 us -> 11.1 us
    pallas_call x0 -> x2, Pallas kernels: none -> 47.4 us  [exchange(): pl.pallas_call(exchange_kernel, out_shape=jax.ShapeDtypeStruct(outbox.sha...]
    all_to_all x1 -> x0, blocking collectives: 34.6 us -> none  [on_device(): lax.all_to_all(outbox, 'pix', split_axis=0, concat_axis=0, tiled=True)]
    all_to_all x1 -> x0, waiting for transfers between devices: 11.9 us -> none  [on_device(): lax.all_to_all(slot_gradient, 'pix', split_axis=0, concat_axis=0, tiled=T...]
    all_to_all x1 -> x0, starting transfers between devices: 8.39 us -> none  [on_device(): lax.all_to_all(slot_gradient, 'pix', split_axis=0, concat_axis=0, tiled=T...]
    reshape x0 -> x4, local copies, waits for them, and re-layouts: none -> 5.32 us  [the longest x1 1.72 us: on_device(): slot_gradient.reshape(pix_count, capacity, -1)]
    dot_general x1, matrix products: 3.5 us -> 1.34 us  [on_device(): jnp.dot(residual.reshape(row_count * col_count, frame_count), jnp.asarray...]
    all_to_all x4 -> x0, local copies, waits for them, and re-layouts: 2.15 us -> none  [the longest x2 1.82 us: on_device(): lax.all_to_all(slot_gradient, 'pix', split_axis=0, concat_axis=0, tiled=T...]
    ppermute x1, waiting for transfers between devices: 4.42 us -> 6.46 us  [on_device(): top_halo = lax.ppermute(residual[row_count - halo:], 'pix', up)]
  transfers between devices with their start and end apart: 5 -> 4, of which waited for: 3 -> 2; matrix products, arithmetic and copies ran while one was open for 6% -> 5% of each run, Pallas kernels for 0% -> 0%
where the time goes in v2:
time: 171 us
  Pallas kernels  112 us (65%)
  local copies, waits for them, and re-layouts  21.1 us (12%)
  matrix products  11.1 us (6%)
  waiting for transfers between devices  10.9 us (6%)
  starting transfers between devices  9.42 us (6%)
  other arithmetic  5.69 us (3%)
    pallas_call x1, Pallas kernels, stencil(): pl.pallas_call(stencil_kernel, grid=grid, in_specs=[pl.BlockSpec(memory_s...  64.2 us
    pallas_call x2, Pallas kernels, exchange(): pl.pallas_call(exchange_kernel, out_shape=jax.ShapeDtypeStruct(outbox.sha...  47.4 us
    dot_general x1, local copies, waits for them, and re-layouts, on_device(): jnp.einsum('srj,sjc->rsc', tile_grid, column_onehot, preferred_element_ty...  6.53 us
    ppermute x1, waiting for transfers between devices, on_device(): top_halo = lax.ppermute(residual[row_count - halo:], 'pix', up)  6.46 us
    dot_general x1, matrix products, on_device(): jnp.einsum('rsc,st->rct', frows, trace_inbox, preferred_element_type=jnp....  5.21 us
    ppermute x1, waiting for transfers between devices, on_device(): bottom_halo = lax.ppermute(residual[:halo], 'pix', down)  4.39 us
  transfers between devices with their start and end apart: 4, of which 2 were waited for; matrix products, arithmetic and copies ran while one was open for 5% of the time, Pallas kernels for 0%

profile of v2, /device:TPU:1, one launch (start us, length us, event | category | flops | bytes accessed | tf_op | source)
XLA Modules:
  0.0 170.8 jit_solution(3283069033214133863)
XLA Ops:
  0.6 0.9 convert_reduce_fusion
  1.5 0.7 multiply_add_fusion.2
  2.2 0.7 convert_bitcast_fusion
  2.9 0.1 broadcast_in_dim.10
  2.9 1.5 convolution_convert_fusion
  4.4 1.0 reshape.222.out_ref
  5.4 29.9 %shard_map.122 = bf16[64,4,1408]{2,1,0:T(4,128)(2,1)} custom-call(bf16[64,4,1408]{2,1,0:T(4,128)(2,1)} %reshape.222.out_ref), custom_call_target="tpu_custom_call" | custom-call | tf_op jit(solution)/shard_map/pallas_call | solution.py:242
  35.3 1.5 reshape.223
  36.9 0.1 slice.90
  36.9 0.1 add_reduce_fusion
  37.1 0.2 copy.19
  37.3 3.0 %copy.20 = bf16[256,32,32]{2,1,0:T(8,128)(2,1)S(1)} copy(bf16[256,32,32]{0,2,1:T(8,128)(2,1)S(1)} %bitcast.64) | data formatting | bytes 1048576 | tf_op jit(solution)/shard_map/reshape | solution.py:291
  40.3 0.0 copy-start.8
  40.3 0.1 iota_add_fusion
  40.4 2.8 %fusion.1 = bf16[256,256,32]{1,2,0:T(8,128)(2,1)S(1)} fusion(bf16[256,32,32]{2,1,0:T(8,128)(2,1)S(1)} %copy.20, s32[256,32]{1,0:T(8,128)S(1)} %iota_add_fusion), kind=kOutput, calls=%fused_computation.5 | convolution fusion | flops 136314880 | bytes 4751360 | tf_op jit(solution)/shard_map/srj,sjc->rsc/dot_general | solution.py:292
  43.2 0.0 copy-done.8
  43.2 0.0 copy-start.1
  43.2 5.2 %fusion.own_ref = bf16[32,256,256]{2,1,0:T(8,128)(2,1)S(1)} fusion(bf16[1,32,256,256]{3,2,1,0:T(8,128)(2,1)S(1)} %copy-done.8, bf16[256,1408]{1,0:T(8,128)(2,1)S(1)} %reshape.223, bf16[256,256,32]{1,2,0:T(8,128)(2,1)S(1)} %fusion.1), kind=kOutput, calls=%fused_computation.2 | convolution fusion | flops 1080033280 | bytes 12713984 | tf_op jit(solution)/shard_map/rsc,st->rct/dot_general | solution.py:295
  48.4 0.0 copy-done.1
  48.4 0.0 copy-start
  48.5 0.0 copy-start.9
  48.5 2.5 %fusion.65 = (bf16[15,256,256]{2,1,0:T(8,128)(2,1)}, bf16[15,256,256]{2,1,0:T(8,128)(2,1)}) fusion(bf16[32,256,256]{2,1,0:T(8,128)(2,1)S(1)} %fusion.own_ref), kind=kLoop, calls=%fused_computation.113 | loop fusion | bytes 7864320 | tf_op jit(solution)/shard_map/slice | solution.py:304
  51.0 2.9 %collective-permute-start = (bf16[15,256,256]{2,1,0:T(8,128)(2,1)}, bf16[15,256,256]{2,1,0:T(8,128)(2,1)S(1)}, u32[]{:S(2)}, u32[]{:S(2)}) collective-permute-start(bf16[15,256,256]{2,1,0:T(8,128)(2,1)} %get-tuple-element.11), channel_id=1, source_target_pairs={{0,4},{4,8},{8,12},{12,16},{16,20},{20,24},{24,28},{28,32},{32,36}... | collective-permute-start | bytes 5898248 | tf_op jit(solution)/shard_map/ppermute | solution.py:303
  53.9 1.9 %collective-permute-start.1 = (bf16[15,256,256]{2,1,0:T(8,128)(2,1)}, bf16[15,256,256]{2,1,0:T(8,128)(2,1)}, u32[]{:S(2)}, u32[]{:S(2)}) collective-permute-start(bf16[15,256,256]{2,1,0:T(8,128)(2,1)} %get-tuple-element.10), channel_id=1, source_target_pairs={{4,0},{8,4},{12,8},{16,12},{20,16},{24,20},{28,24},{32,28},{36,32}... | collective-permute-start | bytes 5898248 | tf_op jit(solution)/shard_map/ppermute | solution.py:304
  55.8 0.0 copy-done.9
  55.9 0.0 copy-start.3
  55.9 0.0 copy-start.7
  55.9 0.0 copy-start.5
  55.9 0.0 copy-start.6
  55.9 1.3 fusion.4
  57.2 0.0 copy-done
  57.3 3.1 %collective-permute-start.2 = (f32[1,32,256]{2,1,0:T(8,128)S(1)}, f32[1,32,256]{2,1,0:T(8,128)S(1)}, u32[]{:S(2)}, u32[]{:S(2)}) collective-permute-start(f32[1,32,256]{2,1,0:T(8,128)S(1)} %div.43), channel_id=1, source_target_pairs={{0,1},{1,2},{2,3},{4,5},{5,6},{6,7},{8,9},{9,10},{10,11},{12,13},{... | collective-permute-start | bytes 98312 | tf_op jit(solution)/shard_map/ppermute | solution.py:29
  60.4 1.5 collective-permute-start.3
  61.9 0.0 copy-done.3
  61.9 0.1 multiply_reduce_fusion
  62.1 0.0 copy-done.7
  62.1 0.6 add_convert_fusion.edge_ref
  62.7 6.5 %copy.28 = bf16[256,256,32]{1,0,2:T(8,128)(2,1)} copy(bf16[256,256,32]{1,2,0:T(8,128)(2,1)} %copy-done.1) | data formatting | bytes 8388608 | tf_op jit(solution)/shard_map/srj,sjc->rsc/dot_general | solution.py:292
  69.3 0.0 collective-permute-done.2
  69.3 0.0 collective-permute-done.3
  69.3 6.5 %collective-permute-done.top_ref = bf16[15,256,256]{2,1,0:T(8,128)(2,1)S(1)} collective-permute-done((bf16[15,256,256]{2,1,0:T(8,128)(2,1)}, bf16[15,256,256]{2,1,0:T(8,128)(2,1)S(1)}, u32[]{:S(2)}, u32[]{:S(2)}) %collective-permute-start) | collective-permute-done | bytes 1966112 | tf_op jit(solution)/shard_map/ppermute | solution.py:303
  75.8 4.4 %collective-permute-done.1.bot_ref = bf16[15,256,256]{2,1,0:T(8,128)(2,1)} collective-permute-done((bf16[15,256,256]{2,1,0:T(8,128)(2,1)}, bf16[15,256,256]{2,1,0:T(8,128)(2,1)}, u32[]{:S(2)}, u32[]{:S(2)}) %collective-permute-start.1) | collective-permute-done | bytes 1966112 | tf_op jit(solution)/shard_map/ppermute | solution.py:304
  80.2 2.6 %broadcast_in_dim.12.recip_ref = f32[32,256,128]{2,1,0:T(8,128)} broadcast(f32[32,256]{1,0:T(8,128)S(1)} %fusion.55), dimensions={0,1} | broadcast | bytes 4227072 | tf_op jit(solution)/shard_map/broadcast_in_dim | solution.py:321
  82.8 0.8 broadcast_in_dim.11.scale_ref
  83.5 0.0 copy-done.2
  83.5 64.2 %shard_map.123 = (bf16[32,256,256]{2,1,0:T(8,128)(2,1)}, f32[256,256]{1,0:T(8,128)}) custom-call(f32[2]{0:T(128)} %add_convert_fusion.edge_ref, bf16[15,256,256]{2,1,0:T(8,128)(2,1)} %copy-done.2, bf16[32,256,256]{2,1,0:T(8,128)(2,1)} %copy-done, bf16[15,256,256]{2,1,0:T(8,128)(2,1)} %collective-permute-done.1.bot_ref, ...), custom_call_target="tpu_custom_call" | custom-call | tf_op jit(solution)/shard_map/pallas_call | solution.py:171
  147.7 1.7 %reshape.226.out_ref = f32[64,4,256]{2,1,0:T(4,128)} reshape(f32[256,256]{1,0:T(8,128)} %get-tuple-element.5) | data formatting | bytes 524288 | tf_op jit(solution)/shard_map/reshape | solution.py:329
  149.4 17.5 %shard_map.124 = f32[64,4,256]{2,1,0:T(4,128)} custom-call(f32[64,4,256]{2,1,0:T(4,128)} %reshape.226.out_ref), custom_call_target="tpu_custom_call" | custom-call | tf_op jit(solution)/shard_map/pallas_call | solution.py:242
  167.0 1.0 reshape.227
  168.0 0.3 fusion.5
  168.3 0.2 fusion.15
  168.5 0.2 multiply_add_fusion
  168.6 0.2 fusion.18
  168.8 0.1 fusion.38
  168.9 0.1 fusion.40
  169.1 0.1 fusion.20
  169.2 0.1 fusion.22
  169.3 0.1 fusion.42
  169.4 0.1 fusion.44
  169.6 0.1 fusion.46
  169.7 0.1 fusion.24
  169.8 0.1 fusion.26
  169.9 0.1 fusion.28
  170.0 0.8 fusion.34
  (13 shorter events, 0.1 us)
Async XLA Ops:
  40.3 2.9 %copy-start.8 = (bf16[1,32,256,256]{3,2,1,0:T(8,128)(2,1)S(1)}, bf16[1,32,256,256]{3,2,1,0:T(8,128)(2,1)}, u32[]{:S(2)}) copy-start(bf16[1,32,256,256]{3,2,1,0:T(8,128)(2,1)} %param.11) | copy-start | bytes 12582916
  43.2 5.2 %copy-start.1 = (bf16[256,256,32]{1,2,0:T(8,128)(2,1)}, bf16[256,256,32]{1,2,0:T(8,128)(2,1)S(1)}, u32[]{:S(2)}) copy-start(bf16[256,256,32]{1,2,0:T(8,128)(2,1)S(1)} %fusion.1) | copy-start | bytes 12582916
  48.4 8.8 %copy-start = (bf16[32,256,256]{2,1,0:T(8,128)(2,1)}, bf16[32,256,256]{2,1,0:T(8,128)(2,1)S(1)}, u32[]{:S(2)}) copy-start(bf16[32,256,256]{2,1,0:T(8,128)(2,1)S(1)} %fusion.own_ref) | copy-start | bytes 12582916
  48.5 7.4 %copy-start.9 = (bf16[256,256]{1,0:T(8,128)(2,1)S(1)}, bf16[256,256]{1,0:T(8,128)(2,1)}, u32[]{:S(2)}) copy-start(bf16[256,256]{1,0:T(8,128)(2,1)} %constant.48.clone) | copy-start | bytes 393220
  51.0 24.8 %collective-permute-start = (bf16[15,256,256]{2,1,0:T(8,128)(2,1)}, bf16[15,256,256]{2,1,0:T(8,128)(2,1)S(1)}, u32[]{:S(2)}, u32[]{:S(2)}) collective-permute-start(bf16[15,256,256]{2,1,0:T(8,128)(2,1)} %get-tuple-element.11), channel_id=1, source_target_pairs={{0,4},{4,8},{8,12},{12,16},{16,20},{20,24},{24,28},{28,32},{32,36}... | collective-permute-start | bytes 5898248 | tf_op jit(solution)/shard_map/ppermute | solution.py:303
  53.9 26.3 %collective-permute-start.1 = (bf16[15,256,256]{2,1,0:T(8,128)(2,1)}, bf16[15,256,256]{2,1,0:T(8,128)(2,1)}, u32[]{:S(2)}, u32[]{:S(2)}) collective-permute-start(bf16[15,256,256]{2,1,0:T(8,128)(2,1)} %get-tuple-element.10), channel_id=1, source_target_pairs={{4,0},{8,4},{12,8},{16,12},{20,16},{24,20},{28,24},{32,28},{36,32}... | collective-permute-start | bytes 5898248 | tf_op jit(solution)/shard_map/ppermute | solution.py:304
  55.9 6.1 %copy-start.3 = (bf16[1,128,1024]{2,1,0:T(8,128)(2,1)S(1)}, bf16[1,128,1024]{2,1,0:T(8,128)(2,1)}, u32[]{:S(2)}) copy-start(bf16[1,128,1024]{2,1,0:T(8,128)(2,1)} %param.12) | copy-start | bytes 786436
  55.9 6.2 %copy-start.7 = (f32[1,256]{1,0:T(1,128)S(1)}, f32[1,256]{1,0:T(1,128)}, u32[]{:S(2)}) copy-start(f32[1,256]{1,0:T(1,128)} %param.16) | copy-start | bytes 3076
  55.9 6.2 %copy-start.5 = (f32[1,128]{1,0:T(1,128)S(1)}, f32[1,128]{1,0:T(1,128)}, u32[]{:S(2)}) copy-start(f32[1,128]{1,0:T(1,128)} %param.18) | copy-start | bytes 1540
  55.9 6.2 %copy-start.6 = (f32[1,128]{1,0:T(1,128)S(1)}, f32[1,128]{1,0:T(1,128)}, u32[]{:S(2)}) copy-start(f32[1,128]{1,0:T(1,128)} %param.17) | copy-start | bytes 1540
  57.3 12.0 %collective-permute-start.2 = (f32[1,32,256]{2,1,0:T(8,128)S(1)}, f32[1,32,256]{2,1,0:T(8,128)S(1)}, u32[]{:S(2)}, u32[]{:S(2)}) collective-permute-start(f32[1,32,256]{2,1,0:T(8,128)S(1)} %div.43), channel_id=1, source_target_pairs={{0,1},{1,2},{2,3},{4,5},{5,6},{6,7},{8,9},{9,10},{10,11},{12,13},{... | collective-permute-start | bytes 98312 | tf_op jit(solution)/shard_map/ppermute | solution.py:29
  60.4 8.9 %collective-permute-start.3 = (f32[1,32,256]{2,1,0:T(8,128)S(1)}, f32[1,32,256]{2,1,0:T(8,128)S(1)}, u32[]{:S(2)}, u32[]{:S(2)}) collective-permute-start(f32[1,32,256]{2,1,0:T(8,128)S(1)} %div.43), channel_id=1, source_target_pairs={{1,0},{2,1},{3,2},{5,4},{6,5},{7,6},{9,8},{10,9},{11,10},{13,12},{... | collective-permute-start | bytes 98312 | tf_op jit(solution)/shard_map/ppermute | solution.py:30
  75.8 7.7 %copy-start.2 = (bf16[15,256,256]{2,1,0:T(8,128)(2,1)}, bf16[15,256,256]{2,1,0:T(8,128)(2,1)S(1)}, u32[]{:S(2)}) copy-start(bf16[15,256,256]{2,1,0:T(8,128)(2,1)S(1)} %collective-permute-done.top_ref) | copy-start | bytes 5898244
  83.5 84.5 %copy-start.4 = (bf16[1,128,256]{2,1,0:T(8,128)(2,1)S(1)}, bf16[1,128,256]{2,1,0:T(8,128)(2,1)}, u32[]{:S(2)}) copy-start(bf16[1,128,256]{2,1,0:T(8,128)(2,1)} %param.13) | copy-start | bytes 196612

commit v3 on v1

--- a/solution.py
+++ b/solution.py
@@ -1,3 +1,4 @@
+import functools
 import numpy as np
 import ml_dtypes
 import jax
@@ -82,7 +83,7 @@
 
 
 def stencil_kernel(edge_ref, top_ref, own_ref, bot_ref, wcat_ref, blur_ref, scale_ref, recip_ref,
-                   frows_ref, back_ref, grad_ref, hsum_ref, ssum_ref, rows_ref):
+                   frows_ref, back_ref, grad_ref, hsum_ref, ssum_ref, rows_ref, norm_ref):
     halo = top_ref.shape[0]
     own = own_ref.shape[0]
     cols = own_ref.shape[1]
@@ -146,22 +147,24 @@
     side = lax.fori_loop(0, own, own_d, side)
     side = lax.fori_loop(0, GR, bot_d, side)
 
-    grad_ref[...] = jnp.zeros_like(grad_ref)
-
     def smooth(y, c):
         acc = taps[GR] * rows_ref[y + GR]
         for o in range(GR):
             acc = acc + taps[o] * (rows_ref[y + o] + rows_ref[y + 2 * GR - o])
-        normalized = (acc * recip_ref[y]).astype(jnp.bfloat16)
-        grad_ref[...] += jnp.dot(frows_ref[y], normalized, preferred_element_type=jnp.float32)
+        norm_ref[y] = (acc * recip_ref[y]).astype(jnp.bfloat16)
         return c
 
     lax.fori_loop(0, own, smooth, 0)
+    frame_block = norm_ref.shape[2]
+    grad_ref[...] = jnp.dot(
+        frows_ref[...], norm_ref[...].reshape(own * cols, frame_block),
+        preferred_element_type=jnp.float32,
+    )
 
 
 def stencil(edge, top, own, bot, scale, recip, frows, frame_block=128):
     halo, own_rows, cols, frames = top.shape[0], own.shape[0], own.shape[1], own.shape[2]
-    slots = frows.shape[1]
+    slots = frows.shape[0]
     ext = 2 * halo + own_rows
     wcat, blur = band_constants(cols)
     grid = (frames // frame_block,)
@@ -174,7 +177,7 @@
             pl.BlockSpec(memory_space=pltpu.SMEM),
             row_block(halo), row_block(own_rows), row_block(halo),
             fixed((2 * cols, cols)), fixed((cols, cols)), fixed((cols, frame_block)),
-            fixed((own_rows, cols, frame_block)), fixed((own_rows, slots, cols)),
+            fixed((own_rows, cols, frame_block)), fixed((slots, own_rows * cols)),
         ],
         out_specs=[row_block(own_rows), pl.BlockSpec((slots, frame_block), lambda j: (0, j))],
         out_shape=[jax.ShapeDtypeStruct(own.shape, jnp.bfloat16),
@@ -183,9 +186,117 @@
             pltpu.VMEM((ext, cols, frame_block), jnp.float32),
             pltpu.VMEM((ext, cols, frame_block), jnp.float32),
             pltpu.VMEM((own_rows + 2 * GR, cols, frame_block), jnp.float32),
+            pltpu.VMEM((own_rows, cols, frame_block), jnp.bfloat16),
         ],
         compiler_params=pltpu.CompilerParams(vmem_limit_bytes=60 * 1024 * 1024),
     )(edge, top, own, bot, jnp.asarray(wcat), jnp.asarray(blur), scale, recip, frows)
+
+
+MESH = pl.DeviceIdType.MESH
+
+
+def exchange_kernel(out_ref, in_ref, mid_ref, first_send, first_recv, second_send, second_recv, local_sem):
+    major, minor = out_ref.shape[0], out_ref.shape[1]
+    me = lax.axis_index("pix")
+    row, col = me // minor, me % minor
+    barrier = pltpu.get_barrier_semaphore()
+
+    def col_peer(k):
+        return lax.rem(col + k, minor)
+
+    def row_peer(k):
+        return lax.rem(row + k, major)
+
+    def first_copy(target_col, source_col):
+        return pltpu.make_async_remote_copy(
+            src_ref=out_ref.at[:, target_col],
+            dst_ref=mid_ref.at[source_col],
+            send_sem=first_send.at[target_col],
+            recv_sem=first_recv.at[source_col],
+            device_id={"pix": row * minor + target_col},
+            device_id_type=MESH,
+        )
+
+    def second_copy(target_row, source_row):
+        return pltpu.make_async_remote_copy(
+            src_ref=mid_ref.at[:, target_row],
+            dst_ref=in_ref.at[source_row],
+            send_sem=second_send.at[target_row],
+            recv_sem=second_recv.at[source_row],
+            device_id={"pix": target_row * minor + col},
+            device_id_type=MESH,
+        )
+
+    def greet_col(k, c):
+        pl.semaphore_signal(barrier, inc=1, device_id={"pix": row * minor + col_peer(k)}, device_id_type=MESH)
+        return c
+
+    def greet_row(k, c):
+        pl.semaphore_signal(barrier, inc=1, device_id={"pix": row_peer(k) * minor + col}, device_id_type=MESH)
+        return c
+
+    lax.fori_loop(1, minor, greet_col, 0)
+    lax.fori_loop(1, major, greet_row, 0)
+    pl.semaphore_wait(barrier, minor + major - 2)
+
+    def launch_first(k, c):
+        first_copy(col_peer(k), col).start()
+        return c
+
+    lax.fori_loop(1, minor, launch_first, 0)
+    local = pltpu.make_async_copy(out_ref.at[:, col], mid_ref.at[col], local_sem)
+    local.start()
+    local.wait()
+
+    def finish_first(k, c):
+        first_copy(col_peer(k), col).wait_send()
+        source = lax.rem(col + minor - k, minor)
+        first_copy(source, source).wait_recv()
+        return c
+
+    lax.fori_loop(1, minor, finish_first, 0)
+
+    def launch_second(k, c):
+        second_copy(row_peer(k), row).start()
+        return c
+
+    lax.fori_loop(1, major, launch_second, 0)
+    local = pltpu.make_async_copy(mid_ref.at[:, row], in_ref.at[row], local_sem)
+    local.start()
+    local.wait()
+
+    def finish_second(k, c):
+        second_copy(row_peer(k), row).wait_send()
+        source = lax.rem(row + major - k, major)
+        second_copy(source, source).wait_recv()
+        return c
+
+    lax.fori_loop(1, major, finish_second, 0)
+
+
+def exchange(outbox, collective):
+    count = outbox.shape[0]
+    major = 4 if count % 4 == 0 and count > 4 else 1
+    minor = count // major
+    blocks = outbox.reshape((major, minor) + outbox.shape[1:])
+    received, _ = pl.pallas_call(
+        exchange_kernel,
+        out_shape=[
+            jax.ShapeDtypeStruct(blocks.shape, outbox.dtype),
+            jax.ShapeDtypeStruct((minor, major) + outbox.shape[1:], outbox.dtype),
+        ],
+        in_specs=[pl.BlockSpec(memory_space=pl.ANY)],
+        out_specs=[pl.BlockSpec(memory_space=pl.ANY), pl.BlockSpec(memory_space=pl.ANY)],
+        scratch_shapes=[
+            pltpu.SemaphoreType.DMA((minor,)),
+            pltpu.SemaphoreType.DMA((minor,)),
+            pltpu.SemaphoreType.DMA((major,)),
+            pltpu.SemaphoreType.DMA((major,)),
+            pltpu.SemaphoreType.DMA,
+        ],
+        compiler_params=pltpu.CompilerParams(collective_id=collective, has_side_effects=True),
+    )(blocks)
+    return received.reshape(outbox.shape)
 
 
 def on_device(movie, footprints, traces, stripe, column, annulus_gain, decay_slow, decay_fast):
@@ -214,7 +325,7 @@
     outbox = lax.dot_general(
         placement_b, payload, contract_first, preferred_element_type=jnp.float32
     ).astype(jnp.bfloat16)
-    inbox = lax.all_to_all(outbox, "pix", split_axis=0, concat_axis=0, tiled=True)
+    inbox = exchange(outbox.reshape(pix_count, capacity, -1), 0).reshape(slot_count, -1)
     tile_inbox = inbox[:, :tile_width]
     trace_inbox = inbox[:, tile_width : tile_width + trace_width]
     column_inbox = inbox[:, tile_width + trace_width].astype(jnp.int32)
@@ -225,10 +336,10 @@
     )
     tile_grid = tile_inbox.reshape(slot_count, FOOT, FOOT)
     frows = jnp.einsum(
-        "srj,sjc->rsc", tile_grid, column_onehot, preferred_element_type=jnp.float32
+        "srj,sjc->src", tile_grid, column_onehot, preferred_element_type=jnp.float32
     ).astype(jnp.bfloat16)
     model_image = jnp.einsum(
-        "rsc,st->rct", frows, trace_inbox, preferred_element_type=jnp.float32
+        "src,st->rct", frows, trace_inbox, preferred_element_type=jnp.float32
     )
     residual = (movie[0].astype(jnp.float32) - model_image).astype(jnp.bfloat16)
     halo = RAD + GR
@@ -259,9 +370,12 @@
     scale = jnp.broadcast_to((annulus_gain[0] / (8.0 * RAD))[:, None], (col_count, frame_block))
     edge = jnp.stack([pix_index > 0, pix_index < pix_count - 1]).astype(jnp.float32)
     background, slot_gradient = stencil(
-        edge, top_halo, residual, bottom_halo, scale, recip, frows, frame_block
-    )
-    home_gradient = lax.all_to_all(slot_gradient, "pix", split_axis=0, concat_axis=0, tiled=True)
+        edge, top_halo, residual, bottom_halo, scale, recip,
+        frows.reshape(slot_count, row_count * col_count), frame_block
+    )
+    home_gradient = exchange(slot_gradient.reshape(pix_count, capacity, -1), 1).reshape(
+        slot_count, -1
+    )
     gradient = lax.dot_general(
         placement.astype(jnp.float32),
         home_gradient,

time: 178 us -> 173 us (0.972)
  Pallas kernels: 64.2 us -> 114 us
  blocking collectives: 34.6 us -> 0 us
  waiting for transfers between devices: 20.8 us -> 8.95 us
  starting transfers between devices: 18.1 us -> 9.67 us
  local copies, waits for them, and re-layouts: 19.6 us -> 23 us
  matrix products: 13.2 us -> 11 us
    pallas_call x0 -> x2, Pallas kernels: none -> 57.4 us  [exchange(): pl.pallas_call(exchange_kernel, out_shape=[jax.ShapeDtypeStruct(blocks.sh...]
    all_to_all x1 -> x0, blocking collectives: 34.6 us -> none  [on_device(): lax.all_to_all(outbox, 'pix', split_axis=0, concat_axis=0, tiled=True)]
    all_to_all x1 -> x0, waiting for transfers between devices: 11.9 us -> none  [on_device(): lax.all_to_all(slot_gradient, 'pix', split_axis=0, concat_axis=0, tiled=T...]
    all_to_all x1 -> x0, starting transfers between devices: 8.39 us -> none  [on_device(): lax.all_to_all(slot_gradient, 'pix', split_axis=0, concat_axis=0, tiled=T...]
    pallas_call x1, Pallas kernels: 64.2 us -> 56.2 us  [stencil(): pl.pallas_call(stencil_kernel, grid=grid, in_specs=[pl.BlockSpec(memory_s...]
    dot_general x1 -> x0, local copies, waits for them, and re-layouts: 6.52 us -> none  [on_device(): jnp.einsum('srj,sjc->rsc', tile_grid, column_onehot, preferred_element_ty...]
    unnamed x20 -> x21, local copies, waits for them, and re-layouts: 1.99 us -> 8.5 us
    another operation x0 -> x4, local copies, waits for them, and re-layouts: none -> 5.33 us  [the longest x2 2.75 us: exchange(): blocks = outbox.reshape((major, minor) + outbox.shape[1:])]
  transfers between devices with their start and end apart: 5 -> 4, of which waited for: 3 -> 2; matrix products, arithmetic and copies ran while one was open for 6% -> 6% of each run, Pallas kernels for 0% -> 0%
where the time goes in v3:
time: 173 us
  Pallas kernels  114 us (66%)
  local copies, waits for them, and re-layouts  23 us (13%)
  matrix products  11 us (6%)
  starting transfers between devices  9.67 us (6%)
  waiting for transfers between devices  8.95 us (5%)
  other arithmetic  5.7 us (3%)
    pallas_call x2, Pallas kernels, exchange(): pl.pallas_call(exchange_kernel, out_shape=[jax.ShapeDtypeStruct(blocks.sh...  57.4 us
    pallas_call x1, Pallas kernels, stencil(): pl.pallas_call(stencil_kernel, grid=grid, in_specs=[pl.BlockSpec(memory_s...  56.2 us
    unnamed x21, local copies, waits for them, and re-layouts  8.5 us
    dot_general x1, matrix products, on_device(): jnp.einsum('src,st->rct', frows, trace_inbox, preferred_element_type=jnp....  5.27 us
    ppermute x1, waiting for transfers between devices, on_device(): top_halo = lax.ppermute(residual[row_count - halo:], 'pix', up)  4.55 us
    ppermute x1, waiting for transfers between devices, on_device(): bottom_halo = lax.ppermute(residual[:halo], 'pix', down)  4.39 us
  transfers between devices with their start and end apart: 4, of which 2 were waited for; matrix products, arithmetic and copies ran while one was open for 6% of the time, Pallas kernels for 0%

profile of v3, /device:TPU:1, one launch (start us, length us, event | category | flops | bytes accessed | tf_op | source)
XLA Modules:
  0.0 173.0 jit_solution(10030782977769770474)
XLA Ops:
  0.6 0.9 convert_reduce_fusion
  1.5 0.7 multiply_add_fusion.2
  2.2 0.7 convert_bitcast_fusion
  2.9 0.1 broadcast_in_dim.10
  2.9 1.5 convolution_convert_fusion
  4.4 1.0 reshape_reshape.12.out_ref
  5.4 38.1 %shard_map.122 = (bf16[4,16,4,1408]{3,2,1,0:T(4,128)(2,1)}, bf16[16,4,4,1408]{3,2,1,0:T(4,128)(2,1)}) custom-call(bf16[4,16,4,1408]{3,2,1,0:T(4,128)(2,1)} %reshape_reshape.12.out_ref), custom_call_target="tpu_custom_call" | custom-call | tf_op jit(solution)/shard_map/pallas_call | solution.py:282
  43.6 1.5 reshape_reshape.13
  45.1 0.1 slice.89
  45.2 0.1 add_reduce_fusion
  45.3 0.2 copy.17
  45.5 3.0 %copy.18 = bf16[256,32,32]{2,1,0:T(8,128)(2,1)S(1)} copy(bf16[256,32,32]{0,2,1:T(8,128)(2,1)S(1)} %bitcast.63) | data formatting | bytes 1048576 | tf_op jit(solution)/shard_map/reshape | solution.py:337
  48.5 0.0 copy-start.8
  48.5 0.1 iota_add_fusion
  48.6 2.7 %fusion.5 = bf16[256,32,256]{2,1,0:T(8,128)(2,1)S(1)} fusion(bf16[256,32,32]{2,1,0:T(8,128)(2,1)S(1)} %copy.18, s32[256,32]{1,0:T(8,128)S(1)} %iota_add_fusion), kind=kOutput, calls=%fused_computation.8 | convolution fusion | flops 138412032 | bytes 4751360 | tf_op jit(solution)/shard_map/srj,sjc->src/dot_general | solution.py:338
  51.3 0.0 copy-done.8
  51.3 0.0 copy-start
  51.3 5.3 %fusion.own_ref = bf16[32,256,256]{2,1,0:T(8,128)(2,1)S(1)} fusion(bf16[1,32,256,256]{3,2,1,0:T(8,128)(2,1)S(1)} %copy-done.8, bf16[256,32,256]{2,1,0:T(8,128)(2,1)S(1)} %fusion.5, bf16[256,1408]{1,0:T(8,128)(2,1)S(1)} %reshape_reshape.13), kind=kOutput, calls=%fused_computation.2 | convolution fusion | flops 1080033280 | bytes 12713984 | tf_op jit(solution)/shard_map/src,st->rct/dot_general | solution.py:341
  56.6 0.0 copy-done
  56.6 0.0 copy-start.1
  56.6 0.0 copy-start.9
  56.6 2.5 %fusion.69 = (bf16[15,256,256]{2,1,0:T(8,128)(2,1)}, bf16[15,256,256]{2,1,0:T(8,128)(2,1)}) fusion(bf16[32,256,256]{2,1,0:T(8,128)(2,1)S(1)} %fusion.own_ref), kind=kLoop, calls=%fused_computation.114 | loop fusion | bytes 7864320 | tf_op jit(solution)/shard_map/slice | solution.py:350
  59.2 3.2 %collective-permute-start = (bf16[15,256,256]{2,1,0:T(8,128)(2,1)}, bf16[15,256,256]{2,1,0:T(8,128)(2,1)S(1)}, u32[]{:S(2)}, u32[]{:S(2)}) collective-permute-start(bf16[15,256,256]{2,1,0:T(8,128)(2,1)} %get-tuple-element.15), channel_id=1, source_target_pairs={{0,4},{4,8},{8,12},{12,16},{16,20},{20,24},{24,28},{28,32},{32,36}... | collective-permute-start | bytes 5898248 | tf_op jit(solution)/shard_map/ppermute | solution.py:349
  62.3 1.9 %collective-permute-start.1 = (bf16[15,256,256]{2,1,0:T(8,128)(2,1)}, bf16[15,256,256]{2,1,0:T(8,128)(2,1)}, u32[]{:S(2)}, u32[]{:S(2)}) collective-permute-start(bf16[15,256,256]{2,1,0:T(8,128)(2,1)} %get-tuple-element.14), channel_id=1, source_target_pairs={{4,0},{8,4},{12,8},{16,12},{20,16},{24,20},{28,24},{32,28},{36,32}... | collective-permute-start | bytes 5898248 | tf_op jit(solution)/shard_map/ppermute | solution.py:350
  64.3 0.0 copy-done.9
  64.3 0.0 copy-start.3
  64.3 0.0 copy-start.7
  64.3 0.0 copy-start.5
  64.3 0.0 copy-start.6
  64.3 1.3 fusion.8
  65.7 0.0 copy-done.1
  65.7 3.1 %collective-permute-start.2 = (f32[1,32,256]{2,1,0:T(8,128)S(1)}, f32[1,32,256]{2,1,0:T(8,128)S(1)}, u32[]{:S(2)}, u32[]{:S(2)}) collective-permute-start(f32[1,32,256]{2,1,0:T(8,128)S(1)} %div.43), channel_id=1, source_target_pairs={{0,1},{1,2},{2,3},{4,5},{5,6},{6,7},{8,9},{9,10},{10,11},{12,13},{... | collective-permute-start | bytes 98312 | tf_op jit(solution)/shard_map/ppermute | solution.py:29
  68.8 1.5 collective-permute-start.3
  70.3 0.0 copy-done.3
  70.3 0.1 multiply_reduce_fusion
  70.5 0.0 copy-done.5
  70.5 0.0 copy-done.6
  70.6 0.6 add_convert_fusion.edge_ref
  71.2 8.4 %copy.20 = bf16[32,8,32,256]{3,1,2,0:T(8,128)(2,1)} copy(bf16[32,8,32,256]{3,2,1,0:T(8,128)(2,1)} %bitcast.61) | data formatting | bytes 8388608
  79.6 0.0 collective-permute-done.2
  79.6 0.0 collective-permute-done.3
  79.7 4.6 %collective-permute-done.top_ref = bf16[15,256,256]{2,1,0:T(8,128)(2,1)S(1)} collective-permute-done((bf16[15,256,256]{2,1,0:T(8,128)(2,1)}, bf16[15,256,256]{2,1,0:T(8,128)(2,1)S(1)}, u32[]{:S(2)}, u32[]{:S(2)}) %collective-permute-start) | collective-permute-done | bytes 1966112 | tf_op jit(solution)/shard_map/ppermute | solution.py:349
  84.2 4.4 %collective-permute-done.1.bot_ref = bf16[15,256,256]{2,1,0:T(8,128)(2,1)} collective-permute-done((bf16[15,256,256]{2,1,0:T(8,128)(2,1)}, bf16[15,256,256]{2,1,0:T(8,128)(2,1)}, u32[]{:S(2)}, u32[]{:S(2)}) %collective-permute-start.1) | collective-permute-done | bytes 1966112 | tf_op jit(solution)/shard_map/ppermute | solution.py:350
  88.6 2.6 %broadcast_in_dim.12.recip_ref = f32[32,256,128]{2,1,0:T(8,128)} broadcast(f32[32,256]{1,0:T(8,128)S(1)} %fusion.59), dimensions={0,1} | broadcast | bytes 4227072 | tf_op jit(solution)/shard_map/broadcast_in_dim | solution.py:367
  91.2 0.8 broadcast_in_dim.11.scale_ref
  91.9 56.2 %shard_map.123 = (bf16[32,256,256]{2,1,0:T(8,128)(2,1)}, f32[256,256]{1,0:T(8,128)}) custom-call(f32[2]{0:T(128)} %add_convert_fusion.edge_ref, bf16[15,256,256]{2,1,0:T(8,128)(2,1)} %copy-done.2, bf16[32,256,256]{2,1,0:T(8,128)(2,1)} %copy-done.1, bf16[15,256,256]{2,1,0:T(8,128)(2,1)} %collective-permute-done.1.bot_ref, ...), custom_call_target="tpu_custom_call" | custom-call | tf_op jit(solution)/shard_map/pallas_call | solution.py:173
  148.1 1.7 reshape_reshape.14.out_ref
  149.9 19.2 %shard_map.124 = (f32[4,16,4,256]{3,2,1,0:T(4,128)}, f32[16,4,4,256]{3,2,1,0:T(4,128)}) custom-call(f32[4,16,4,256]{3,2,1,0:T(4,128)} %reshape_reshape.14.out_ref), custom_call_target="tpu_custom_call" | custom-call | tf_op jit(solution)/shard_map/pallas_call | solution.py:282
  169.1 1.0 reshape_reshape.15
  170.2 0.3 fusion.9
  170.4 0.2 fusion.19
  170.6 0.2 multiply_add_fusion
  170.8 0.2 fusion.22
  171.0 0.1 fusion.42
  171.1 0.1 fusion.44
  171.2 0.1 fusion.24
  171.3 0.1 fusion.26
  171.5 0.1 fusion.46
  171.6 0.1 fusion.48
  171.7 0.1 fusion.50
  171.8 0.1 fusion.28
  171.9 0.1 fusion.30
  172.1 0.1 fusion.32
  172.2 0.8 fusion.38
  (13 shorter events, 0.1 us)
Async XLA Ops:
  48.5 2.8 %copy-start.8 = (bf16[1,32,256,256]{3,2,1,0:T(8,128)(2,1)S(1)}, bf16[1,32,256,256]{3,2,1,0:T(8,128)(2,1)}, u32[]{:S(2)}) copy-start(bf16[1,32,256,256]{3,2,1,0:T(8,128)(2,1)} %param.11) | copy-start | bytes 12582916
  51.3 5.3 %copy-start = (bf16[256,32,256]{2,1,0:T(8,128)(2,1)}, bf16[256,32,256]{2,1,0:T(8,128)(2,1)S(1)}, u32[]{:S(2)}) copy-start(bf16[256,32,256]{2,1,0:T(8,128)(2,1)S(1)} %fusion.5) | copy-start | bytes 12582916
  56.6 9.1 %copy-start.1 = (bf16[32,256,256]{2,1,0:T(8,128)(2,1)}, bf16[32,256,256]{2,1,0:T(8,128)(2,1)S(1)}, u32[]{:S(2)}) copy-start(bf16[32,256,256]{2,1,0:T(8,128)(2,1)S(1)} %fusion.own_ref) | copy-start | bytes 12582916
  56.6 7.6 %copy-start.9 = (bf16[256,256]{1,0:T(8,128)(2,1)S(1)}, bf16[256,256]{1,0:T(8,128)(2,1)}, u32[]{:S(2)}) copy-start(bf16[256,256]{1,0:T(8,128)(2,1)} %constant.48.clone) | copy-start | bytes 393220
  59.2 25.0 %collective-permute-start = (bf16[15,256,256]{2,1,0:T(8,128)(2,1)}, bf16[15,256,256]{2,1,0:T(8,128)(2,1)S(1)}, u32[]{:S(2)}, u32[]{:S(2)}) collective-permute-start(bf16[15,256,256]{2,1,0:T(8,128)(2,1)} %get-tuple-element.15), channel_id=1, source_target_pairs={{0,4},{4,8},{8,12},{12,16},{16,20},{20,24},{24,28},{28,32},{32,36}... | collective-permute-start | bytes 5898248 | tf_op jit(solution)/shard_map/ppermute | solution.py:349
  62.3 26.3 %collective-permute-start.1 = (bf16[15,256,256]{2,1,0:T(8,128)(2,1)}, bf16[15,256,256]{2,1,0:T(8,128)(2,1)}, u32[]{:S(2)}, u32[]{:S(2)}) collective-permute-start(bf16[15,256,256]{2,1,0:T(8,128)(2,1)} %get-tuple-element.14), channel_id=1, source_target_pairs={{4,0},{8,4},{12,8},{16,12},{20,16},{24,20},{28,24},{32,28},{36,32}... | collective-permute-start | bytes 5898248 | tf_op jit(solution)/shard_map/ppermute | solution.py:350
  64.3 6.1 %copy-start.3 = (bf16[1,128,1024]{2,1,0:T(8,128)(2,1)S(1)}, bf16[1,128,1024]{2,1,0:T(8,128)(2,1)}, u32[]{:S(2)}) copy-start(bf16[1,128,1024]{2,1,0:T(8,128)(2,1)} %param.12) | copy-start | bytes 786436
  64.3 6.2 %copy-start.7 = (f32[1,256]{1,0:T(1,128)S(1)}, f32[1,256]{1,0:T(1,128)}, u32[]{:S(2)}) copy-start(f32[1,256]{1,0:T(1,128)} %param.16) | copy-start | bytes 3076
  64.3 6.2 %copy-start.5 = (f32[1,128]{1,0:T(1,128)S(1)}, f32[1,128]{1,0:T(1,128)}, u32[]{:S(2)}) copy-start(f32[1,128]{1,0:T(1,128)} %param.18) | copy-start | bytes 1540
  64.3 6.2 %copy-start.6 = (f32[1,128]{1,0:T(1,128)S(1)}, f32[1,128]{1,0:T(1,128)}, u32[]{:S(2)}) copy-start(f32[1,128]{1,0:T(1,128)} %param.17) | copy-start | bytes 1540
  65.7 13.9 %collective-permute-start.2 = (f32[1,32,256]{2,1,0:T(8,128)S(1)}, f32[1,32,256]{2,1,0:T(8,128)S(1)}, u32[]{:S(2)}, u32[]{:S(2)}) collective-permute-start(f32[1,32,256]{2,1,0:T(8,128)S(1)} %div.43), channel_id=1, source_target_pairs={{0,1},{1,2},{2,3},{4,5},{5,6},{6,7},{8,9},{9,10},{10,11},{12,13},{... | collective-permute-start | bytes 98312 | tf_op jit(solution)/shard_map/ppermute | solution.py:29
  68.8 10.8 %collective-permute-start.3 = (f32[1,32,256]{2,1,0:T(8,128)S(1)}, f32[1,32,256]{2,1,0:T(8,128)S(1)}, u32[]{:S(2)}, u32[]{:S(2)}) collective-permute-start(f32[1,32,256]{2,1,0:T(8,128)S(1)} %div.43), channel_id=1, source_target_pairs={{1,0},{2,1},{3,2},{5,4},{6,5},{7,6},{9,8},{10,9},{11,10},{13,12},{... | collective-permute-start | bytes 98312 | tf_op jit(solution)/shard_map/ppermute | solution.py:30
  84.2 7.7 %copy-start.2 = (bf16[15,256,256]{2,1,0:T(8,128)(2,1)}, bf16[15,256,256]{2,1,0:T(8,128)(2,1)S(1)}, u32[]{:S(2)}) copy-start(bf16[15,256,256]{2,1,0:T(8,128)(2,1)S(1)} %collective-permute-done.top_ref) | copy-start | bytes 5898244
  91.9 78.2 %copy-start.4 = (bf16[1,128,256]{2,1,0:T(8,128)(2,1)S(1)}, bf16[1,128,256]{2,1,0:T(8,128)(2,1)}, u32[]{:S(2)}) copy-start(bf16[1,128,256]{2,1,0:T(8,128)(2,1)} %param.13) | copy-start | bytes 196612

commit v4 on v2

--- a/solution.py
+++ b/solution.py
@@ -83,7 +83,7 @@
 
 
 def stencil_kernel(edge_ref, top_ref, own_ref, bot_ref, wcat_ref, blur_ref, scale_ref, recip_ref,
-                   frows_ref, back_ref, grad_ref, hsum_ref, ssum_ref, rows_ref):
+                   frows_ref, back_ref, grad_ref, hsum_ref, ssum_ref, rows_ref, norm_ref):
     halo = top_ref.shape[0]
     own = own_ref.shape[0]
     cols = own_ref.shape[1]
@@ -147,22 +147,24 @@
     side = lax.fori_loop(0, own, own_d, side)
     side = lax.fori_loop(0, GR, bot_d, side)
 
-    grad_ref[...] = jnp.zeros_like(grad_ref)
-
     def smooth(y, c):
         acc = taps[GR] * rows_ref[y + GR]
         for o in range(GR):
             acc = acc + taps[o] * (rows_ref[y + o] + rows_ref[y + 2 * GR - o])
-        normalized = (acc * recip_ref[y]).astype(jnp.bfloat16)
-        grad_ref[...] += jnp.dot(frows_ref[y], normalized, preferred_element_type=jnp.float32)
+        norm_ref[y] = (acc * recip_ref[y]).astype(jnp.bfloat16)
         return c
 
     lax.fori_loop(0, own, smooth, 0)
+    frame_block = norm_ref.shape[2]
+    grad_ref[...] = jnp.dot(
+        frows_ref[...], norm_ref[...].reshape(own * cols, frame_block),
+        preferred_element_type=jnp.float32,
+    )
 
 
 def stencil(edge, top, own, bot, scale, recip, frows, frame_block=128):
     halo, own_rows, cols, frames = top.shape[0], own.shape[0], own.shape[1], own.shape[2]
-    slots = frows.shape[1]
+    slots = frows.shape[0]
     ext = 2 * halo + own_rows
     wcat, blur = band_constants(cols)
     grid = (frames // frame_block,)
@@ -175,7 +177,7 @@
             pl.BlockSpec(memory_space=pltpu.SMEM),
             row_block(halo), row_block(own_rows), row_block(halo),
             fixed((2 * cols, cols)), fixed((cols, cols)), fixed((cols, frame_block)),
-            fixed((own_rows, cols, frame_block)), fixed((own_rows, slots, cols)),
+            fixed((own_rows, cols, frame_block)), fixed((slots, own_rows * cols)),
         ],
         out_specs=[row_block(own_rows), pl.BlockSpec((slots, frame_block), lambda j: (0, j))],
         out_shape=[jax.ShapeDtypeStruct(own.shape, jnp.bfloat16),
@@ -184,6 +186,7 @@
             pltpu.VMEM((ext, cols, frame_block), jnp.float32),
             pltpu.VMEM((ext, cols, frame_block), jnp.float32),
             pltpu.VMEM((own_rows + 2 * GR, cols, frame_block), jnp.float32),
+            pltpu.VMEM((own_rows, cols, frame_block), jnp.bfloat16),
         ],
         compiler_params=pltpu.CompilerParams(vmem_limit_bytes=60 * 1024 * 1024),
     )(edge, top, own, bot, jnp.asarray(wcat), jnp.asarray(blur), scale, recip, frows)
@@ -290,10 +293,13 @@
     )
     tile_grid = tile_inbox.reshape(slot_count, FOOT, FOOT)
     frows = jnp.einsum(
-        "srj,sjc->rsc", tile_grid, column_onehot, preferred_element_type=jnp.float32
+        "srj,sjc->src", tile_grid, column_onehot, preferred_element_type=jnp.float32
+    ).astype(jnp.bfloat16)
+    frows_t = jnp.einsum(
+        "srj,sjc->rcs", tile_grid, column_onehot, preferred_element_type=jnp.float32
     ).astype(jnp.bfloat16)
     model_image = jnp.einsum(
-        "rsc,st->rct", frows, trace_inbox, preferred_element_type=jnp.float32
+        "rcs,st->rct", frows_t, trace_inbox, preferred_element_type=jnp.float32
     )
     residual = (movie[0].astype(jnp.float32) - model_image).astype(jnp.bfloat16)
     halo = RAD + GR
@@ -324,7 +330,8 @@
     scale = jnp.broadcast_to((annulus_gain[0] / (8.0 * RAD))[:, None], (col_count, frame_block))
     edge = jnp.stack([pix_index > 0, pix_index < pix_count - 1]).astype(jnp.float32)
     background, slot_gradient = stencil(
-        edge, top_halo, residual, bottom_halo, scale, recip, frows, frame_block
+        edge, top_halo, residual, bottom_halo, scale, recip,
+        frows.reshape(slot_count, row_count * col_count), frame_block
     )
     home_gradient = exchange(slot_gradient.reshape(pix_count, capacity, -1), 1).reshape(
         slot_count, -1

time: 171 us -> 163 us (0.953)
  Pallas kernels: 112 us -> 104 us
  waiting for transfers between devices: 10.9 us -> 3.93 us
  matrix products: 11.1 us -> 15.2 us
  local copies, waits for them, and re-layouts: 21.1 us -> 23 us
    unnamed x20 -> x17, local copies, waits for them, and re-layouts: 0.06 us -> 8.51 us
    pallas_call x1, Pallas kernels: 64.2 us -> 56.2 us  [stencil(): pl.pallas_call(stencil_kernel, grid=grid, in_specs=[pl.BlockSpec(memory_s...]
    dot_general x1 -> x0, local copies, waits for them, and re-layouts: 6.53 us -> none  [on_device(): jnp.einsum('srj,sjc->rsc', tile_grid, column_onehot, preferred_element_ty...]
    ppermute x1, waiting for transfers between devices: 6.46 us -> 0.01 us  [on_device(): top_halo = lax.ppermute(residual[row_count - halo:], 'pix', up)]
    dot_general x2 -> x3, matrix products: 8 us -> 12.2 us  [the longest x1 5.22 us: on_device(): jnp.einsum('rcs,st->rct', frows_t, trace_inbox, preferred_element_type=jn...]
  transfers between devices with their start and end apart: 4 -> 4, of which waited for: 2 -> 1; matrix products, arithmetic and copies ran while one was open for 5% -> 9% of each run, Pallas kernels for 0% -> 0%
where the time goes in v4:
time: 163 us
  Pallas kernels  104 us (64%)
  local copies, waits for them, and re-layouts  23 us (14%)
  matrix products  15.2 us (9%)
  starting transfers between devices  10.2 us (6%)
  other arithmetic  5.75 us (4%)
  waiting for transfers between devices  3.93 us (2%)
    pallas_call x1, Pallas kernels, stencil(): pl.pallas_call(stencil_kernel, grid=grid, in_specs=[pl.BlockSpec(memory_s...  56.2 us
    pallas_call x2, Pallas kernels, exchange(): pl.pallas_call(exchange_kernel, out_shape=jax.ShapeDtypeStruct(outbox.sha...  47.4 us
    unnamed x17, local copies, waits for them, and re-layouts  8.51 us
    dot_general x1, matrix products, on_device(): jnp.einsum('rcs,st->rct', frows_t, trace_inbox, preferred_element_type=jn...  5.22 us
    dot_general x1, matrix products, on_device(): jnp.einsum('srj,sjc->src', tile_grid, column_onehot, preferred_element_ty...  4.17 us
    ppermute x1, waiting for transfers between devices, on_device(): bottom_halo = lax.ppermute(residual[:halo], 'pix', down)  3.93 us
  transfers between devices with their start and end apart: 4, of which 1 were waited for; matrix products, arithmetic and copies ran while one was open for 9% of the time, Pallas kernels for 0%

profile of v4, /device:TPU:1, one launch (start us, length us, event | category | flops | bytes accessed | tf_op | source)
XLA Modules:
  0.0 162.9 jit_solution(7119667388986582209)
XLA Ops:
  0.6 0.9 convert_reduce_fusion
  1.5 0.7 multiply_add_fusion.2
  2.2 0.7 convert_bitcast_fusion.1
  2.9 0.1 broadcast_in_dim.10
  2.9 1.5 convolution_convert_fusion
  4.4 1.0 reshape.225.out_ref
  5.4 29.9 %shard_map.122 = bf16[64,4,1408]{2,1,0:T(4,128)(2,1)} custom-call(bf16[64,4,1408]{2,1,0:T(4,128)(2,1)} %reshape.225.out_ref), custom_call_target="tpu_custom_call" | custom-call | tf_op jit(solution)/shard_map/pallas_call | solution.py:245
  35.3 1.5 reshape.226
  36.9 0.1 slice.90
  36.9 0.1 add_reduce_fusion
  37.1 0.2 copy.15
  37.3 3.0 %copy.16 = bf16[256,32,32]{2,1,0:T(8,128)(2,1)S(1)} copy(bf16[256,32,32]{0,2,1:T(8,128)(2,1)S(1)} %bitcast.66) | data formatting | bytes 1048576 | tf_op jit(solution)/shard_map/reshape | solution.py:294
  40.3 0.0 copy-start.6
  40.3 0.1 iota_add_fusion
  40.4 2.8 %convert_bitcast_fusion = bf16[32,256,256]{1,0,2:T(8,128)(2,1)S(1)} fusion(bf16[256,32,32]{2,1,0:T(8,128)(2,1)S(1)} %copy.16, s32[256,32]{1,0:T(8,128)S(1)} %iota_add_fusion), kind=kOutput, calls=%fused_computation.8 | convolution fusion | flops 138412032 | bytes 4751360 | tf_op jit(solution)/shard_map/srj,sjc->rcs/dot_general | solution.py:298
  43.2 0.0 copy-done.6
  43.2 5.2 %fusion.own_ref = bf16[32,256,256]{2,1,0:T(8,128)(2,1)S(1)} fusion(bf16[1,32,256,256]{3,2,1,0:T(8,128)(2,1)S(1)} %copy-done.6, bf16[32,256,256]{1,0,2:T(8,128)(2,1)S(1)} %convert_bitcast_fusion, bf16[256,1408]{1,0:T(8,128)(2,1)S(1)} %reshape.226), kind=kOutput, calls=%fused_computation.2 | convolution fusion | flops 1080033280 | bytes 12713984 | tf_op jit(solution)/shard_map/rcs,st->rct/dot_general | solution.py:301
  48.4 0.0 copy-start
  48.4 0.0 copy-start.7
  48.5 2.5 %fusion.71 = (bf16[15,256,256]{2,1,0:T(8,128)(2,1)}, bf16[15,256,256]{2,1,0:T(8,128)(2,1)}) fusion(bf16[32,256,256]{2,1,0:T(8,128)(2,1)S(1)} %fusion.own_ref), kind=kLoop, calls=%fused_computation.117 | loop fusion | bytes 7864320 | tf_op jit(solution)/shard_map/slice | solution.py:310
  51.0 2.9 %collective-permute-start = (bf16[15,256,256]{2,1,0:T(8,128)(2,1)}, bf16[15,256,256]{2,1,0:T(8,128)(2,1)}, u32[]{:S(2)}, u32[]{:S(2)}) collective-permute-start(bf16[15,256,256]{2,1,0:T(8,128)(2,1)} %get-tuple-element.11), channel_id=1, source_target_pairs={{0,4},{4,8},{8,12},{12,16},{16,20},{20,24},{24,28},{28,32},{32,36}... | collective-permute-start | bytes 5898248 | tf_op jit(solution)/shard_map/ppermute | solution.py:309
  53.9 2.7 %collective-permute-start.1 = (bf16[15,256,256]{2,1,0:T(8,128)(2,1)}, bf16[15,256,256]{2,1,0:T(8,128)(2,1)}, u32[]{:S(2)}, u32[]{:S(2)}) collective-permute-start(bf16[15,256,256]{2,1,0:T(8,128)(2,1)} %get-tuple-element.10), channel_id=1, source_target_pairs={{4,0},{8,4},{12,8},{16,12},{20,16},{24,20},{28,24},{32,28},{36,32}... | collective-permute-start | bytes 5898248 | tf_op jit(solution)/shard_map/ppermute | solution.py:310
  56.6 0.0 copy-done.7
  56.6 0.0 copy-start.1
  56.6 0.0 copy-start.5
  56.6 0.0 copy-start.3
  56.7 0.0 copy-start.4
  56.7 1.3 fusion.10
  58.0 0.0 copy-done
  58.1 3.1 %collective-permute-start.2 = (f32[1,32,256]{2,1,0:T(8,128)S(1)}, f32[1,32,256]{2,1,0:T(8,128)S(1)}, u32[]{:S(2)}, u32[]{:S(2)}) collective-permute-start(f32[1,32,256]{2,1,0:T(8,128)S(1)} %div.43), channel_id=1, source_target_pairs={{0,1},{1,2},{2,3},{4,5},{5,6},{6,7},{8,9},{9,10},{10,11},{12,13},{... | collective-permute-start | bytes 98312 | tf_op jit(solution)/shard_map/ppermute | solution.py:29
  61.2 1.5 collective-permute-start.3
  62.7 0.0 copy-done.1
  62.7 0.1 multiply_reduce_fusion
  62.8 0.0 copy-done.5
  62.8 0.0 copy-done.3
  62.9 4.2 %fusion.7 = bf16[256,32,256]{2,1,0:T(8,128)(2,1)} fusion(bf16[256,32,32]{2,1,0:T(8,128)(2,1)S(1)} %copy.16, s32[256,32]{1,0:T(8,128)S(1)} %iota_add_fusion), kind=kOutput, calls=%fused_computation.11 | convolution fusion | flops 138412032 | bytes 4751360 | tf_op jit(solution)/shard_map/srj,sjc->src/dot_general | solution.py:295
  67.1 0.7 add_convert_fusion.edge_ref
  67.8 8.5 %copy.19 = bf16[32,8,32,256]{3,1,2,0:T(8,128)(2,1)} copy(bf16[32,8,32,256]{3,2,1,0:T(8,128)(2,1)} %bitcast.64) | data formatting | bytes 8388608
  76.2 0.0 collective-permute-done.2
  76.2 0.0 collective-permute-done.3
  76.2 0.0 collective-permute-done.top_ref
  76.2 3.9 %collective-permute-done.1.bot_ref = bf16[15,256,256]{2,1,0:T(8,128)(2,1)} collective-permute-done((bf16[15,256,256]{2,1,0:T(8,128)(2,1)}, bf16[15,256,256]{2,1,0:T(8,128)(2,1)}, u32[]{:S(2)}, u32[]{:S(2)}) %collective-permute-start.1) | collective-permute-done | bytes 1966112 | tf_op jit(solution)/shard_map/ppermute | solution.py:310
  80.2 2.6 %broadcast_in_dim.12.recip_ref = f32[32,256,128]{2,1,0:T(8,128)} broadcast(f32[32,256]{1,0:T(8,128)S(1)} %fusion.61), dimensions={0,1} | broadcast | bytes 4227072 | tf_op jit(solution)/shard_map/broadcast_in_dim | solution.py:327
  82.7 0.8 broadcast_in_dim.11.scale_ref
  83.5 56.2 %shard_map.123 = (bf16[32,256,256]{2,1,0:T(8,128)(2,1)}, f32[256,256]{1,0:T(8,128)}) custom-call(f32[2]{0:T(128)} %add_convert_fusion.edge_ref, bf16[15,256,256]{2,1,0:T(8,128)(2,1)} %collective-permute-done.top_ref, bf16[32,256,256]{2,1,0:T(8,128)(2,1)} %copy-done, bf16[15,256,256]{2,1,0:T(8,128)(2,1)} %collective-permute-done.1.bot_ref, ...), custom_call_target="tpu_custom_call" | custom-call | tf_op jit(solution)/shard_map/pallas_call | solution.py:173
  139.7 1.7 %reshape.230.out_ref = f32[64,4,256]{2,1,0:T(4,128)} reshape(f32[256,256]{1,0:T(8,128)} %get-tuple-element.5) | data formatting | bytes 524288 | tf_op jit(solution)/shard_map/reshape | solution.py:336
  141.5 17.5 %shard_map.124 = f32[64,4,256]{2,1,0:T(4,128)} custom-call(f32[64,4,256]{2,1,0:T(4,128)} %reshape.230.out_ref), custom_call_target="tpu_custom_call" | custom-call | tf_op jit(solution)/shard_map/pallas_call | solution.py:245
  159.0 1.0 reshape.231
  160.0 0.0 copy-done.2
  160.0 0.3 fusion.11
  160.3 0.2 fusion.21
  160.5 0.2 multiply_add_fusion
  160.7 0.2 fusion.24
  160.9 0.1 fusion.44
  161.0 0.1 fusion.46
  161.1 0.1 fusion.26
  161.2 0.1 fusion.28
  161.3 0.1 fusion.48
  161.5 0.1 fusion.50
  161.6 0.1 fusion.52
  161.7 0.1 fusion.30
  161.8 0.1 fusion.32
  162.0 0.1 fusion.34
  162.1 0.8 fusion.40
  (10 shorter events, 0.1 us)
Async XLA Ops:
  40.3 2.9 %copy-start.6 = (bf16[1,32,256,256]{3,2,1,0:T(8,128)(2,1)S(1)}, bf16[1,32,256,256]{3,2,1,0:T(8,128)(2,1)}, u32[]{:S(2)}) copy-start(bf16[1,32,256,256]{3,2,1,0:T(8,128)(2,1)} %param.11) | copy-start | bytes 12582916
  48.4 9.6 %copy-start = (bf16[32,256,256]{2,1,0:T(8,128)(2,1)}, bf16[32,256,256]{2,1,0:T(8,128)(2,1)S(1)}, u32[]{:S(2)}) copy-start(bf16[32,256,256]{2,1,0:T(8,128)(2,1)S(1)} %fusion.own_ref) | copy-start | bytes 12582916
  48.4 8.2 %copy-start.7 = (bf16[256,256]{1,0:T(8,128)(2,1)S(1)}, bf16[256,256]{1,0:T(8,128)(2,1)}, u32[]{:S(2)}) copy-start(bf16[256,256]{1,0:T(8,128)(2,1)} %constant.48.clone) | copy-start | bytes 393220
  51.0 25.3 %collective-permute-start = (bf16[15,256,256]{2,1,0:T(8,128)(2,1)}, bf16[15,256,256]{2,1,0:T(8,128)(2,1)}, u32[]{:S(2)}, u32[]{:S(2)}) collective-permute-start(bf16[15,256,256]{2,1,0:T(8,128)(2,1)} %get-tuple-element.11), channel_id=1, source_target_pairs={{0,4},{4,8},{8,12},{12,16},{16,20},{20,24},{24,28},{28,32},{32,36}... | collective-permute-start | bytes 5898248 | tf_op jit(solution)/shard_map/ppermute | solution.py:309
  53.9 26.3 %collective-permute-start.1 = (bf16[15,256,256]{2,1,0:T(8,128)(2,1)}, bf16[15,256,256]{2,1,0:T(8,128)(2,1)}, u32[]{:S(2)}, u32[]{:S(2)}) collective-permute-start(bf16[15,256,256]{2,1,0:T(8,128)(2,1)} %get-tuple-element.10), channel_id=1, source_target_pairs={{4,0},{8,4},{12,8},{16,12},{20,16},{24,20},{28,24},{32,28},{36,32}... | collective-permute-start | bytes 5898248 | tf_op jit(solution)/shard_map/ppermute | solution.py:310
  56.6 6.1 %copy-start.1 = (bf16[1,128,1024]{2,1,0:T(8,128)(2,1)S(1)}, bf16[1,128,1024]{2,1,0:T(8,128)(2,1)}, u32[]{:S(2)}) copy-start(bf16[1,128,1024]{2,1,0:T(8,128)(2,1)} %param.12) | copy-start | bytes 786436
  56.6 6.2 %copy-start.5 = (f32[1,256]{1,0:T(1,128)S(1)}, f32[1,256]{1,0:T(1,128)}, u32[]{:S(2)}) copy-start(f32[1,256]{1,0:T(1,128)} %param.16) | copy-start | bytes 3076
  56.6 6.2 %copy-start.3 = (f32[1,128]{1,0:T(1,128)S(1)}, f32[1,128]{1,0:T(1,128)}, u32[]{:S(2)}) copy-start(f32[1,128]{1,0:T(1,128)} %param.18) | copy-start | bytes 1540
  56.7 6.2 %copy-start.4 = (f32[1,128]{1,0:T(1,128)S(1)}, f32[1,128]{1,0:T(1,128)}, u32[]{:S(2)}) copy-start(f32[1,128]{1,0:T(1,128)} %param.17) | copy-start | bytes 1540
  58.1 18.1 %collective-permute-start.2 = (f32[1,32,256]{2,1,0:T(8,128)S(1)}, f32[1,32,256]{2,1,0:T(8,128)S(1)}, u32[]{:S(2)}, u32[]{:S(2)}) collective-permute-start(f32[1,32,256]{2,1,0:T(8,128)S(1)} %div.43), channel_id=1, source_target_pairs={{0,1},{1,2},{2,3},{4,5},{5,6},{6,7},{8,9},{9,10},{10,11},{12,13},{... | collective-permute-start | bytes 98312 | tf_op jit(solution)/shard_map/ppermute | solution.py:29
  61.2 15.0 %collective-permute-start.3 = (f32[1,32,256]{2,1,0:T(8,128)S(1)}, f32[1,32,256]{2,1,0:T(8,128)S(1)}, u32[]{:S(2)}, u32[]{:S(2)}) collective-permute-start(f32[1,32,256]{2,1,0:T(8,128)S(1)} %div.43), channel_id=1, source_target_pairs={{1,0},{2,1},{3,2},{5,4},{6,5},{7,6},{9,8},{10,9},{11,10},{13,12},{... | collective-permute-start | bytes 98312 | tf_op jit(solution)/shard_map/ppermute | solution.py:30
  83.5 76.5 %copy-start.2 = (bf16[1,128,256]{2,1,0:T(8,128)(2,1)S(1)}, bf16[1,128,256]{2,1,0:T(8,128)(2,1)}, u32[]{:S(2)}) copy-start(bf16[1,128,256]{2,1,0:T(8,128)(2,1)} %param.13) | copy-start | bytes 196612

commit v5 on v4

--- a/solution.py
+++ b/solution.py
@@ -306,8 +306,16 @@
     pix_index = lax.axis_index("pix")
     up = [(i, i + 1) for i in range(pix_count - 1)]
     down = [(j, i) for i, j in up]
-    top_halo = lax.ppermute(residual[row_count - halo :], "pix", up)
-    bottom_halo = lax.ppermute(residual[:halo], "pix", down)
+    def edge_rows(first, count):
+        model_rows = jnp.einsum(
+            "rcs,st->rct", frows_t[first : first + count], trace_inbox,
+            preferred_element_type=jnp.float32,
+        )
+        movie_rows = movie[0, first : first + count].astype(jnp.float32)
+        return (movie_rows - model_rows).astype(jnp.bfloat16)
+
+    top_halo = lax.ppermute(edge_rows(row_count - halo, halo), "pix", up)
+    bottom_halo = lax.ppermute(edge_rows(0, halo), "pix", down)
     frame_index = np.arange(frame_count)
     step_matrix = (
         (frame_index[:, None] == frame_index[None, :] + 1).astype(np.float32)

time: 163 us -> 165 us (1.012)
  matrix products: 15.2 us -> 21.1 us
  waiting for transfers between devices: 3.93 us -> 0.01 us
  Pallas kernels: 104 us -> 102 us
    dot_general x0 -> x2, matrix products: none -> 5.9 us  [edge_rows(): jnp.einsum('rcs,st->rct', frows_t[first:first + count], trace_inbox, pref...]
    ppermute x2, waiting for transfers between devices: 3.93 us -> 0.01 us  [the longest x1 0.01 us: on_device(): bottom_halo = lax.ppermute(edge_rows(0, halo), 'pix', down)]
    unnamed x17, local copies, waits for them, and re-layouts: 8.51 us -> 10.2 us
  transfers between devices with their start and end apart: 4 -> 4, of which waited for: 1 -> 0; matrix products, arithmetic and copies ran while one was open for 9% -> 14% of each run, Pallas kernels for 0% -> 0%
where the time goes in v5:
time: 165 us; the launch traced here: 164 us
  Pallas kernels  102 us (62%)
  local copies, waits for them, and re-layouts  23.2 us (14%)
  matrix products  21.1 us (13%)
  starting transfers between devices  10.5 us (6%)
  other arithmetic  5.75 us (3%)
    pallas_call x1, Pallas kernels, stencil(): pl.pallas_call(stencil_kernel, grid=grid, in_specs=[pl.BlockSpec(memory_s...  56.2 us
    pallas_call x2, Pallas kernels, exchange(): pl.pallas_call(exchange_kernel, out_shape=jax.ShapeDtypeStruct(outbox.sha...  46.1 us
    unnamed x17, local copies, waits for them, and re-layouts  10.2 us
    dot_general x2, matrix products, edge_rows(): jnp.einsum('rcs,st->rct', frows_t[first:first + count], trace_inbox, pref...  5.9 us
    dot_general x1, matrix products, on_device(): jnp.einsum('rcs,st->rct', frows_t, trace_inbox, preferred_element_type=jn...  5.22 us
    dot_general x1, matrix products, on_device(): jnp.einsum('srj,sjc->src', tile_grid, column_onehot, preferred_element_ty...  4.17 us
    ppermute x1, starting transfers between devices, on_device(): top_halo = lax.ppermute(edge_rows(row_count - halo, halo), 'pix', up)  3.56 us
  transfers between devices with their start and end apart: 4, of which 0 were waited for; matrix products, arithmetic and copies ran while one was open for 14% of the time, Pallas kernels for 0%

profile of v5, /device:TPU:1, one launch (start us, length us, event | category | flops | bytes accessed | tf_op | source)
XLA Modules:
  0.0 163.9 jit_solution(12521540243863137250)
XLA Ops:
  0.6 0.9 convert_reduce_fusion
  1.5 0.7 multiply_add_fusion.2
  2.2 0.7 convert_bitcast_fusion.1
  2.9 0.1 broadcast_in_dim.10
  2.9 1.5 convolution_convert_fusion
  4.4 1.0 reshape.229.out_ref
  5.4 29.9 %shard_map.122 = bf16[64,4,1408]{2,1,0:T(4,128)(2,1)} custom-call(bf16[64,4,1408]{2,1,0:T(4,128)(2,1)} %reshape.229.out_ref), custom_call_target="tpu_custom_call" | custom-call | tf_op jit(solution)/shard_map/pallas_call | solution.py:245
  35.3 1.5 reshape.230
  36.9 0.1 slice.98
  36.9 0.1 add_reduce_fusion
  37.1 0.2 copy.22
  37.3 3.0 %copy.23 = bf16[256,32,32]{2,1,0:T(8,128)(2,1)S(1)} copy(bf16[256,32,32]{0,2,1:T(8,128)(2,1)S(1)} %bitcast.74) | data formatting | bytes 1048576 | tf_op jit(solution)/shard_map/reshape | solution.py:294
  40.3 0.1 iota_add_fusion
  40.4 2.8 %convert_bitcast_fusion = bf16[32,256,256]{1,0,2:T(8,128)(2,1)S(1)} fusion(bf16[256,32,32]{2,1,0:T(8,128)(2,1)S(1)} %copy.23, s32[256,32]{1,0:T(8,128)S(1)} %iota_add_fusion), kind=kOutput, calls=%fused_computation.8 | convolution fusion | flops 138412032 | bytes 4751360 | tf_op jit(solution)/shard_map/srj,sjc->rcs/dot_general | solution.py:298
  43.2 0.0 copy-start.6
  43.2 1.0 fusion.75
  44.2 1.2 copy-done.6
  45.4 3.0 %fusion.7 = bf16[15,256,256]{2,1,0:T(8,128)(2,1)} fusion(bf16[15,256,256]{1,0,2:T(8,128)(2,1)S(1)} %get-tuple-element.10, bf16[1,32,256,256]{3,2,1,0:T(8,128)(2,1)S(1)} %copy-done.6, bf16[256,1408]{1,0:T(8,128)(2,1)S(1)} %reshape.230), kind=kOutput, calls=%fused_computation.12 | convolution fusion | flops 506265600 | bytes 6160384 | tf_op jit(solution)/shard_map/rcs,st->rct/dot_general | solution.py:310
  48.4 2.3 %collective-permute-start.1 = (bf16[15,256,256]{2,1,0:T(8,128)(2,1)}, bf16[15,256,256]{2,1,0:T(8,128)(2,1)}, u32[]{:S(2)}, u32[]{:S(2)}) collective-permute-start(bf16[15,256,256]{2,1,0:T(8,128)(2,1)} %fusion.7), channel_id=1, source_target_pairs={{4,0},{8,4},{12,8},{16,12},{20,16},{24,20},{28,24},{32,28},{36,32}... | collective-permute-start | bytes 5898248 | tf_op jit(solution)/shard_map/ppermute | solution.py:318
  50.7 2.9 %fusion.8 = bf16[15,256,256]{2,1,0:T(8,128)(2,1)} fusion(bf16[15,256,256]{1,0,2:T(8,128)(2,1)S(1)} %get-tuple-element.11, bf16[1,32,256,256]{3,2,1,0:T(8,128)(2,1)S(1)} %copy-done.6, bf16[256,1408]{1,0:T(8,128)(2,1)S(1)} %reshape.230), kind=kOutput, calls=%fused_computation.14 | convolution fusion | flops 506265600 | bytes 6160384 | tf_op jit(solution)/shard_map/rcs,st->rct/dot_general | solution.py:310
  53.6 3.6 %collective-permute-start = (bf16[15,256,256]{2,1,0:T(8,128)(2,1)}, bf16[15,256,256]{2,1,0:T(8,128)(2,1)}, u32[]{:S(2)}, u32[]{:S(2)}) collective-permute-start(bf16[15,256,256]{2,1,0:T(8,128)(2,1)} %fusion.8), channel_id=1, source_target_pairs={{0,4},{4,8},{8,12},{12,16},{16,20},{20,24},{24,28},{28,32},{32,36}... | collective-permute-start | bytes 5898248 | tf_op jit(solution)/shard_map/ppermute | solution.py:317
  57.2 5.2 %fusion.own_ref = bf16[32,256,256]{2,1,0:T(8,128)(2,1)S(1)} fusion(bf16[1,32,256,256]{3,2,1,0:T(8,128)(2,1)S(1)} %copy-done.6, bf16[32,256,256]{1,0,2:T(8,128)(2,1)S(1)} %convert_bitcast_fusion, bf16[256,1408]{1,0:T(8,128)(2,1)S(1)} %reshape.230), kind=kOutput, calls=%fused_computation.2 | convolution fusion | flops 1080033280 | bytes 12713984 | tf_op jit(solution)/shard_map/rcs,st->rct/dot_general | solution.py:301
  62.4 0.0 copy-start
  62.4 0.0 copy-done.7
  62.4 0.0 copy-start.1
  62.4 0.0 copy-start.5
  62.4 0.0 copy-start.3
  62.4 0.0 copy-start.4
  62.4 1.3 fusion.12
  63.8 0.5 copy-done
  64.3 3.1 %collective-permute-start.2 = (f32[1,32,256]{2,1,0:T(8,128)S(1)}, f32[1,32,256]{2,1,0:T(8,128)S(1)}, u32[]{:S(2)}, u32[]{:S(2)}) collective-permute-start(f32[1,32,256]{2,1,0:T(8,128)S(1)} %div.43), channel_id=1, source_target_pairs={{0,1},{1,2},{2,3},{4,5},{5,6},{6,7},{8,9},{9,10},{10,11},{12,13},{... | collective-permute-start | bytes 98312 | tf_op jit(solution)/shard_map/ppermute | solution.py:29
  67.5 1.5 collective-permute-start.3
  69.0 0.0 copy-done.1
  69.0 0.1 multiply_reduce_fusion
  69.1 0.0 copy-done.5
  69.2 4.2 %fusion.9 = bf16[256,32,256]{2,1,0:T(8,128)(2,1)} fusion(bf16[256,32,32]{2,1,0:T(8,128)(2,1)S(1)} %copy.23, s32[256,32]{1,0:T(8,128)S(1)} %iota_add_fusion), kind=kOutput, calls=%fused_computation.15 | convolution fusion | flops 138412032 | bytes 4751360 | tf_op jit(solution)/shard_map/srj,sjc->src/dot_general | solution.py:295
  73.4 0.7 add_convert_fusion.edge_ref
  74.1 8.5 %copy.28 = bf16[32,8,32,256]{3,1,2,0:T(8,128)(2,1)} copy(bf16[32,8,32,256]{3,2,1,0:T(8,128)(2,1)} %bitcast.72) | data formatting | bytes 8388608
  82.5 0.0 collective-permute-done.2
  82.5 0.0 collective-permute-done.3
  82.6 0.0 collective-permute-done.1.bot_ref
  82.6 0.0 collective-permute-done.top_ref
  82.6 2.6 %broadcast_in_dim.12.recip_ref = f32[32,256,128]{2,1,0:T(8,128)} broadcast(f32[32,256]{1,0:T(8,128)S(1)} %fusion.65), dimensions={0,1} | broadcast | bytes 4227072 | tf_op jit(solution)/shard_map/broadcast_in_dim | solution.py:335
  85.2 0.8 broadcast_in_dim.11.scale_ref
  85.9 56.2 %shard_map.123 = (bf16[32,256,256]{2,1,0:T(8,128)(2,1)}, f32[256,256]{1,0:T(8,128)}) custom-call(f32[2]{0:T(128)} %add_convert_fusion.edge_ref, bf16[15,256,256]{2,1,0:T(8,128)(2,1)} %collective-permute-done.top_ref, bf16[32,256,256]{2,1,0:T(8,128)(2,1)} %copy-done, bf16[15,256,256]{2,1,0:T(8,128)(2,1)} %collective-permute-done.1.bot_ref, ...), custom_call_target="tpu_custom_call" | custom-call | tf_op jit(solution)/shard_map/pallas_call | solution.py:173
  142.2 1.7 %reshape.234.out_ref = f32[64,4,256]{2,1,0:T(4,128)} reshape(f32[256,256]{1,0:T(8,128)} %get-tuple-element.5) | data formatting | bytes 524288 | tf_op jit(solution)/shard_map/reshape | solution.py:344
  143.9 16.2 %shard_map.124 = f32[64,4,256]{2,1,0:T(4,128)} custom-call(f32[64,4,256]{2,1,0:T(4,128)} %reshape.234.out_ref), custom_call_target="tpu_custom_call" | custom-call | tf_op jit(solution)/shard_map/pallas_call | solution.py:245
  160.1 1.0 reshape.235
  161.1 0.0 copy-done.2
  161.1 0.3 fusion.15
  161.4 0.2 fusion.25
  161.6 0.2 multiply_add_fusion
  161.7 0.2 fusion.28
  161.9 0.1 fusion.48
  162.0 0.1 fusion.50
  162.2 0.1 fusion.30
  162.3 0.1 fusion.32
  162.4 0.1 fusion.52
  162.5 0.1 fusion.54
  162.6 0.1 fusion.56
  162.8 0.1 fusion.34
  162.9 0.1 fusion.36
  163.0 0.1 fusion.38
  163.1 0.8 fusion.44
  (12 shorter events, 0.1 us)
Async XLA Ops:
  43.2 2.2 %copy-start.6 = (bf16[1,32,256,256]{3,2,1,0:T(8,128)(2,1)S(1)}, bf16[1,32,256,256]{3,2,1,0:T(8,128)(2,1)}, u32[]{:S(2)}) copy-start(bf16[1,32,256,256]{3,2,1,0:T(8,128)(2,1)} %param.11) | copy-start | bytes 12582916
  48.4 34.2 %collective-permute-start.1 = (bf16[15,256,256]{2,1,0:T(8,128)(2,1)}, bf16[15,256,256]{2,1,0:T(8,128)(2,1)}, u32[]{:S(2)}, u32[]{:S(2)}) collective-permute-start(bf16[15,256,256]{2,1,0:T(8,128)(2,1)} %fusion.7), channel_id=1, source_target_pairs={{4,0},{8,4},{12,8},{16,12},{20,16},{24,20},{28,24},{32,28},{36,32}... | collective-permute-start | bytes 5898248 | tf_op jit(solution)/shard_map/ppermute | solution.py:318
  53.6 8.8 %copy-start.7 = (bf16[256,256]{1,0:T(8,128)(2,1)S(1)}, bf16[256,256]{1,0:T(8,128)(2,1)}, u32[]{:S(2)}) copy-start(bf16[256,256]{1,0:T(8,128)(2,1)} %constant.48.clone) | copy-start | bytes 393220
  53.6 29.0 %collective-permute-start = (bf16[15,256,256]{2,1,0:T(8,128)(2,1)}, bf16[15,256,256]{2,1,0:T(8,128)(2,1)}, u32[]{:S(2)}, u32[]{:S(2)}) collective-permute-start(bf16[15,256,256]{2,1,0:T(8,128)(2,1)} %fusion.8), channel_id=1, source_target_pairs={{0,4},{4,8},{8,12},{12,16},{16,20},{20,24},{24,28},{28,32},{32,36}... | collective-permute-start | bytes 5898248 | tf_op jit(solution)/shard_map/ppermute | solution.py:317
  62.4 1.9 %copy-start = (bf16[32,256,256]{2,1,0:T(8,128)(2,1)}, bf16[32,256,256]{2,1,0:T(8,128)(2,1)S(1)}, u32[]{:S(2)}) copy-start(bf16[32,256,256]{2,1,0:T(8,128)(2,1)S(1)} %fusion.own_ref) | copy-start | bytes 12582916
  62.4 6.6 %copy-start.1 = (bf16[1,128,1024]{2,1,0:T(8,128)(2,1)S(1)}, bf16[1,128,1024]{2,1,0:T(8,128)(2,1)}, u32[]{:S(2)}) copy-start(bf16[1,128,1024]{2,1,0:T(8,128)(2,1)} %param.12) | copy-start | bytes 786436
  62.4 6.7 %copy-start.5 = (f32[1,256]{1,0:T(1,128)S(1)}, f32[1,256]{1,0:T(1,128)}, u32[]{:S(2)}) copy-start(f32[1,256]{1,0:T(1,128)} %param.16) | copy-start | bytes 3076
  62.4 6.7 %copy-start.3 = (f32[1,128]{1,0:T(1,128)S(1)}, f32[1,128]{1,0:T(1,128)}, u32[]{:S(2)}) copy-start(f32[1,128]{1,0:T(1,128)} %param.18) | copy-start | bytes 1540
  62.4 6.7 %copy-start.4 = (f32[1,128]{1,0:T(1,128)S(1)}, f32[1,128]{1,0:T(1,128)}, u32[]{:S(2)}) copy-start(f32[1,128]{1,0:T(1,128)} %param.17) | copy-start | bytes 1540
  64.3 18.2 %collective-permute-start.2 = (f32[1,32,256]{2,1,0:T(8,128)S(1)}, f32[1,32,256]{2,1,0:T(8,128)S(1)}, u32[]{:S(2)}, u32[]{:S(2)}) collective-permute-start(f32[1,32,256]{2,1,0:T(8,128)S(1)} %div.43), channel_id=1, source_target_pairs={{0,1},{1,2},{2,3},{4,5},{5,6},{6,7},{8,9},{9,10},{10,11},{12,13},{... | collective-permute-start | bytes 98312 | tf_op jit(solution)/shard_map/ppermute | solution.py:29
  67.5 15.1 %collective-permute-start.3 = (f32[1,32,256]{2,1,0:T(8,128)S(1)}, f32[1,32,256]{2,1,0:T(8,128)S(1)}, u32[]{:S(2)}, u32[]{:S(2)}) collective-permute-start(f32[1,32,256]{2,1,0:T(8,128)S(1)} %div.43), channel_id=1, source_target_pairs={{1,0},{2,1},{3,2},{5,4},{6,5},{7,6},{9,8},{10,9},{11,10},{13,12},{... | collective-permute-start | bytes 98312 | tf_op jit(solution)/shard_map/ppermute | solution.py:30
  85.9 75.2 %copy-start.2 = (bf16[1,128,256]{2,1,0:T(8,128)(2,1)S(1)}, bf16[1,128,256]{2,1,0:T(8,128)(2,1)}, u32[]{:S(2)}) copy-start(bf16[1,128,256]{2,1,0:T(8,128)(2,1)} %param.13) | copy-start | bytes 196612

commit v6 on v4

--- a/solution.py
+++ b/solution.py
@@ -78,49 +78,56 @@
     blur = np.zeros((col_count, col_count), np.float32)
     for offset in range(-GR, GR + 1):
         blur = blur + np.where(gap == offset, taps[offset + GR], 0.0)
-    wcat = np.concatenate([box, side], axis=0).astype(ml_dtypes.bfloat16)
-    return wcat, blur.astype(ml_dtypes.bfloat16)
-
-
-def stencil_kernel(edge_ref, top_ref, own_ref, bot_ref, wcat_ref, blur_ref, scale_ref, recip_ref,
-                   frows_ref, back_ref, grad_ref, hsum_ref, ssum_ref, rows_ref, norm_ref):
+    as_bf16 = lambda x: x.astype(ml_dtypes.bfloat16)
+    pair = np.concatenate([box, box], axis=1)
+    slide = np.concatenate([side, -side], axis=1)
+    return as_bf16(pair), as_bf16(slide), as_bf16(side), as_bf16(blur)
+
+
+def stencil_kernel(edge_ref, top_ref, own_ref, bot_ref, pair_ref, slide_ref, side_ref, blur_ref,
+                   scale_ref, recip_ref, frows_ref, back_ref, grad_ref, ext_ref, rows_ref, norm_ref):
     halo = top_ref.shape[0]
     own = own_ref.shape[0]
-    cols = own_ref.shape[1]
     taps = [float(v) for v in tap_values()]
 
-    def horizontal(e, row):
-        prod = jnp.dot(wcat_ref[...], row, preferred_element_type=jnp.float32)
-        hsum_ref[e] = prod[:cols]
-        ssum_ref[e] = prod[cols:]
-
-    def top_h(r, c):
-        horizontal(r, top_ref[r])
-        return c
-
-    def own_h(r, c):
-        horizontal(halo + r, own_ref[r])
-        return c
-
-    def bot_h(r, c):
-        horizontal(halo + own + r, bot_ref[r])
-        return c
-
-    lax.fori_loop(0, halo, top_h, 0)
-    lax.fori_loop(0, own, own_h, 0)
-    lax.fori_loop(0, halo, bot_h, 0)
+    def copy_top(r, c):
+        ext_ref[r] = top_ref[r]
+        return c
+
+    def copy_own(r, c):
+        ext_ref[halo + r] = own_ref[r]
+        return c
+
+    def copy_bot(r, c):
+        ext_ref[halo + own + r] = bot_ref[r]
+        return c
+
+    lax.fori_loop(0, halo, copy_top, 0)
+    lax.fori_loop(0, own, copy_own, 0)
+    lax.fori_loop(0, halo, copy_bot, 0)
 
     first = halo - GR
-    side = ssum_ref[first - RAD]
+    side = jnp.dot(side_ref[...], ext_ref[first - RAD], preferred_element_type=jnp.float32)
     for i in range(1, 2 * RAD - 1):
-        side = side + ssum_ref[first - RAD + i]
-
-    def detrend(k, side, row, keep):
+        side = side + jnp.dot(
+            side_ref[...], ext_ref[first - RAD + i], preferred_element_type=jnp.float32
+        )
+
+    def detrend(k, side, keep):
         e = first + k
-        side = side + ssum_ref[e + RAD - 1] - ssum_ref[e - RAD]
-        total = hsum_ref[e - RAD] + hsum_ref[e + RAD] + side
+        above, below = ext_ref[e - RAD], ext_ref[e + RAD]
+        step = jnp.dot(
+            slide_ref[...], jnp.concatenate([ext_ref[e + RAD - 1], above], axis=0),
+            preferred_element_type=jnp.float32,
+        )
+        side = side + step
+        ring = jnp.dot(
+            pair_ref[...], jnp.concatenate([above, below], axis=0),
+            preferred_element_type=jnp.float32,
+        )
+        total = ring + side
         fit = scale_ref[...] * total
-        residual_f = row.astype(jnp.float32)
+        residual_f = ext_ref[e].astype(jnp.float32)
         det = (residual_f - fit).astype(jnp.bfloat16)
         if keep is not None:
             det = (det.astype(jnp.float32) * keep).astype(jnp.bfloat16)
@@ -131,16 +138,16 @@
     keep_bot = edge_ref[1]
 
     def top_d(k, side):
-        side, _ = detrend(k, side, top_ref[first + k], keep_top)
+        side, _ = detrend(k, side, keep_top)
         return side
 
     def own_d(r, side):
-        side, fit = detrend(GR + r, side, own_ref[r], None)
+        side, fit = detrend(GR + r, side, None)
         back_ref[r] = fit.astype(back_ref.dtype)
         return side
 
     def bot_d(r, side):
-        side, _ = detrend(GR + own + r, side, bot_ref[r], keep_bot)
+        side, _ = detrend(GR + own + r, side, keep_bot)
         return side
 
     side = lax.fori_loop(0, GR, top_d, side)
@@ -155,7 +162,7 @@
         return c
 
     lax.fori_loop(0, own, smooth, 0)
-    frame_block = norm_ref.shape[2]
+    cols, frame_block = norm_ref.shape[1], norm_ref.shape[2]
     grad_ref[...] = jnp.dot(
         frows_ref[...], norm_ref[...].reshape(own * cols, frame_block),
         preferred_element_type=jnp.float32,
@@ -166,7 +173,7 @@
     halo, own_rows, cols, frames = top.shape[0], own.shape[0], own.shape[1], own.shape[2]
     slots = frows.shape[0]
     ext = 2 * halo + own_rows
-    wcat, blur = band_constants(cols)
+    pair, slide, side, blur = band_constants(cols)
     grid = (frames // frame_block,)
     row_block = lambda n: pl.BlockSpec((n, cols, frame_block), lambda j: (0, 0, j))
     fixed = lambda shape: pl.BlockSpec(shape, lambda j: (0,) * len(shape))
@@ -176,20 +183,20 @@
         in_specs=[
             pl.BlockSpec(memory_space=pltpu.SMEM),
             row_block(halo), row_block(own_rows), row_block(halo),
-            fixed((2 * cols, cols)), fixed((cols, cols)), fixed((cols, frame_block)),
+            fixed((cols, 2 * cols)), fixed((cols, 2 * cols)), fixed((cols, cols)),
+            fixed((cols, cols)), fixed((cols, frame_block)),
             fixed((own_rows, cols, frame_block)), fixed((slots, own_rows * cols)),
         ],
         out_specs=[row_block(own_rows), pl.BlockSpec((slots, frame_block), lambda j: (0, j))],
         out_shape=[jax.ShapeDtypeStruct(own.shape, jnp.bfloat16),
                    jax.ShapeDtypeStruct((slots, frames), jnp.float32)],
         scratch_shapes=[
-            pltpu.VMEM((ext, cols, frame_block), jnp.float32),
-            pltpu.VMEM((ext, cols, frame_block), jnp.float32),
+            pltpu.VMEM((ext, cols, frame_block), jnp.bfloat16),
             pltpu.VMEM((own_rows + 2 * GR, cols, frame_block), jnp.float32),
             pltpu.VMEM((own_rows, cols, frame_block), jnp.bfloat16),
         ],
         compiler_params=pltpu.CompilerParams(vmem_limit_bytes=60 * 1024 * 1024),
-    )(edge, top, own, bot, jnp.asarray(wcat), jnp.asarray(blur), scale, recip, frows)
+    )(edge, top, own, bot, *(jnp.asarray(m) for m in (pair, slide, side, blur)), scale, recip, frows)
 
 
 MESH = pl.DeviceIdType.MESH

time: 163 us -> 161 us (0.988)
  Pallas kernels: 104 us -> 101 us
    pallas_call x1, Pallas kernels: 56.2 us -> 53.6 us  [stencil(): pl.pallas_call(stencil_kernel, grid=grid, in_specs=[pl.BlockSpec(memory_s...]
where the time goes in v6:
time: 161 us; the launch traced here: 160 us
  Pallas kernels  101 us (63%)
  local copies, waits for them, and re-layouts  23 us (14%)
  matrix products  15.2 us (9%)
  starting transfers between devices  10.2 us (6%)
  other arithmetic  5.75 us (4%)
  waiting for transfers between devices  3.93 us (2%)
    pallas_call x1, Pallas kernels, stencil(): pl.pallas_call(stencil_kernel, grid=grid, in_specs=[pl.BlockSpec(memory_s...  53.6 us
    pallas_call x2, Pallas kernels, exchange(): pl.pallas_call(exchange_kernel, out_shape=jax.ShapeDtypeStruct(outbox.sha...  47.4 us
    unnamed x17, local copies, waits for them, and re-layouts  8.51 us
    dot_general x1, matrix products, on_device(): jnp.einsum('rcs,st->rct', frows_t, trace_inbox, preferred_element_type=jn...  5.22 us
    dot_general x1, matrix products, on_device(): jnp.einsum('srj,sjc->src', tile_grid, column_onehot, preferred_element_ty...  4.17 us
    ppermute x1, waiting for transfers between devices, on_device(): bottom_halo = lax.ppermute(residual[:halo], 'pix', down)  3.93 us
  transfers between devices with their start and end apart: 4, of which 1 were waited for; matrix products, arithmetic and copies ran while one was open for 9% of the time, Pallas kernels for 0%

profile of v6, /device:TPU:1, one launch (start us, length us, event | category | flops | bytes accessed | tf_op | source)
XLA Modules:
  0.0 160.2 jit_solution(15442937813027684389)
XLA Ops:
  0.6 0.9 convert_reduce_fusion
  1.5 0.7 multiply_add_fusion.2
  2.2 0.7 convert_bitcast_fusion.1
  2.9 0.1 broadcast_in_dim.10
  2.9 1.5 convolution_convert_fusion
  4.4 1.0 reshape.225.out_ref
  5.4 29.9 %shard_map.140 = bf16[64,4,1408]{2,1,0:T(4,128)(2,1)} custom-call(bf16[64,4,1408]{2,1,0:T(4,128)(2,1)} %reshape.225.out_ref), custom_call_target="tpu_custom_call" | custom-call | tf_op jit(solution)/shard_map/pallas_call | solution.py:252
  35.3 1.5 reshape.226
  36.9 0.1 slice.90
  36.9 0.1 add_reduce_fusion
  37.1 0.2 copy.17
  37.3 3.0 %copy.18 = bf16[256,32,32]{2,1,0:T(8,128)(2,1)S(1)} copy(bf16[256,32,32]{0,2,1:T(8,128)(2,1)S(1)} %bitcast.66) | data formatting | bytes 1048576 | tf_op jit(solution)/shard_map/reshape | solution.py:301
  40.3 0.0 copy-start.6
  40.3 0.1 iota_add_fusion
  40.4 2.8 %convert_bitcast_fusion = bf16[32,256,256]{1,0,2:T(8,128)(2,1)S(1)} fusion(bf16[256,32,32]{2,1,0:T(8,128)(2,1)S(1)} %copy.18, s32[256,32]{1,0:T(8,128)S(1)} %iota_add_fusion), kind=kOutput, calls=%fused_computation.8 | convolution fusion | flops 138412032 | bytes 4751360 | tf_op jit(solution)/shard_map/srj,sjc->rcs/dot_general | solution.py:305
  43.2 0.0 copy-done.6
  43.2 5.2 %fusion.own_ref = bf16[32,256,256]{2,1,0:T(8,128)(2,1)S(1)} fusion(bf16[1,32,256,256]{3,2,1,0:T(8,128)(2,1)S(1)} %copy-done.6, bf16[32,256,256]{1,0,2:T(8,128)(2,1)S(1)} %convert_bitcast_fusion, bf16[256,1408]{1,0:T(8,128)(2,1)S(1)} %reshape.226), kind=kOutput, calls=%fused_computation.2 | convolution fusion | flops 1080033280 | bytes 12713984 | tf_op jit(solution)/shard_map/rcs,st->rct/dot_general | solution.py:308
  48.4 0.0 copy-start
  48.4 0.0 copy-start.7
  48.5 2.5 %fusion.71 = (bf16[15,256,256]{2,1,0:T(8,128)(2,1)}, bf16[15,256,256]{2,1,0:T(8,128)(2,1)}) fusion(bf16[32,256,256]{2,1,0:T(8,128)(2,1)S(1)} %fusion.own_ref), kind=kLoop, calls=%fused_computation.117 | loop fusion | bytes 7864320 | tf_op jit(solution)/shard_map/slice | solution.py:317
  51.0 2.9 %collective-permute-start = (bf16[15,256,256]{2,1,0:T(8,128)(2,1)}, bf16[15,256,256]{2,1,0:T(8,128)(2,1)}, u32[]{:S(2)}, u32[]{:S(2)}) collective-permute-start(bf16[15,256,256]{2,1,0:T(8,128)(2,1)} %get-tuple-element.11), channel_id=1, source_target_pairs={{0,4},{4,8},{8,12},{12,16},{16,20},{20,24},{24,28},{28,32},{32,36}... | collective-permute-start | bytes 5898248 | tf_op jit(solution)/shard_map/ppermute | solution.py:316
  53.9 2.7 %collective-permute-start.1 = (bf16[15,256,256]{2,1,0:T(8,128)(2,1)}, bf16[15,256,256]{2,1,0:T(8,128)(2,1)}, u32[]{:S(2)}, u32[]{:S(2)}) collective-permute-start(bf16[15,256,256]{2,1,0:T(8,128)(2,1)} %get-tuple-element.10), channel_id=1, source_target_pairs={{4,0},{8,4},{12,8},{16,12},{20,16},{24,20},{28,24},{32,28},{36,32}... | collective-permute-start | bytes 5898248 | tf_op jit(solution)/shard_map/ppermute | solution.py:317
  56.6 0.0 copy-done.7
  56.6 0.0 copy-start.1
  56.6 0.0 copy-start.5
  56.6 0.0 copy-start.3
  56.7 0.0 copy-start.4
  56.7 1.3 fusion.10
  58.0 0.0 copy-done
  58.1 3.1 %collective-permute-start.2 = (f32[1,32,256]{2,1,0:T(8,128)S(1)}, f32[1,32,256]{2,1,0:T(8,128)S(1)}, u32[]{:S(2)}, u32[]{:S(2)}) collective-permute-start(f32[1,32,256]{2,1,0:T(8,128)S(1)} %div.43), channel_id=1, source_target_pairs={{0,1},{1,2},{2,3},{4,5},{5,6},{6,7},{8,9},{9,10},{10,11},{12,13},{... | collective-permute-start | bytes 98312 | tf_op jit(solution)/shard_map/ppermute | solution.py:29
  61.2 1.5 collective-permute-start.3
  62.7 0.0 copy-done.1
  62.7 0.1 multiply_reduce_fusion
  62.8 0.0 copy-done.5
  62.8 0.0 copy-done.3
  62.9 0.0 copy-done.4
  62.9 4.2 %fusion.7 = bf16[256,32,256]{2,1,0:T(8,128)(2,1)} fusion(bf16[256,32,32]{2,1,0:T(8,128)(2,1)S(1)} %copy.18, s32[256,32]{1,0:T(8,128)S(1)} %iota_add_fusion), kind=kOutput, calls=%fused_computation.11 | convolution fusion | flops 138412032 | bytes 4751360 | tf_op jit(solution)/shard_map/srj,sjc->src/dot_general | solution.py:302
  67.1 0.7 add_convert_fusion.edge_ref
  67.8 8.5 %copy.21 = bf16[32,8,32,256]{3,1,2,0:T(8,128)(2,1)} copy(bf16[32,8,32,256]{3,2,1,0:T(8,128)(2,1)} %bitcast.64) | data formatting | bytes 8388608
  76.2 0.0 collective-permute-done.2
  76.2 0.0 collective-permute-done.3
  76.2 0.0 collective-permute-done.top_ref
  76.2 3.9 %collective-permute-done.1.bot_ref = bf16[15,256,256]{2,1,0:T(8,128)(2,1)} collective-permute-done((bf16[15,256,256]{2,1,0:T(8,128)(2,1)}, bf16[15,256,256]{2,1,0:T(8,128)(2,1)}, u32[]{:S(2)}, u32[]{:S(2)}) %collective-permute-start.1) | collective-permute-done | bytes 1966112 | tf_op jit(solution)/shard_map/ppermute | solution.py:317
  80.2 2.6 %broadcast_in_dim.12.recip_ref = f32[32,256,128]{2,1,0:T(8,128)} broadcast(f32[32,256]{1,0:T(8,128)S(1)} %fusion.61), dimensions={0,1} | broadcast | bytes 4227072 | tf_op jit(solution)/shard_map/broadcast_in_dim | solution.py:334
  82.7 0.8 broadcast_in_dim.11.scale_ref
  83.5 53.6 %shard_map.141 = (bf16[32,256,256]{2,1,0:T(8,128)(2,1)}, f32[256,256]{1,0:T(8,128)}) custom-call(f32[2]{0:T(128)} %add_convert_fusion.edge_ref, bf16[15,256,256]{2,1,0:T(8,128)(2,1)} %collective-permute-done.top_ref, bf16[32,256,256]{2,1,0:T(8,128)(2,1)} %copy-done, bf16[15,256,256]{2,1,0:T(8,128)(2,1)} %collective-permute-done.1.bot_ref, ...), custom_call_target="tpu_custom_call" | custom-call | tf_op jit(solution)/shard_map/pallas_call | solution.py:180
  137.1 1.7 %reshape.230.out_ref = f32[64,4,256]{2,1,0:T(4,128)} reshape(f32[256,256]{1,0:T(8,128)} %get-tuple-element.5) | data formatting | bytes 524288 | tf_op jit(solution)/shard_map/reshape | solution.py:343
  138.8 17.5 %shard_map.142 = f32[64,4,256]{2,1,0:T(4,128)} custom-call(f32[64,4,256]{2,1,0:T(4,128)} %reshape.230.out_ref), custom_call_target="tpu_custom_call" | custom-call | tf_op jit(solution)/shard_map/pallas_call | solution.py:252
  156.3 1.0 reshape.231
  157.4 0.3 fusion.11
  157.6 0.2 fusion.21
  157.8 0.2 multiply_add_fusion
  158.0 0.2 fusion.24
  158.2 0.1 fusion.44
  158.3 0.1 fusion.46
  158.4 0.1 fusion.26
  158.5 0.1 fusion.28
  158.7 0.1 fusion.48
  158.8 0.1 fusion.50
  158.9 0.1 fusion.52
  159.0 0.1 fusion.30
  159.2 0.1 fusion.32
  159.3 0.1 fusion.34
  159.4 0.8 fusion.40
  (10 shorter events, 0.1 us)
Async XLA Ops:
  40.3 2.9 %copy-start.6 = (bf16[1,32,256,256]{3,2,1,0:T(8,128)(2,1)S(1)}, bf16[1,32,256,256]{3,2,1,0:T(8,128)(2,1)}, u32[]{:S(2)}) copy-start(bf16[1,32,256,256]{3,2,1,0:T(8,128)(2,1)} %param.13) | copy-start | bytes 12582916
  48.4 9.6 %copy-start = (bf16[32,256,256]{2,1,0:T(8,128)(2,1)}, bf16[32,256,256]{2,1,0:T(8,128)(2,1)S(1)}, u32[]{:S(2)}) copy-start(bf16[32,256,256]{2,1,0:T(8,128)(2,1)S(1)} %fusion.own_ref) | copy-start | bytes 12582916
  48.4 8.2 %copy-start.7 = (bf16[256,256]{1,0:T(8,128)(2,1)S(1)}, bf16[256,256]{1,0:T(8,128)(2,1)}, u32[]{:S(2)}) copy-start(bf16[256,256]{1,0:T(8,128)(2,1)} %constant.52.clone) | copy-start | bytes 393220
  51.0 25.3 %collective-permute-start = (bf16[15,256,256]{2,1,0:T(8,128)(2,1)}, bf16[15,256,256]{2,1,0:T(8,128)(2,1)}, u32[]{:S(2)}, u32[]{:S(2)}) collective-permute-start(bf16[15,256,256]{2,1,0:T(8,128)(2,1)} %get-tuple-element.11), channel_id=1, source_target_pairs={{0,4},{4,8},{8,12},{12,16},{16,20},{20,24},{24,28},{28,32},{32,36}... | collective-permute-start | bytes 5898248 | tf_op jit(solution)/shard_map/ppermute | solution.py:316
  53.9 26.3 %collective-permute-start.1 = (bf16[15,256,256]{2,1,0:T(8,128)(2,1)}, bf16[15,256,256]{2,1,0:T(8,128)(2,1)}, u32[]{:S(2)}, u32[]{:S(2)}) collective-permute-start(bf16[15,256,256]{2,1,0:T(8,128)(2,1)} %get-tuple-element.10), channel_id=1, source_target_pairs={{4,0},{8,4},{12,8},{16,12},{20,16},{24,20},{28,24},{32,28},{36,32}... | collective-permute-start | bytes 5898248 | tf_op jit(solution)/shard_map/ppermute | solution.py:317
  56.6 6.1 %copy-start.1 = (bf16[1,128,1024]{2,1,0:T(8,128)(2,1)S(1)}, bf16[1,128,1024]{2,1,0:T(8,128)(2,1)}, u32[]{:S(2)}) copy-start(bf16[1,128,1024]{2,1,0:T(8,128)(2,1)} %param.14) | copy-start | bytes 786436
  56.6 6.2 %copy-start.5 = (f32[1,256]{1,0:T(1,128)S(1)}, f32[1,256]{1,0:T(1,128)}, u32[]{:S(2)}) copy-start(f32[1,256]{1,0:T(1,128)} %param.18) | copy-start | bytes 3076
  56.6 6.2 %copy-start.3 = (f32[1,128]{1,0:T(1,128)S(1)}, f32[1,128]{1,0:T(1,128)}, u32[]{:S(2)}) copy-start(f32[1,128]{1,0:T(1,128)} %param.20) | copy-start | bytes 1540
  56.7 6.2 %copy-start.4 = (f32[1,128]{1,0:T(1,128)S(1)}, f32[1,128]{1,0:T(1,128)}, u32[]{:S(2)}) copy-start(f32[1,128]{1,0:T(1,128)} %param.19) | copy-start | bytes 1540
  58.1 18.1 %collective-permute-start.2 = (f32[1,32,256]{2,1,0:T(8,128)S(1)}, f32[1,32,256]{2,1,0:T(8,128)S(1)}, u32[]{:S(2)}, u32[]{:S(2)}) collective-permute-start(f32[1,32,256]{2,1,0:T(8,128)S(1)} %div.43), channel_id=1, source_target_pairs={{0,1},{1,2},{2,3},{4,5},{5,6},{6,7},{8,9},{9,10},{10,11},{12,13},{... | collective-permute-start | bytes 98312 | tf_op jit(solution)/shard_map/ppermute | solution.py:29
  61.2 15.0 %collective-permute-start.3 = (f32[1,32,256]{2,1,0:T(8,128)S(1)}, f32[1,32,256]{2,1,0:T(8,128)S(1)}, u32[]{:S(2)}, u32[]{:S(2)}) collective-permute-start(f32[1,32,256]{2,1,0:T(8,128)S(1)} %div.43), channel_id=1, source_target_pairs={{1,0},{2,1},{3,2},{5,4},{6,5},{7,6},{9,8},{10,9},{11,10},{13,12},{... | collective-permute-start | bytes 98312 | tf_op jit(solution)/shard_map/ppermute | solution.py:30
  83.5 73.9 %copy-start.2 = (bf16[1,128,256]{2,1,0:T(8,128)(2,1)S(1)}, bf16[1,128,256]{2,1,0:T(8,128)(2,1)}, u32[]{:S(2)}) copy-start(bf16[1,128,256]{2,1,0:T(8,128)(2,1)} %param.15) | copy-start | bytes 196612

commit v7 on v6

--- a/solution.py
+++ b/solution.py
@@ -85,10 +85,17 @@
 
 
 def stencil_kernel(edge_ref, top_ref, own_ref, bot_ref, pair_ref, slide_ref, side_ref, blur_ref,
-                   scale_ref, recip_ref, frows_ref, back_ref, grad_ref, ext_ref, rows_ref, norm_ref):
+                   scale_ref, recip_ref, frows_hbm, back_ref, grad_ref, ext_ref, rows_ref, norm_ref,
+                   frows_ref, frows_sem):
     halo = top_ref.shape[0]
     own = own_ref.shape[0]
     taps = [float(v) for v in tap_values()]
+    first_step = pl.program_id(0) == 0
+    frows_copy = pltpu.make_async_copy(frows_hbm, frows_ref, frows_sem)
+
+    @pl.when(first_step)
+    def _():
+        frows_copy.start()
 
     def copy_top(r, c):
         ext_ref[r] = top_ref[r]
@@ -163,6 +170,11 @@
 
     lax.fori_loop(0, own, smooth, 0)
     cols, frame_block = norm_ref.shape[1], norm_ref.shape[2]
+
+    @pl.when(first_step)
+    def _():
+        frows_copy.wait()
+
     grad_ref[...] = jnp.dot(
         frows_ref[...], norm_ref[...].reshape(own * cols, frame_block),
         preferred_element_type=jnp.float32,
@@ -185,7 +197,7 @@
             row_block(halo), row_block(own_rows), row_block(halo),
             fixed((cols, 2 * cols)), fixed((cols, 2 * cols)), fixed((cols, cols)),
             fixed((cols, cols)), fixed((cols, frame_block)),
-            fixed((own_rows, cols, frame_block)), fixed((slots, own_rows * cols)),
+            fixed((own_rows, cols, frame_block)), pl.BlockSpec(memory_space=pl.ANY),
         ],
         out_specs=[row_block(own_rows), pl.BlockSpec((slots, frame_block), lambda j: (0, j))],
         out_shape=[jax.ShapeDtypeStruct(own.shape, jnp.bfloat16),
@@ -194,6 +206,8 @@
             pltpu.VMEM((ext, cols, frame_block), jnp.bfloat16),
             pltpu.VMEM((own_rows + 2 * GR, cols, frame_block), jnp.float32),
             pltpu.VMEM((own_rows, cols, frame_block), jnp.bfloat16),
+            pltpu.VMEM((slots, own_rows * cols), jnp.bfloat16),
+            pltpu.SemaphoreType.DMA,
         ],
         compiler_params=pltpu.CompilerParams(vmem_limit_bytes=60 * 1024 * 1024),
     )(edge, top, own, bot, *(jnp.asarray(m) for m in (pair, slide, side, blur)), scale, recip, frows)

time: 161 us -> 159 us (0.988)
  no operation moved by 1% of the time
where the time goes in v7:
time: 159 us
  Pallas kernels  99.6 us (63%)
  local copies, waits for them, and re-layouts  23.1 us (15%)
  matrix products  15.2 us (10%)
  starting transfers between devices  10.2 us (6%)
  other arithmetic  5.75 us (4%)
  waiting for transfers between devices  3.93 us (2%)
    pallas_call x1, Pallas kernels, stencil(): pl.pallas_call(stencil_kernel, grid=grid, in_specs=[pl.BlockSpec(memory_s...  52.2 us
    pallas_call x2, Pallas kernels, exchange(): pl.pallas_call(exchange_kernel, out_shape=jax.ShapeDtypeStruct(outbox.sha...  47.4 us
    unnamed x17, local copies, waits for them, and re-layouts  8.51 us
    dot_general x1, matrix products, on_device(): jnp.einsum('rcs,st->rct', frows_t, trace_inbox, preferred_element_type=jn...  5.22 us
    dot_general x1, matrix products, on_device(): jnp.einsum('srj,sjc->src', tile_grid, column_onehot, preferred_element_ty...  4.17 us
    ppermute x1, waiting for transfers between devices, on_device(): bottom_halo = lax.ppermute(residual[:halo], 'pix', down)  3.93 us
  transfers between devices with their start and end apart: 4, of which 1 were waited for; matrix products, arithmetic and copies ran while one was open for 9% of the time, Pallas kernels for 0%

profile of v7, /device:TPU:1, one launch (start us, length us, event | category | flops | bytes accessed | tf_op | source)
XLA Modules:
  0.0 158.9 jit_solution(10521108745373544347)
XLA Ops:
  0.6 0.9 convert_reduce_fusion
  1.5 0.7 multiply_add_fusion.2
  2.2 0.7 convert_bitcast_fusion.1
  2.9 0.1 broadcast_in_dim.10
  2.9 1.5 convolution_convert_fusion
  4.4 1.0 reshape.225.out_ref
  5.4 29.9 %shard_map.140 = bf16[64,4,1408]{2,1,0:T(4,128)(2,1)} custom-call(bf16[64,4,1408]{2,1,0:T(4,128)(2,1)} %reshape.225.out_ref), custom_call_target="tpu_custom_call" | custom-call | tf_op jit(solution)/shard_map/pallas_call | solution.py:266
  35.3 1.5 reshape.226
  36.9 0.1 slice.90
  36.9 0.1 add_reduce_fusion
  37.1 0.2 copy.17
  37.3 3.0 %copy.18 = bf16[256,32,32]{2,1,0:T(8,128)(2,1)S(1)} copy(bf16[256,32,32]{0,2,1:T(8,128)(2,1)S(1)} %bitcast.66) | data formatting | bytes 1048576 | tf_op jit(solution)/shard_map/reshape | solution.py:315
  40.3 0.0 copy-start.6
  40.3 0.1 iota_add_fusion
  40.4 2.8 %convert_bitcast_fusion = bf16[32,256,256]{1,0,2:T(8,128)(2,1)S(1)} fusion(bf16[256,32,32]{2,1,0:T(8,128)(2,1)S(1)} %copy.18, s32[256,32]{1,0:T(8,128)S(1)} %iota_add_fusion), kind=kOutput, calls=%fused_computation.8 | convolution fusion | flops 138412032 | bytes 4751360 | tf_op jit(solution)/shard_map/srj,sjc->rcs/dot_general | solution.py:319
  43.2 0.0 copy-done.6
  43.2 5.2 %fusion.own_ref = bf16[32,256,256]{2,1,0:T(8,128)(2,1)S(1)} fusion(bf16[1,32,256,256]{3,2,1,0:T(8,128)(2,1)S(1)} %copy-done.6, bf16[32,256,256]{1,0,2:T(8,128)(2,1)S(1)} %convert_bitcast_fusion, bf16[256,1408]{1,0:T(8,128)(2,1)S(1)} %reshape.226), kind=kOutput, calls=%fused_computation.2 | convolution fusion | flops 1080033280 | bytes 12713984 | tf_op jit(solution)/shard_map/rcs,st->rct/dot_general | solution.py:322
  48.4 0.0 copy-start
  48.4 0.0 copy-start.7
  48.5 2.5 %fusion.71 = (bf16[15,256,256]{2,1,0:T(8,128)(2,1)}, bf16[15,256,256]{2,1,0:T(8,128)(2,1)}) fusion(bf16[32,256,256]{2,1,0:T(8,128)(2,1)S(1)} %fusion.own_ref), kind=kLoop, calls=%fused_computation.117 | loop fusion | bytes 7864320 | tf_op jit(solution)/shard_map/slice | solution.py:331
  51.0 2.9 %collective-permute-start = (bf16[15,256,256]{2,1,0:T(8,128)(2,1)}, bf16[15,256,256]{2,1,0:T(8,128)(2,1)}, u32[]{:S(2)}, u32[]{:S(2)}) collective-permute-start(bf16[15,256,256]{2,1,0:T(8,128)(2,1)} %get-tuple-element.11), channel_id=1, source_target_pairs={{0,4},{4,8},{8,12},{12,16},{16,20},{20,24},{24,28},{28,32},{32,36}... | collective-permute-start | bytes 5898248 | tf_op jit(solution)/shard_map/ppermute | solution.py:330
  53.9 2.7 %collective-permute-start.1 = (bf16[15,256,256]{2,1,0:T(8,128)(2,1)}, bf16[15,256,256]{2,1,0:T(8,128)(2,1)}, u32[]{:S(2)}, u32[]{:S(2)}) collective-permute-start(bf16[15,256,256]{2,1,0:T(8,128)(2,1)} %get-tuple-element.10), channel_id=1, source_target_pairs={{4,0},{8,4},{12,8},{16,12},{20,16},{24,20},{28,24},{32,28},{36,32}... | collective-permute-start | bytes 5898248 | tf_op jit(solution)/shard_map/ppermute | solution.py:331
  56.6 0.0 copy-done.7
  56.6 0.0 copy-start.1
  56.6 0.0 copy-start.5
  56.6 0.0 copy-start.3
  56.7 0.0 copy-start.4
  56.7 1.3 fusion.10
  58.0 0.0 copy-done
  58.1 3.1 %collective-permute-start.2 = (f32[1,32,256]{2,1,0:T(8,128)S(1)}, f32[1,32,256]{2,1,0:T(8,128)S(1)}, u32[]{:S(2)}, u32[]{:S(2)}) collective-permute-start(f32[1,32,256]{2,1,0:T(8,128)S(1)} %div.43), channel_id=1, source_target_pairs={{0,1},{1,2},{2,3},{4,5},{5,6},{6,7},{8,9},{9,10},{10,11},{12,13},{... | collective-permute-start | bytes 98312 | tf_op jit(solution)/shard_map/ppermute | solution.py:29
  61.2 1.5 collective-permute-start.3
  62.7 0.0 copy-done.1
  62.7 0.1 multiply_reduce_fusion
  62.8 0.0 copy-done.5
  62.8 0.0 copy-done.3
  62.9 0.0 copy-done.4
  62.9 4.2 %fusion.7 = bf16[256,32,256]{2,1,0:T(8,128)(2,1)} fusion(bf16[256,32,32]{2,1,0:T(8,128)(2,1)S(1)} %copy.18, s32[256,32]{1,0:T(8,128)S(1)} %iota_add_fusion), kind=kOutput, calls=%fused_computation.11 | convolution fusion | flops 138412032 | bytes 4751360 | tf_op jit(solution)/shard_map/srj,sjc->src/dot_general | solution.py:316
  67.1 0.7 add_convert_fusion.edge_ref
  67.8 8.5 %copy.21 = bf16[32,8,32,256]{3,1,2,0:T(8,128)(2,1)} copy(bf16[32,8,32,256]{3,2,1,0:T(8,128)(2,1)} %bitcast.64) | data formatting | bytes 8388608
  76.2 0.0 collective-permute-done.2
  76.2 0.0 collective-permute-done.3
  76.2 0.0 collective-permute-done.top_ref
  76.2 3.9 %collective-permute-done.1.bot_ref = bf16[15,256,256]{2,1,0:T(8,128)(2,1)} collective-permute-done((bf16[15,256,256]{2,1,0:T(8,128)(2,1)}, bf16[15,256,256]{2,1,0:T(8,128)(2,1)}, u32[]{:S(2)}, u32[]{:S(2)}) %collective-permute-start.1) | collective-permute-done | bytes 1966112 | tf_op jit(solution)/shard_map/ppermute | solution.py:331
  80.2 2.6 %broadcast_in_dim.12.recip_ref = f32[32,256,128]{2,1,0:T(8,128)} broadcast(f32[32,256]{1,0:T(8,128)S(1)} %fusion.61), dimensions={0,1} | broadcast | bytes 4227072 | tf_op jit(solution)/shard_map/broadcast_in_dim | solution.py:348
  82.7 0.8 broadcast_in_dim.11.scale_ref
  83.5 52.2 %shard_map.141 = (bf16[32,256,256]{2,1,0:T(8,128)(2,1)}, f32[256,256]{1,0:T(8,128)}) custom-call(f32[2]{0:T(128)} %add_convert_fusion.edge_ref, bf16[15,256,256]{2,1,0:T(8,128)(2,1)} %collective-permute-done.top_ref, bf16[32,256,256]{2,1,0:T(8,128)(2,1)} %copy-done, bf16[15,256,256]{2,1,0:T(8,128)(2,1)} %collective-permute-done.1.bot_ref, ...), custom_call_target="tpu_custom_call" | custom-call | tf_op jit(solution)/shard_map/pallas_call | solution.py:192
  135.7 1.7 %reshape.230.out_ref = f32[64,4,256]{2,1,0:T(4,128)} reshape(f32[256,256]{1,0:T(8,128)} %get-tuple-element.5) | data formatting | bytes 524288 | tf_op jit(solution)/shard_map/reshape | solution.py:357
  137.5 17.5 %shard_map.142 = f32[64,4,256]{2,1,0:T(4,128)} custom-call(f32[64,4,256]{2,1,0:T(4,128)} %reshape.230.out_ref), custom_call_target="tpu_custom_call" | custom-call | tf_op jit(solution)/shard_map/pallas_call | solution.py:266
  155.0 1.0 reshape.231
  156.0 0.3 fusion.11
  156.3 0.2 fusion.21
  156.5 0.2 multiply_add_fusion
  156.7 0.2 fusion.24
  156.9 0.1 fusion.44
  157.0 0.1 fusion.46
  157.1 0.1 fusion.26
  157.2 0.1 fusion.28
  157.3 0.1 fusion.48
  157.5 0.1 fusion.50
  157.6 0.1 fusion.52
  157.7 0.1 fusion.30
  157.8 0.1 fusion.32
  157.9 0.1 fusion.34
  158.1 0.8 fusion.40
  (10 shorter events, 0.1 us)
Async XLA Ops:
  40.3 2.9 %copy-start.6 = (bf16[1,32,256,256]{3,2,1,0:T(8,128)(2,1)S(1)}, bf16[1,32,256,256]{3,2,1,0:T(8,128)(2,1)}, u32[]{:S(2)}) copy-start(bf16[1,32,256,256]{3,2,1,0:T(8,128)(2,1)} %param.13) | copy-start | bytes 12582916
  48.4 9.6 %copy-start = (bf16[32,256,256]{2,1,0:T(8,128)(2,1)}, bf16[32,256,256]{2,1,0:T(8,128)(2,1)S(1)}, u32[]{:S(2)}) copy-start(bf16[32,256,256]{2,1,0:T(8,128)(2,1)S(1)} %fusion.own_ref) | copy-start | bytes 12582916
  48.4 8.2 %copy-start.7 = (bf16[256,256]{1,0:T(8,128)(2,1)S(1)}, bf16[256,256]{1,0:T(8,128)(2,1)}, u32[]{:S(2)}) copy-start(bf16[256,256]{1,0:T(8,128)(2,1)} %constant.52.clone) | copy-start | bytes 393220
  51.0 25.3 %collective-permute-start = (bf16[15,256,256]{2,1,0:T(8,128)(2,1)}, bf16[15,256,256]{2,1,0:T(8,128)(2,1)}, u32[]{:S(2)}, u32[]{:S(2)}) collective-permute-start(bf16[15,256,256]{2,1,0:T(8,128)(2,1)} %get-tuple-element.11), channel_id=1, source_target_pairs={{0,4},{4,8},{8,12},{12,16},{16,20},{20,24},{24,28},{28,32},{32,36}... | collective-permute-start | bytes 5898248 | tf_op jit(solution)/shard_map/ppermute | solution.py:330
  53.9 26.3 %collective-permute-start.1 = (bf16[15,256,256]{2,1,0:T(8,128)(2,1)}, bf16[15,256,256]{2,1,0:T(8,128)(2,1)}, u32[]{:S(2)}, u32[]{:S(2)}) collective-permute-start(bf16[15,256,256]{2,1,0:T(8,128)(2,1)} %get-tuple-element.10), channel_id=1, source_target_pairs={{4,0},{8,4},{12,8},{16,12},{20,16},{24,20},{28,24},{32,28},{36,32}... | collective-permute-start | bytes 5898248 | tf_op jit(solution)/shard_map/ppermute | solution.py:331
  56.6 6.1 %copy-start.1 = (bf16[1,128,1024]{2,1,0:T(8,128)(2,1)S(1)}, bf16[1,128,1024]{2,1,0:T(8,128)(2,1)}, u32[]{:S(2)}) copy-start(bf16[1,128,1024]{2,1,0:T(8,128)(2,1)} %param.14) | copy-start | bytes 786436
  56.6 6.2 %copy-start.5 = (f32[1,256]{1,0:T(1,128)S(1)}, f32[1,256]{1,0:T(1,128)}, u32[]{:S(2)}) copy-start(f32[1,256]{1,0:T(1,128)} %param.18) | copy-start | bytes 3076
  56.6 6.2 %copy-start.3 = (f32[1,128]{1,0:T(1,128)S(1)}, f32[1,128]{1,0:T(1,128)}, u32[]{:S(2)}) copy-start(f32[1,128]{1,0:T(1,128)} %param.20) | copy-start | bytes 1540
  56.7 6.2 %copy-start.4 = (f32[1,128]{1,0:T(1,128)S(1)}, f32[1,128]{1,0:T(1,128)}, u32[]{:S(2)}) copy-start(f32[1,128]{1,0:T(1,128)} %param.19) | copy-start | bytes 1540
  58.1 18.1 %collective-permute-start.2 = (f32[1,32,256]{2,1,0:T(8,128)S(1)}, f32[1,32,256]{2,1,0:T(8,128)S(1)}, u32[]{:S(2)}, u32[]{:S(2)}) collective-permute-start(f32[1,32,256]{2,1,0:T(8,128)S(1)} %div.43), channel_id=1, source_target_pairs={{0,1},{1,2},{2,3},{4,5},{5,6},{6,7},{8,9},{9,10},{10,11},{12,13},{... | collective-permute-start | bytes 98312 | tf_op jit(solution)/shard_map/ppermute | solution.py:29
  61.2 15.0 %collective-permute-start.3 = (f32[1,32,256]{2,1,0:T(8,128)S(1)}, f32[1,32,256]{2,1,0:T(8,128)S(1)}, u32[]{:S(2)}, u32[]{:S(2)}) collective-permute-start(f32[1,32,256]{2,1,0:T(8,128)S(1)} %div.43), channel_id=1, source_target_pairs={{1,0},{2,1},{3,2},{5,4},{6,5},{7,6},{9,8},{10,9},{11,10},{13,12},{... | collective-permute-start | bytes 98312 | tf_op jit(solution)/shard_map/ppermute | solution.py:30
  83.5 72.5 %copy-start.2 = (bf16[1,128,256]{2,1,0:T(8,128)(2,1)S(1)}, bf16[1,128,256]{2,1,0:T(8,128)(2,1)}, u32[]{:S(2)}) copy-start(bf16[1,128,256]{2,1,0:T(8,128)(2,1)} %param.15) | copy-start | bytes 196612

commit v8 on v7

--- a/solution.py
+++ b/solution.py
@@ -85,16 +85,18 @@
 
 
 def stencil_kernel(edge_ref, top_ref, own_ref, bot_ref, pair_ref, slide_ref, side_ref, blur_ref,
-                   scale_ref, recip_ref, frows_hbm, back_ref, grad_ref, ext_ref, rows_ref, norm_ref,
-                   frows_ref, frows_sem):
+                   scale_ref, recip_hbm, frows_hbm, back_ref, grad_ref, ext_ref, rows_ref, norm_ref,
+                   frows_ref, frows_sem, recip_ref, recip_sem):
     halo = top_ref.shape[0]
     own = own_ref.shape[0]
     taps = [float(v) for v in tap_values()]
     first_step = pl.program_id(0) == 0
     frows_copy = pltpu.make_async_copy(frows_hbm, frows_ref, frows_sem)
+    recip_copy = pltpu.make_async_copy(recip_hbm, recip_ref, recip_sem)
 
     @pl.when(first_step)
     def _():
+        recip_copy.start()
         frows_copy.start()
 
     def copy_top(r, c):
@@ -161,6 +163,10 @@
     side = lax.fori_loop(0, own, own_d, side)
     side = lax.fori_loop(0, GR, bot_d, side)
 
+    @pl.when(first_step)
+    def _():
+        recip_copy.wait()
+
     def smooth(y, c):
         acc = taps[GR] * rows_ref[y + GR]
         for o in range(GR):
@@ -197,7 +203,7 @@
             row_block(halo), row_block(own_rows), row_block(halo),
             fixed((cols, 2 * cols)), fixed((cols, 2 * cols)), fixed((cols, cols)),
             fixed((cols, cols)), fixed((cols, frame_block)),
-            fixed((own_rows, cols, frame_block)), pl.BlockSpec(memory_space=pl.ANY),
+            pl.BlockSpec(memory_space=pl.ANY), pl.BlockSpec(memory_space=pl.ANY),
         ],
         out_specs=[row_block(own_rows), pl.BlockSpec((slots, frame_block), lambda j: (0, j))],
         out_shape=[jax.ShapeDtypeStruct(own.shape, jnp.bfloat16),
@@ -207,6 +213,8 @@
             pltpu.VMEM((own_rows + 2 * GR, cols, frame_block), jnp.float32),
             pltpu.VMEM((own_rows, cols, frame_block), jnp.bfloat16),
             pltpu.VMEM((slots, own_rows * cols), jnp.bfloat16),
+            pltpu.SemaphoreType.DMA,
+            pltpu.VMEM((own_rows, cols, frame_block), jnp.float32),
             pltpu.SemaphoreType.DMA,
         ],
         compiler_params=pltpu.CompilerParams(vmem_limit_bytes=60 * 1024 * 1024),
@@ -300,10 +308,11 @@
         (column[0] + 1).astype(jnp.bfloat16)[:, None], (neuron_count, 128)
     )
     payload = jnp.concatenate([footprints[0], traces[0], column_lanes], axis=1)
-    outbox = lax.dot_general(
-        placement_b, payload, contract_first, preferred_element_type=jnp.float32
+    placement_3d = placement_b.reshape(neuron_count, pix_count, capacity)
+    outbox = jnp.einsum(
+        "ndk,nw->dkw", placement_3d, payload, preferred_element_type=jnp.float32
     ).astype(jnp.bfloat16)
-    inbox = exchange(outbox.reshape(pix_count, capacity, -1), 0).reshape(slot_count, -1)
+    inbox = exchange(outbox, 0).reshape(slot_count, -1)
     tile_inbox = inbox[:, :tile_width]
     trace_inbox = inbox[:, tile_width : tile_width + trace_width]
     column_inbox = inbox[:, tile_width + trace_width].astype(jnp.int32)
@@ -354,13 +363,11 @@
         edge, top_halo, residual, bottom_halo, scale, recip,
         frows.reshape(slot_count, row_count * col_count), frame_block
     )
-    home_gradient = exchange(slot_gradient.reshape(pix_count, capacity, -1), 1).reshape(
-        slot_count, -1
-    )
-    gradient = lax.dot_general(
-        placement.astype(jnp.float32),
+    home_gradient = exchange(slot_gradient.reshape(pix_count, capacity, -1), 1)
+    gradient = jnp.einsum(
+        "ndk,dkf->nf",
+        placement.astype(jnp.float32).reshape(neuron_count, pix_count, capacity),
         home_gradient,
-        (((1,), (0,)), ((), ())),
         precision=lax.Precision.HIGHEST,
     )
     foot_f = footprints[0].astype(jnp.float32)

time: 159 us -> 158 us (level)
    reshape x4 -> x2, local copies, waits for them, and re-layouts: 5.32 us -> 3.26 us  [the longest x1 1.72 us: on_device(): home_gradient = exchange(slot_gradient.reshape(pix_count, capacity, -1), 1)]
where the time goes in v8:
time: 158 us
  Pallas kernels  98.5 us (62%)
  local copies, waits for them, and re-layouts  22.4 us (14%)
  matrix products  16.2 us (10%)
  starting transfers between devices  10.2 us (6%)
  other arithmetic  5.76 us (4%)
  waiting for transfers between devices  3.93 us (2%)
    pallas_call x1, Pallas kernels, stencil(): pl.pallas_call(stencil_kernel, grid=grid, in_specs=[pl.BlockSpec(memory_s...  51 us
    pallas_call x2, Pallas kernels, exchange(): pl.pallas_call(exchange_kernel, out_shape=jax.ShapeDtypeStruct(outbox.sha...  47.4 us
    unnamed x17, local copies, waits for them, and re-layouts  8.51 us
    dot_general x1, matrix products, on_device(): jnp.einsum('rcs,st->rct', frows_t, trace_inbox, preferred_element_type=jn...  5.22 us
    dot_general x1, matrix products, on_device(): jnp.einsum('srj,sjc->src', tile_grid, column_onehot, preferred_element_ty...  4.17 us
    ppermute x1, waiting for transfers between devices, on_device(): bottom_halo = lax.ppermute(residual[:halo], 'pix', down)  3.92 us
  transfers between devices with their start and end apart: 4, of which 1 were waited for; matrix products, arithmetic and copies ran while one was open for 9% of the time, Pallas kernels for 0%

profile of v8, /device:TPU:1, one launch (start us, length us, event | category | flops | bytes accessed | tf_op | source)
XLA Modules:
  0.0 158.0 jit_solution(11009285753320497613)
XLA Ops:
  0.6 0.9 convert_reduce_fusion
  1.5 0.7 multiply_add_fusion.3
  2.2 0.7 convert_bitcast_fusion.1
  2.9 0.1 broadcast_in_dim.10
  3.0 1.4 fusion.13
  4.4 1.4 copy.35.out_ref
  5.8 29.9 %shard_map.140 = bf16[64,4,1408]{2,1,0:T(4,128)(2,1)} custom-call(bf16[64,4,1408]{2,1,0:T(4,128)(2,1)} %copy.35.out_ref), custom_call_target="tpu_custom_call" | custom-call | tf_op jit(solution)/shard_map/pallas_call | solution.py:274
  35.7 1.5 reshape.235
  37.2 0.1 slice.90
  37.3 0.1 add_reduce_fusion
  37.4 0.2 copy.22
  37.6 3.0 %copy.23 = bf16[256,32,32]{2,1,0:T(8,128)(2,1)S(1)} copy(bf16[256,32,32]{0,2,1:T(8,128)(2,1)S(1)} %bitcast.74) | data formatting | bytes 1048576 | tf_op jit(solution)/shard_map/reshape | solution.py:324
  40.6 0.0 copy-start.6
  40.6 0.1 iota_add_fusion
  40.7 2.8 %convert_bitcast_fusion = bf16[32,256,256]{1,0,2:T(8,128)(2,1)S(1)} fusion(bf16[256,32,32]{2,1,0:T(8,128)(2,1)S(1)} %copy.23, s32[256,32]{1,0:T(8,128)S(1)} %iota_add_fusion), kind=kOutput, calls=%fused_computation.8 | convolution fusion | flops 138412032 | bytes 4751360 | tf_op jit(solution)/shard_map/srj,sjc->rcs/dot_general | solution.py:328
  43.5 0.0 copy-done.6
  43.5 5.2 %fusion.own_ref = bf16[32,256,256]{2,1,0:T(8,128)(2,1)S(1)} fusion(bf16[1,32,256,256]{3,2,1,0:T(8,128)(2,1)S(1)} %copy-done.6, bf16[32,256,256]{1,0,2:T(8,128)(2,1)S(1)} %convert_bitcast_fusion, bf16[256,1408]{1,0:T(8,128)(2,1)S(1)} %reshape.235), kind=kOutput, calls=%fused_computation.2 | convolution fusion | flops 1080033280 | bytes 12713984 | tf_op jit(solution)/shard_map/rcs,st->rct/dot_general | solution.py:331
  48.8 0.0 copy-start
  48.8 0.0 copy-start.7
  48.8 2.5 %fusion.77 = (bf16[15,256,256]{2,1,0:T(8,128)(2,1)}, bf16[15,256,256]{2,1,0:T(8,128)(2,1)}) fusion(bf16[32,256,256]{2,1,0:T(8,128)(2,1)S(1)} %fusion.own_ref), kind=kLoop, calls=%fused_computation.124 | loop fusion | bytes 7864320 | tf_op jit(solution)/shard_map/slice | solution.py:340
  51.3 2.9 %collective-permute-start = (bf16[15,256,256]{2,1,0:T(8,128)(2,1)}, bf16[15,256,256]{2,1,0:T(8,128)(2,1)}, u32[]{:S(2)}, u32[]{:S(2)}) collective-permute-start(bf16[15,256,256]{2,1,0:T(8,128)(2,1)} %get-tuple-element.11), channel_id=1, source_target_pairs={{0,4},{4,8},{8,12},{12,16},{16,20},{20,24},{24,28},{28,32},{32,36}... | collective-permute-start | bytes 5898248 | tf_op jit(solution)/shard_map/ppermute | solution.py:339
  54.2 2.7 %collective-permute-start.1 = (bf16[15,256,256]{2,1,0:T(8,128)(2,1)}, bf16[15,256,256]{2,1,0:T(8,128)(2,1)}, u32[]{:S(2)}, u32[]{:S(2)}) collective-permute-start(bf16[15,256,256]{2,1,0:T(8,128)(2,1)} %get-tuple-element.10), channel_id=1, source_target_pairs={{4,0},{8,4},{12,8},{16,12},{20,16},{24,20},{28,24},{32,28},{36,32}... | collective-permute-start | bytes 5898248 | tf_op jit(solution)/shard_map/ppermute | solution.py:340
  57.0 0.0 copy-done.7
  57.0 0.0 copy-start.1
  57.0 0.0 copy-start.5
  57.0 0.0 copy-start.3
  57.0 0.0 copy-start.4
  57.0 1.3 fusion.10
  58.4 0.0 copy-done
  58.4 3.1 %collective-permute-start.2 = (f32[1,32,256]{2,1,0:T(8,128)S(1)}, f32[1,32,256]{2,1,0:T(8,128)S(1)}, u32[]{:S(2)}, u32[]{:S(2)}) collective-permute-start(f32[1,32,256]{2,1,0:T(8,128)S(1)} %div.43), channel_id=1, source_target_pairs={{0,1},{1,2},{2,3},{4,5},{5,6},{6,7},{8,9},{9,10},{10,11},{12,13},{... | collective-permute-start | bytes 98312 | tf_op jit(solution)/shard_map/ppermute | solution.py:29
  61.5 1.5 collective-permute-start.3
  63.0 0.0 copy-done.1
  63.0 0.1 multiply_reduce_fusion
  63.2 0.0 copy-done.5
  63.2 0.0 copy-done.3
  63.2 0.0 copy-done.4
  63.2 4.2 %fusion.7 = bf16[256,32,256]{2,1,0:T(8,128)(2,1)} fusion(bf16[256,32,32]{2,1,0:T(8,128)(2,1)S(1)} %copy.23, s32[256,32]{1,0:T(8,128)S(1)} %iota_add_fusion), kind=kOutput, calls=%fused_computation.11 | convolution fusion | flops 138412032 | bytes 4751360 | tf_op jit(solution)/shard_map/srj,sjc->src/dot_general | solution.py:325
  67.4 0.7 add_convert_fusion.edge_ref
  68.1 8.5 %copy.27 = bf16[32,8,32,256]{3,1,2,0:T(8,128)(2,1)} copy(bf16[32,8,32,256]{3,2,1,0:T(8,128)(2,1)} %bitcast.72) | data formatting | bytes 8388608
  76.5 0.0 collective-permute-done.2
  76.5 0.0 collective-permute-done.3
  76.6 0.0 collective-permute-done.top_ref
  76.6 3.9 %collective-permute-done.1.bot_ref = bf16[15,256,256]{2,1,0:T(8,128)(2,1)} collective-permute-done((bf16[15,256,256]{2,1,0:T(8,128)(2,1)}, bf16[15,256,256]{2,1,0:T(8,128)(2,1)}, u32[]{:S(2)}, u32[]{:S(2)}) %collective-permute-start.1) | collective-permute-done | bytes 1966112 | tf_op jit(solution)/shard_map/ppermute | solution.py:340
  80.5 2.6 %broadcast_in_dim.12.recip_hbm = f32[32,256,128]{2,1,0:T(8,128)} broadcast(f32[32,256]{1,0:T(8,128)S(1)} %fusion.67), dimensions={0,1} | broadcast | bytes 4227072 | tf_op jit(solution)/shard_map/broadcast_in_dim | solution.py:357
  83.1 0.8 broadcast_in_dim.11.scale_ref
  83.8 51.0 %shard_map.141 = (bf16[32,256,256]{2,1,0:T(8,128)(2,1)}, f32[256,256]{1,0:T(8,128)}) custom-call(f32[2]{0:T(128)} %add_convert_fusion.edge_ref, bf16[15,256,256]{2,1,0:T(8,128)(2,1)} %collective-permute-done.top_ref, bf16[32,256,256]{2,1,0:T(8,128)(2,1)} %copy-done, bf16[15,256,256]{2,1,0:T(8,128)(2,1)} %collective-permute-done.1.bot_ref, ...), custom_call_target="tpu_custom_call" | custom-call | tf_op jit(solution)/shard_map/pallas_call | solution.py:198
  134.9 1.7 %reshape.239.out_ref = f32[64,4,256]{2,1,0:T(4,128)} reshape(f32[256,256]{1,0:T(8,128)} %get-tuple-element.5) | data formatting | bytes 524288 | tf_op jit(solution)/shard_map/reshape | solution.py:366
  136.6 17.5 %shard_map.142 = f32[64,4,256]{2,1,0:T(4,128)} custom-call(f32[64,4,256]{2,1,0:T(4,128)} %reshape.239.out_ref), custom_call_target="tpu_custom_call" | custom-call | tf_op jit(solution)/shard_map/pallas_call | solution.py:274
  154.1 0.0 copy-done.2
  154.1 1.3 fusion.12
  155.5 0.2 fusion.25
  155.6 0.2 multiply_add_fusion
  155.8 0.2 fusion.28
  156.0 0.1 fusion.48
  156.1 0.1 fusion.50
  156.2 0.1 fusion.30
  156.3 0.1 fusion.32
  156.5 0.1 fusion.52
  156.6 0.1 fusion.54
  156.7 0.1 fusion.56
  156.8 0.1 fusion.34
  157.0 0.1 fusion.36
  157.1 0.1 fusion.38
  157.2 0.8 fusion.44
  (10 shorter events, 0.1 us)
Async XLA Ops:
  40.6 2.9 %copy-start.6 = (bf16[1,32,256,256]{3,2,1,0:T(8,128)(2,1)S(1)}, bf16[1,32,256,256]{3,2,1,0:T(8,128)(2,1)}, u32[]{:S(2)}) copy-start(bf16[1,32,256,256]{3,2,1,0:T(8,128)(2,1)} %param.13) | copy-start | bytes 12582916
  48.8 9.6 %copy-start = (bf16[32,256,256]{2,1,0:T(8,128)(2,1)}, bf16[32,256,256]{2,1,0:T(8,128)(2,1)S(1)}, u32[]{:S(2)}) copy-start(bf16[32,256,256]{2,1,0:T(8,128)(2,1)S(1)} %fusion.own_ref) | copy-start | bytes 12582916
  48.8 8.2 %copy-start.7 = (bf16[256,256]{1,0:T(8,128)(2,1)S(1)}, bf16[256,256]{1,0:T(8,128)(2,1)}, u32[]{:S(2)}) copy-start(bf16[256,256]{1,0:T(8,128)(2,1)} %constant.53.clone) | copy-start | bytes 393220
  51.3 25.3 %collective-permute-start = (bf16[15,256,256]{2,1,0:T(8,128)(2,1)}, bf16[15,256,256]{2,1,0:T(8,128)(2,1)}, u32[]{:S(2)}, u32[]{:S(2)}) collective-permute-start(bf16[15,256,256]{2,1,0:T(8,128)(2,1)} %get-tuple-element.11), channel_id=1, source_target_pairs={{0,4},{4,8},{8,12},{12,16},{16,20},{20,24},{24,28},{28,32},{32,36}... | collective-permute-start | bytes 5898248 | tf_op jit(solution)/shard_map/ppermute | solution.py:339
  54.2 26.3 %collective-permute-start.1 = (bf16[15,256,256]{2,1,0:T(8,128)(2,1)}, bf16[15,256,256]{2,1,0:T(8,128)(2,1)}, u32[]{:S(2)}, u32[]{:S(2)}) collective-permute-start(bf16[15,256,256]{2,1,0:T(8,128)(2,1)} %get-tuple-element.10), channel_id=1, source_target_pairs={{4,0},{8,4},{12,8},{16,12},{20,16},{24,20},{28,24},{32,28},{36,32}... | collective-permute-start | bytes 5898248 | tf_op jit(solution)/shard_map/ppermute | solution.py:340
  57.0 6.1 %copy-start.1 = (bf16[1,128,1024]{2,1,0:T(8,128)(2,1)S(1)}, bf16[1,128,1024]{2,1,0:T(8,128)(2,1)}, u32[]{:S(2)}) copy-start(bf16[1,128,1024]{2,1,0:T(8,128)(2,1)} %param.14) | copy-start | bytes 786436
  57.0 6.2 %copy-start.5 = (f32[1,256]{1,0:T(1,128)S(1)}, f32[1,256]{1,0:T(1,128)}, u32[]{:S(2)}) copy-start(f32[1,256]{1,0:T(1,128)} %param.18) | copy-start | bytes 3076
  57.0 6.2 %copy-start.3 = (f32[1,128]{1,0:T(1,128)S(1)}, f32[1,128]{1,0:T(1,128)}, u32[]{:S(2)}) copy-start(f32[1,128]{1,0:T(1,128)} %param.20) | copy-start | bytes 1540
  57.0 6.2 %copy-start.4 = (f32[1,128]{1,0:T(1,128)S(1)}, f32[1,128]{1,0:T(1,128)}, u32[]{:S(2)}) copy-start(f32[1,128]{1,0:T(1,128)} %param.19) | copy-start | bytes 1540
  58.4 18.2 %collective-permute-start.2 = (f32[1,32,256]{2,1,0:T(8,128)S(1)}, f32[1,32,256]{2,1,0:T(8,128)S(1)}, u32[]{:S(2)}, u32[]{:S(2)}) collective-permute-start(f32[1,32,256]{2,1,0:T(8,128)S(1)} %div.43), channel_id=1, source_target_pairs={{0,1},{1,2},{2,3},{4,5},{5,6},{6,7},{8,9},{9,10},{10,11},{12,13},{... | collective-permute-start | bytes 98312 | tf_op jit(solution)/shard_map/ppermute | solution.py:29
  61.5 15.0 %collective-permute-start.3 = (f32[1,32,256]{2,1,0:T(8,128)S(1)}, f32[1,32,256]{2,1,0:T(8,128)S(1)}, u32[]{:S(2)}, u32[]{:S(2)}) collective-permute-start(f32[1,32,256]{2,1,0:T(8,128)S(1)} %div.43), channel_id=1, source_target_pairs={{1,0},{2,1},{3,2},{5,4},{6,5},{7,6},{9,8},{10,9},{11,10},{13,12},{... | collective-permute-start | bytes 98312 | tf_op jit(solution)/shard_map/ppermute | solution.py:30
  83.8 70.3 %copy-start.2 = (bf16[1,128,256]{2,1,0:T(8,128)(2,1)S(1)}, bf16[1,128,256]{2,1,0:T(8,128)(2,1)}, u32[]{:S(2)}) copy-start(bf16[1,128,256]{2,1,0:T(8,128)(2,1)} %param.15) | copy-start | bytes 196612

commit v9 on v8

--- a/solution.py
+++ b/solution.py
@@ -116,11 +116,16 @@
     lax.fori_loop(0, halo, copy_bot, 0)
 
     first = halo - GR
-    side = jnp.dot(side_ref[...], ext_ref[first - RAD], preferred_element_type=jnp.float32)
+    column_sum = ext_ref[first - RAD].astype(jnp.float32)
     for i in range(1, 2 * RAD - 1):
-        side = side + jnp.dot(
-            side_ref[...], ext_ref[first - RAD + i], preferred_element_type=jnp.float32
-        )
+        column_sum = column_sum + ext_ref[first - RAD + i].astype(jnp.float32)
+    high = column_sum.astype(jnp.bfloat16)
+    rest = column_sum - high.astype(jnp.float32)
+    middle = rest.astype(jnp.bfloat16)
+    low = (rest - middle.astype(jnp.float32)).astype(jnp.bfloat16)
+    side = jnp.dot(side_ref[...], high, preferred_element_type=jnp.float32)
+    side = side + jnp.dot(side_ref[...], middle, preferred_element_type=jnp.float32)
+    side = side + jnp.dot(side_ref[...], low, preferred_element_type=jnp.float32)
 
     def detrend(k, side, keep):
         e = first + k

time: 158 us -> 157 us (level)
  no operation moved by 1% of the time
where the time goes in v9:
time: 157 us
  Pallas kernels  97.5 us (62%)
  local copies, waits for them, and re-layouts  22.4 us (14%)
  matrix products  16.2 us (10%)
  starting transfers between devices  10.2 us (6%)
  other arithmetic  5.76 us (4%)
  waiting for transfers between devices  3.93 us (3%)
    pallas_call x1, Pallas kernels, stencil(): pl.pallas_call(stencil_kernel, grid=grid, in_specs=[pl.BlockSpec(memory_s...  50.1 us
    pallas_call x2, Pallas kernels, exchange(): pl.pallas_call(exchange_kernel, out_shape=jax.ShapeDtypeStruct(outbox.sha...  47.4 us
    unnamed x17, local copies, waits for them, and re-layouts  8.51 us
    dot_general x1, matrix products, on_device(): jnp.einsum('rcs,st->rct', frows_t, trace_inbox, preferred_element_type=jn...  5.22 us
    dot_general x1, matrix products, on_device(): jnp.einsum('srj,sjc->src', tile_grid, column_onehot, preferred_element_ty...  4.17 us
    ppermute x1, waiting for transfers between devices, on_device(): bottom_halo = lax.ppermute(residual[:halo], 'pix', down)  3.92 us
  transfers between devices with their start and end apart: 4, of which 1 were waited for; matrix products, arithmetic and copies ran while one was open for 9% of the time, Pallas kernels for 0%

profile of v9, /device:TPU:1, one launch (start us, length us, event | category | flops | bytes accessed | tf_op | source)
XLA Modules:
  0.0 157.0 jit_solution(1127374490092066822)
XLA Ops:
  0.6 0.9 convert_reduce_fusion
  1.5 0.7 multiply_add_fusion.3
  2.2 0.7 convert_bitcast_fusion.1
  2.9 0.1 broadcast_in_dim.10
  3.0 1.4 fusion.13
  4.4 1.4 copy.35.out_ref
  5.8 29.9 %shard_map.140 = bf16[64,4,1408]{2,1,0:T(4,128)(2,1)} custom-call(bf16[64,4,1408]{2,1,0:T(4,128)(2,1)} %copy.35.out_ref), custom_call_target="tpu_custom_call" | custom-call | tf_op jit(solution)/shard_map/pallas_call | solution.py:279
  35.7 1.5 reshape.235
  37.2 0.1 slice.90
  37.3 0.1 add_reduce_fusion
  37.4 0.2 copy.22
  37.6 3.0 %copy.23 = bf16[256,32,32]{2,1,0:T(8,128)(2,1)S(1)} copy(bf16[256,32,32]{0,2,1:T(8,128)(2,1)S(1)} %bitcast.74) | data formatting | bytes 1048576 | tf_op jit(solution)/shard_map/reshape | solution.py:329
  40.6 0.0 copy-start.6
  40.6 0.1 iota_add_fusion
  40.7 2.8 %convert_bitcast_fusion = bf16[32,256,256]{1,0,2:T(8,128)(2,1)S(1)} fusion(bf16[256,32,32]{2,1,0:T(8,128)(2,1)S(1)} %copy.23, s32[256,32]{1,0:T(8,128)S(1)} %iota_add_fusion), kind=kOutput, calls=%fused_computation.8 | convolution fusion | flops 138412032 | bytes 4751360 | tf_op jit(solution)/shard_map/srj,sjc->rcs/dot_general | solution.py:333
  43.5 0.0 copy-done.6
  43.5 5.2 %fusion.own_ref = bf16[32,256,256]{2,1,0:T(8,128)(2,1)S(1)} fusion(bf16[1,32,256,256]{3,2,1,0:T(8,128)(2,1)S(1)} %copy-done.6, bf16[32,256,256]{1,0,2:T(8,128)(2,1)S(1)} %convert_bitcast_fusion, bf16[256,1408]{1,0:T(8,128)(2,1)S(1)} %reshape.235), kind=kOutput, calls=%fused_computation.2 | convolution fusion | flops 1080033280 | bytes 12713984 | tf_op jit(solution)/shard_map/rcs,st->rct/dot_general | solution.py:336
  48.8 0.0 copy-start
  48.8 0.0 copy-start.7
  48.8 2.5 %fusion.77 = (bf16[15,256,256]{2,1,0:T(8,128)(2,1)}, bf16[15,256,256]{2,1,0:T(8,128)(2,1)}) fusion(bf16[32,256,256]{2,1,0:T(8,128)(2,1)S(1)} %fusion.own_ref), kind=kLoop, calls=%fused_computation.124 | loop fusion | bytes 7864320 | tf_op jit(solution)/shard_map/slice | solution.py:345
  51.3 2.9 %collective-permute-start = (bf16[15,256,256]{2,1,0:T(8,128)(2,1)}, bf16[15,256,256]{2,1,0:T(8,128)(2,1)}, u32[]{:S(2)}, u32[]{:S(2)}) collective-permute-start(bf16[15,256,256]{2,1,0:T(8,128)(2,1)} %get-tuple-element.11), channel_id=1, source_target_pairs={{0,4},{4,8},{8,12},{12,16},{16,20},{20,24},{24,28},{28,32},{32,36}... | collective-permute-start | bytes 5898248 | tf_op jit(solution)/shard_map/ppermute | solution.py:344
  54.2 2.7 %collective-permute-start.1 = (bf16[15,256,256]{2,1,0:T(8,128)(2,1)}, bf16[15,256,256]{2,1,0:T(8,128)(2,1)}, u32[]{:S(2)}, u32[]{:S(2)}) collective-permute-start(bf16[15,256,256]{2,1,0:T(8,128)(2,1)} %get-tuple-element.10), channel_id=1, source_target_pairs={{4,0},{8,4},{12,8},{16,12},{20,16},{24,20},{28,24},{32,28},{36,32}... | collective-permute-start | bytes 5898248 | tf_op jit(solution)/shard_map/ppermute | solution.py:345
  57.0 0.0 copy-done.7
  57.0 0.0 copy-start.1
  57.0 0.0 copy-start.5
  57.0 0.0 copy-start.3
  57.0 0.0 copy-start.4
  57.0 1.3 fusion.10
  58.4 0.0 copy-done
  58.4 3.1 %collective-permute-start.2 = (f32[1,32,256]{2,1,0:T(8,128)S(1)}, f32[1,32,256]{2,1,0:T(8,128)S(1)}, u32[]{:S(2)}, u32[]{:S(2)}) collective-permute-start(f32[1,32,256]{2,1,0:T(8,128)S(1)} %div.43), channel_id=1, source_target_pairs={{0,1},{1,2},{2,3},{4,5},{5,6},{6,7},{8,9},{9,10},{10,11},{12,13},{... | collective-permute-start | bytes 98312 | tf_op jit(solution)/shard_map/ppermute | solution.py:29
  61.5 1.5 collective-permute-start.3
  63.0 0.0 copy-done.1
  63.0 0.1 multiply_reduce_fusion
  63.2 0.0 copy-done.5
  63.2 0.0 copy-done.3
  63.2 0.0 copy-done.4
  63.2 4.2 %fusion.7 = bf16[256,32,256]{2,1,0:T(8,128)(2,1)} fusion(bf16[256,32,32]{2,1,0:T(8,128)(2,1)S(1)} %copy.23, s32[256,32]{1,0:T(8,128)S(1)} %iota_add_fusion), kind=kOutput, calls=%fused_computation.11 | convolution fusion | flops 138412032 | bytes 4751360 | tf_op jit(solution)/shard_map/srj,sjc->src/dot_general | solution.py:330
  67.4 0.7 add_convert_fusion.edge_ref
  68.1 8.5 %copy.27 = bf16[32,8,32,256]{3,1,2,0:T(8,128)(2,1)} copy(bf16[32,8,32,256]{3,2,1,0:T(8,128)(2,1)} %bitcast.72) | data formatting | bytes 8388608
  76.5 0.0 collective-permute-done.2
  76.5 0.0 collective-permute-done.3
  76.6 0.0 collective-permute-done.top_ref
  76.6 3.9 %collective-permute-done.1.bot_ref = bf16[15,256,256]{2,1,0:T(8,128)(2,1)} collective-permute-done((bf16[15,256,256]{2,1,0:T(8,128)(2,1)}, bf16[15,256,256]{2,1,0:T(8,128)(2,1)}, u32[]{:S(2)}, u32[]{:S(2)}) %collective-permute-start.1) | collective-permute-done | bytes 1966112 | tf_op jit(solution)/shard_map/ppermute | solution.py:345
  80.5 2.6 %broadcast_in_dim.12.recip_hbm = f32[32,256,128]{2,1,0:T(8,128)} broadcast(f32[32,256]{1,0:T(8,128)S(1)} %fusion.67), dimensions={0,1} | broadcast | bytes 4227072 | tf_op jit(solution)/shard_map/broadcast_in_dim | solution.py:362
  83.1 0.8 broadcast_in_dim.11.scale_ref
  83.8 50.1 %shard_map.141 = (bf16[32,256,256]{2,1,0:T(8,128)(2,1)}, f32[256,256]{1,0:T(8,128)}) custom-call(f32[2]{0:T(128)} %add_convert_fusion.edge_ref, bf16[15,256,256]{2,1,0:T(8,128)(2,1)} %collective-permute-done.top_ref, bf16[32,256,256]{2,1,0:T(8,128)(2,1)} %copy-done, bf16[15,256,256]{2,1,0:T(8,128)(2,1)} %collective-permute-done.1.bot_ref, ...), custom_call_target="tpu_custom_call" | custom-call | tf_op jit(solution)/shard_map/pallas_call | solution.py:203
  133.9 1.7 %reshape.239.out_ref = f32[64,4,256]{2,1,0:T(4,128)} reshape(f32[256,256]{1,0:T(8,128)} %get-tuple-element.5) | data formatting | bytes 524288 | tf_op jit(solution)/shard_map/reshape | solution.py:371
  135.6 17.5 %shard_map.142 = f32[64,4,256]{2,1,0:T(4,128)} custom-call(f32[64,4,256]{2,1,0:T(4,128)} %reshape.239.out_ref), custom_call_target="tpu_custom_call" | custom-call | tf_op jit(solution)/shard_map/pallas_call | solution.py:279
  153.2 0.0 copy-done.2
  153.2 1.3 fusion.12
  154.5 0.2 fusion.25
  154.7 0.2 multiply_add_fusion
  154.8 0.2 fusion.28
  155.0 0.1 fusion.48
  155.1 0.1 fusion.50
  155.3 0.1 fusion.30
  155.4 0.1 fusion.32
  155.5 0.1 fusion.52
  155.6 0.1 fusion.54
  155.7 0.1 fusion.56
  155.9 0.1 fusion.34
  156.0 0.1 fusion.36
  156.1 0.1 fusion.38
  156.2 0.8 fusion.44
  (10 shorter events, 0.1 us)
Async XLA Ops:
  40.6 2.9 %copy-start.6 = (bf16[1,32,256,256]{3,2,1,0:T(8,128)(2,1)S(1)}, bf16[1,32,256,256]{3,2,1,0:T(8,128)(2,1)}, u32[]{:S(2)}) copy-start(bf16[1,32,256,256]{3,2,1,0:T(8,128)(2,1)} %param.13) | copy-start | bytes 12582916
  48.8 9.6 %copy-start = (bf16[32,256,256]{2,1,0:T(8,128)(2,1)}, bf16[32,256,256]{2,1,0:T(8,128)(2,1)S(1)}, u32[]{:S(2)}) copy-start(bf16[32,256,256]{2,1,0:T(8,128)(2,1)S(1)} %fusion.own_ref) | copy-start | bytes 12582916
  48.8 8.2 %copy-start.7 = (bf16[256,256]{1,0:T(8,128)(2,1)S(1)}, bf16[256,256]{1,0:T(8,128)(2,1)}, u32[]{:S(2)}) copy-start(bf16[256,256]{1,0:T(8,128)(2,1)} %constant.53.clone) | copy-start | bytes 393220
  51.3 25.3 %collective-permute-start = (bf16[15,256,256]{2,1,0:T(8,128)(2,1)}, bf16[15,256,256]{2,1,0:T(8,128)(2,1)}, u32[]{:S(2)}, u32[]{:S(2)}) collective-permute-start(bf16[15,256,256]{2,1,0:T(8,128)(2,1)} %get-tuple-element.11), channel_id=1, source_target_pairs={{0,4},{4,8},{8,12},{12,16},{16,20},{20,24},{24,28},{28,32},{32,36}... | collective-permute-start | bytes 5898248 | tf_op jit(solution)/shard_map/ppermute | solution.py:344
  54.2 26.3 %collective-permute-start.1 = (bf16[15,256,256]{2,1,0:T(8,128)(2,1)}, bf16[15,256,256]{2,1,0:T(8,128)(2,1)}, u32[]{:S(2)}, u32[]{:S(2)}) collective-permute-start(bf16[15,256,256]{2,1,0:T(8,128)(2,1)} %get-tuple-element.10), channel_id=1, source_target_pairs={{4,0},{8,4},{12,8},{16,12},{20,16},{24,20},{28,24},{32,28},{36,32}... | collective-permute-start | bytes 5898248 | tf_op jit(solution)/shard_map/ppermute | solution.py:345
  57.0 6.1 %copy-start.1 = (bf16[1,128,1024]{2,1,0:T(8,128)(2,1)S(1)}, bf16[1,128,1024]{2,1,0:T(8,128)(2,1)}, u32[]{:S(2)}) copy-start(bf16[1,128,1024]{2,1,0:T(8,128)(2,1)} %param.14) | copy-start | bytes 786436
  57.0 6.2 %copy-start.5 = (f32[1,256]{1,0:T(1,128)S(1)}, f32[1,256]{1,0:T(1,128)}, u32[]{:S(2)}) copy-start(f32[1,256]{1,0:T(1,128)} %param.18) | copy-start | bytes 3076
  57.0 6.2 %copy-start.3 = (f32[1,128]{1,0:T(1,128)S(1)}, f32[1,128]{1,0:T(1,128)}, u32[]{:S(2)}) copy-start(f32[1,128]{1,0:T(1,128)} %param.20) | copy-start | bytes 1540
  57.0 6.2 %copy-start.4 = (f32[1,128]{1,0:T(1,128)S(1)}, f32[1,128]{1,0:T(1,128)}, u32[]{:S(2)}) copy-start(f32[1,128]{1,0:T(1,128)} %param.19) | copy-start | bytes 1540
  58.4 18.2 %collective-permute-start.2 = (f32[1,32,256]{2,1,0:T(8,128)S(1)}, f32[1,32,256]{2,1,0:T(8,128)S(1)}, u32[]{:S(2)}, u32[]{:S(2)}) collective-permute-start(f32[1,32,256]{2,1,0:T(8,128)S(1)} %div.43), channel_id=1, source_target_pairs={{0,1},{1,2},{2,3},{4,5},{5,6},{6,7},{8,9},{9,10},{10,11},{12,13},{... | collective-permute-start | bytes 98312 | tf_op jit(solution)/shard_map/ppermute | solution.py:29
  61.5 15.0 %collective-permute-start.3 = (f32[1,32,256]{2,1,0:T(8,128)S(1)}, f32[1,32,256]{2,1,0:T(8,128)S(1)}, u32[]{:S(2)}, u32[]{:S(2)}) collective-permute-start(f32[1,32,256]{2,1,0:T(8,128)S(1)} %div.43), channel_id=1, source_target_pairs={{1,0},{2,1},{3,2},{5,4},{6,5},{7,6},{9,8},{10,9},{11,10},{13,12},{... | collective-permute-start | bytes 98312 | tf_op jit(solution)/shard_map/ppermute | solution.py:30
  83.8 69.3 %copy-start.2 = (bf16[1,128,256]{2,1,0:T(8,128)(2,1)S(1)}, bf16[1,128,256]{2,1,0:T(8,128)(2,1)}, u32[]{:S(2)}) copy-start(bf16[1,128,256]{2,1,0:T(8,128)(2,1)} %param.15) | copy-start | bytes 196612

commit v10 on v9

--- a/solution.py
+++ b/solution.py
@@ -255,6 +255,8 @@
         return c
 
     lax.fori_loop(1, count, greet, 0)
+    local = pltpu.make_async_copy(out_ref.at[me], in_ref.at[me], local_sem)
+    local.start()
     pl.semaphore_wait(barrier, count - 1)
 
     def launch(k, c):
@@ -262,8 +264,6 @@
         return c
 
     lax.fori_loop(1, count, launch, 0)
-    local = pltpu.make_async_copy(out_ref.at[me], in_ref.at[me], local_sem)
-    local.start()
     local.wait()
 
     def finish(k, c):

time: 157 us -> 157 us (level)
  no operation moved by 1% of the time
where the time goes in v10:
time: 157 us
  Pallas kernels  97.5 us (62%)
  local copies, waits for them, and re-layouts  22.4 us (14%)
  matrix products  16.2 us (10%)
  starting transfers between devices  10.2 us (6%)
  other arithmetic  5.76 us (4%)
  waiting for transfers between devices  3.94 us (3%)
    pallas_call x1, Pallas kernels, stencil(): pl.pallas_call(stencil_kernel, grid=grid, in_specs=[pl.BlockSpec(memory_s...  50.1 us
    pallas_call x2, Pallas kernels, exchange(): pl.pallas_call(exchange_kernel, out_shape=jax.ShapeDtypeStruct(outbox.sha...  47.4 us
    unnamed x17, local copies, waits for them, and re-layouts  8.51 us
    dot_general x1, matrix products, on_device(): jnp.einsum('rcs,st->rct', frows_t, trace_inbox, preferred_element_type=jn...  5.22 us
    dot_general x1, matrix products, on_device(): jnp.einsum('srj,sjc->src', tile_grid, column_onehot, preferred_element_ty...  4.17 us
    ppermute x1, waiting for transfers between devices, on_device(): bottom_halo = lax.ppermute(residual[:halo], 'pix', down)  3.93 us
  transfers between devices with their start and end apart: 4, of which 1 were waited for; matrix products, arithmetic and copies ran while one was open for 9% of the time, Pallas kernels for 0%

profile of v10, /device:TPU:1, one launch (start us, length us, event | category | flops | bytes accessed | tf_op | source)
XLA Modules:
  0.0 157.1 jit_solution(13349546627723664884)
XLA Ops:
  0.6 0.9 convert_reduce_fusion
  1.5 0.7 multiply_add_fusion.3
  2.2 0.7 convert_bitcast_fusion.1
  2.9 0.1 broadcast_in_dim.10
  3.0 1.4 fusion.13
  4.4 1.4 copy.35.out_ref
  5.8 29.9 %shard_map.140 = bf16[64,4,1408]{2,1,0:T(4,128)(2,1)} custom-call(bf16[64,4,1408]{2,1,0:T(4,128)(2,1)} %copy.35.out_ref), custom_call_target="tpu_custom_call" | custom-call | tf_op jit(solution)/shard_map/pallas_call | solution.py:279
  35.7 1.5 reshape.235
  37.2 0.1 slice.90
  37.3 0.1 add_reduce_fusion
  37.4 0.2 copy.22
  37.6 3.0 %copy.23 = bf16[256,32,32]{2,1,0:T(8,128)(2,1)S(1)} copy(bf16[256,32,32]{0,2,1:T(8,128)(2,1)S(1)} %bitcast.74) | data formatting | bytes 1048576 | tf_op jit(solution)/shard_map/reshape | solution.py:329
  40.6 0.0 copy-start.6
  40.6 0.1 iota_add_fusion
  40.8 2.8 %convert_bitcast_fusion = bf16[32,256,256]{1,0,2:T(8,128)(2,1)S(1)} fusion(bf16[256,32,32]{2,1,0:T(8,128)(2,1)S(1)} %copy.23, s32[256,32]{1,0:T(8,128)S(1)} %iota_add_fusion), kind=kOutput, calls=%fused_computation.8 | convolution fusion | flops 138412032 | bytes 4751360 | tf_op jit(solution)/shard_map/srj,sjc->rcs/dot_general | solution.py:333
  43.5 0.0 copy-done.6
  43.6 5.2 %fusion.own_ref = bf16[32,256,256]{2,1,0:T(8,128)(2,1)S(1)} fusion(bf16[1,32,256,256]{3,2,1,0:T(8,128)(2,1)S(1)} %copy-done.6, bf16[32,256,256]{1,0,2:T(8,128)(2,1)S(1)} %convert_bitcast_fusion, bf16[256,1408]{1,0:T(8,128)(2,1)S(1)} %reshape.235), kind=kOutput, calls=%fused_computation.2 | convolution fusion | flops 1080033280 | bytes 12713984 | tf_op jit(solution)/shard_map/rcs,st->rct/dot_general | solution.py:336
  48.8 0.0 copy-start
  48.8 0.0 copy-start.7
  48.8 2.5 %fusion.77 = (bf16[15,256,256]{2,1,0:T(8,128)(2,1)}, bf16[15,256,256]{2,1,0:T(8,128)(2,1)}) fusion(bf16[32,256,256]{2,1,0:T(8,128)(2,1)S(1)} %fusion.own_ref), kind=kLoop, calls=%fused_computation.124 | loop fusion | bytes 7864320 | tf_op jit(solution)/shard_map/slice | solution.py:345
  51.3 2.9 %collective-permute-start = (bf16[15,256,256]{2,1,0:T(8,128)(2,1)}, bf16[15,256,256]{2,1,0:T(8,128)(2,1)}, u32[]{:S(2)}, u32[]{:S(2)}) collective-permute-start(bf16[15,256,256]{2,1,0:T(8,128)(2,1)} %get-tuple-element.11), channel_id=1, source_target_pairs={{0,4},{4,8},{8,12},{12,16},{16,20},{20,24},{24,28},{28,32},{32,36}... | collective-permute-start | bytes 5898248 | tf_op jit(solution)/shard_map/ppermute | solution.py:344
  54.3 2.7 %collective-permute-start.1 = (bf16[15,256,256]{2,1,0:T(8,128)(2,1)}, bf16[15,256,256]{2,1,0:T(8,128)(2,1)}, u32[]{:S(2)}, u32[]{:S(2)}) collective-permute-start(bf16[15,256,256]{2,1,0:T(8,128)(2,1)} %get-tuple-element.10), channel_id=1, source_target_pairs={{4,0},{8,4},{12,8},{16,12},{20,16},{24,20},{28,24},{32,28},{36,32}... | collective-permute-start | bytes 5898248 | tf_op jit(solution)/shard_map/ppermute | solution.py:345
  57.0 0.0 copy-done.7
  57.0 0.0 copy-start.1
  57.0 0.0 copy-start.5
  57.0 0.0 copy-start.3
  57.0 0.0 copy-start.4
  57.0 1.3 fusion.10
  58.4 0.0 copy-done
  58.4 3.1 %collective-permute-start.2 = (f32[1,32,256]{2,1,0:T(8,128)S(1)}, f32[1,32,256]{2,1,0:T(8,128)S(1)}, u32[]{:S(2)}, u32[]{:S(2)}) collective-permute-start(f32[1,32,256]{2,1,0:T(8,128)S(1)} %div.43), channel_id=1, source_target_pairs={{0,1},{1,2},{2,3},{4,5},{5,6},{6,7},{8,9},{9,10},{10,11},{12,13},{... | collective-permute-start | bytes 98312 | tf_op jit(solution)/shard_map/ppermute | solution.py:29
  61.5 1.5 collective-permute-start.3
  63.0 0.0 copy-done.1
  63.0 0.1 multiply_reduce_fusion
  63.2 0.0 copy-done.5
  63.2 0.0 copy-done.3
  63.2 0.0 copy-done.4
  63.2 4.2 %fusion.7 = bf16[256,32,256]{2,1,0:T(8,128)(2,1)} fusion(bf16[256,32,32]{2,1,0:T(8,128)(2,1)S(1)} %copy.23, s32[256,32]{1,0:T(8,128)S(1)} %iota_add_fusion), kind=kOutput, calls=%fused_computation.11 | convolution fusion | flops 138412032 | bytes 4751360 | tf_op jit(solution)/shard_map/srj,sjc->src/dot_general | solution.py:330
  67.4 0.7 add_convert_fusion.edge_ref
  68.1 8.5 %copy.27 = bf16[32,8,32,256]{3,1,2,0:T(8,128)(2,1)} copy(bf16[32,8,32,256]{3,2,1,0:T(8,128)(2,1)} %bitcast.72) | data formatting | bytes 8388608
  76.6 0.0 collective-permute-done.2
  76.6 0.0 collective-permute-done.3
  76.6 0.0 collective-permute-done.top_ref
  76.6 3.9 %collective-permute-done.1.bot_ref = bf16[15,256,256]{2,1,0:T(8,128)(2,1)} collective-permute-done((bf16[15,256,256]{2,1,0:T(8,128)(2,1)}, bf16[15,256,256]{2,1,0:T(8,128)(2,1)}, u32[]{:S(2)}, u32[]{:S(2)}) %collective-permute-start.1) | collective-permute-done | bytes 1966112 | tf_op jit(solution)/shard_map/ppermute | solution.py:345
  80.5 2.6 %broadcast_in_dim.12.recip_hbm = f32[32,256,128]{2,1,0:T(8,128)} broadcast(f32[32,256]{1,0:T(8,128)S(1)} %fusion.67), dimensions={0,1} | broadcast | bytes 4227072 | tf_op jit(solution)/shard_map/broadcast_in_dim | solution.py:362
  83.1 0.8 broadcast_in_dim.11.scale_ref
  83.8 50.1 %shard_map.141 = (bf16[32,256,256]{2,1,0:T(8,128)(2,1)}, f32[256,256]{1,0:T(8,128)}) custom-call(f32[2]{0:T(128)} %add_convert_fusion.edge_ref, bf16[15,256,256]{2,1,0:T(8,128)(2,1)} %collective-permute-done.top_ref, bf16[32,256,256]{2,1,0:T(8,128)(2,1)} %copy-done, bf16[15,256,256]{2,1,0:T(8,128)(2,1)} %collective-permute-done.1.bot_ref, ...), custom_call_target="tpu_custom_call" | custom-call | tf_op jit(solution)/shard_map/pallas_call | solution.py:203
  133.9 1.7 %reshape.239.out_ref = f32[64,4,256]{2,1,0:T(4,128)} reshape(f32[256,256]{1,0:T(8,128)} %get-tuple-element.5) | data formatting | bytes 524288 | tf_op jit(solution)/shard_map/reshape | solution.py:371
  135.6 17.5 %shard_map.142 = f32[64,4,256]{2,1,0:T(4,128)} custom-call(f32[64,4,256]{2,1,0:T(4,128)} %reshape.239.out_ref), custom_call_target="tpu_custom_call" | custom-call | tf_op jit(solution)/shard_map/pallas_call | solution.py:279
  153.2 0.0 copy-done.2
  153.2 1.3 fusion.12
  154.5 0.2 fusion.25
  154.7 0.2 multiply_add_fusion
  154.9 0.2 fusion.28
  155.0 0.1 fusion.48
  155.1 0.1 fusion.50
  155.3 0.1 fusion.30
  155.4 0.1 fusion.32
  155.5 0.1 fusion.52
  155.6 0.1 fusion.54
  155.8 0.1 fusion.56
  155.9 0.1 fusion.34
  156.0 0.1 fusion.36
  156.1 0.1 fusion.38
  156.2 0.8 fusion.44
  (10 shorter events, 0.1 us)
Async XLA Ops:
  40.6 2.9 %copy-start.6 = (bf16[1,32,256,256]{3,2,1,0:T(8,128)(2,1)S(1)}, bf16[1,32,256,256]{3,2,1,0:T(8,128)(2,1)}, u32[]{:S(2)}) copy-start(bf16[1,32,256,256]{3,2,1,0:T(8,128)(2,1)} %param.13) | copy-start | bytes 12582916
  48.8 9.6 %copy-start = (bf16[32,256,256]{2,1,0:T(8,128)(2,1)}, bf16[32,256,256]{2,1,0:T(8,128)(2,1)S(1)}, u32[]{:S(2)}) copy-start(bf16[32,256,256]{2,1,0:T(8,128)(2,1)S(1)} %fusion.own_ref) | copy-start | bytes 12582916
  48.8 8.2 %copy-start.7 = (bf16[256,256]{1,0:T(8,128)(2,1)S(1)}, bf16[256,256]{1,0:T(8,128)(2,1)}, u32[]{:S(2)}) copy-start(bf16[256,256]{1,0:T(8,128)(2,1)} %constant.53.clone) | copy-start | bytes 393220
  51.3 25.3 %collective-permute-start = (bf16[15,256,256]{2,1,0:T(8,128)(2,1)}, bf16[15,256,256]{2,1,0:T(8,128)(2,1)}, u32[]{:S(2)}, u32[]{:S(2)}) collective-permute-start(bf16[15,256,256]{2,1,0:T(8,128)(2,1)} %get-tuple-element.11), channel_id=1, source_target_pairs={{0,4},{4,8},{8,12},{12,16},{16,20},{20,24},{24,28},{28,32},{32,36}... | collective-permute-start | bytes 5898248 | tf_op jit(solution)/shard_map/ppermute | solution.py:344
  54.3 26.3 %collective-permute-start.1 = (bf16[15,256,256]{2,1,0:T(8,128)(2,1)}, bf16[15,256,256]{2,1,0:T(8,128)(2,1)}, u32[]{:S(2)}, u32[]{:S(2)}) collective-permute-start(bf16[15,256,256]{2,1,0:T(8,128)(2,1)} %get-tuple-element.10), channel_id=1, source_target_pairs={{4,0},{8,4},{12,8},{16,12},{20,16},{24,20},{28,24},{32,28},{36,32}... | collective-permute-start | bytes 5898248 | tf_op jit(solution)/shard_map/ppermute | solution.py:345
  57.0 6.1 %copy-start.1 = (bf16[1,128,1024]{2,1,0:T(8,128)(2,1)S(1)}, bf16[1,128,1024]{2,1,0:T(8,128)(2,1)}, u32[]{:S(2)}) copy-start(bf16[1,128,1024]{2,1,0:T(8,128)(2,1)} %param.14) | copy-start | bytes 786436
  57.0 6.2 %copy-start.5 = (f32[1,256]{1,0:T(1,128)S(1)}, f32[1,256]{1,0:T(1,128)}, u32[]{:S(2)}) copy-start(f32[1,256]{1,0:T(1,128)} %param.18) | copy-start | bytes 3076
  57.0 6.2 %copy-start.3 = (f32[1,128]{1,0:T(1,128)S(1)}, f32[1,128]{1,0:T(1,128)}, u32[]{:S(2)}) copy-start(f32[1,128]{1,0:T(1,128)} %param.20) | copy-start | bytes 1540
  57.0 6.2 %copy-start.4 = (f32[1,128]{1,0:T(1,128)S(1)}, f32[1,128]{1,0:T(1,128)}, u32[]{:S(2)}) copy-start(f32[1,128]{1,0:T(1,128)} %param.19) | copy-start | bytes 1540
  58.4 18.2 %collective-permute-start.2 = (f32[1,32,256]{2,1,0:T(8,128)S(1)}, f32[1,32,256]{2,1,0:T(8,128)S(1)}, u32[]{:S(2)}, u32[]{:S(2)}) collective-permute-start(f32[1,32,256]{2,1,0:T(8,128)S(1)} %div.43), channel_id=1, source_target_pairs={{0,1},{1,2},{2,3},{4,5},{5,6},{6,7},{8,9},{9,10},{10,11},{12,13},{... | collective-permute-start | bytes 98312 | tf_op jit(solution)/shard_map/ppermute | solution.py:29
  61.5 15.0 %collective-permute-start.3 = (f32[1,32,256]{2,1,0:T(8,128)S(1)}, f32[1,32,256]{2,1,0:T(8,128)S(1)}, u32[]{:S(2)}, u32[]{:S(2)}) collective-permute-start(f32[1,32,256]{2,1,0:T(8,128)S(1)} %div.43), channel_id=1, source_target_pairs={{1,0},{2,1},{3,2},{5,4},{6,5},{7,6},{9,8},{10,9},{11,10},{13,12},{... | collective-permute-start | bytes 98312 | tf_op jit(solution)/shard_map/ppermute | solution.py:30
  83.8 69.3 %copy-start.2 = (bf16[1,128,256]{2,1,0:T(8,128)(2,1)S(1)}, bf16[1,128,256]{2,1,0:T(8,128)(2,1)}, u32[]{:S(2)}) copy-start(bf16[1,128,256]{2,1,0:T(8,128)(2,1)} %param.15) | copy-start | bytes 196612
